TPU v7x, 32 devices: a whole 2x2x4 slice. The times are simulated.
32 devices in a mesh: groups: 2 (over y), ep: 4 (over z), half: 2 (over x), tp: 2 (over core).
Axes of the slice: x: 2, y: 2, z: 4, core: 2. Of those that a mesh axis runs over, the one named last changes fastest.
Arguments:
- queries: bfloat16 [512, 2048], P(('groups', 'ep', 'half'), 'tp'), parts along dimension 0, may hold values from -6 to 6
- new_keys: bfloat16 [512, 256], P(('groups', 'ep', 'half'), 'tp'), parts along dimension 0, may hold values from -4 to 4
- new_values: bfloat16 [512, 256], P(('groups', 'ep', 'half'), 'tp'), parts along dimension 0, may hold values from -4 to 4
- cache_keys: bfloat16 [512, 2, 64, 128], P(('groups', 'ep', 'half'), 'tp'), parts along dimension 0, may hold values from -4 to 4
- cache_values: bfloat16 [512, 2, 64, 128], P(('groups', 'ep', 'half'), 'tp'), parts along dimension 0, may hold values from -4 to 4
- lengths: int32 [512], P(('groups', 'ep', 'half')), parts along dimension 0, may hold values from 1 to 64, as said below
- out_weight: bfloat16 [2048, 2048], P('tp', 'half'), may hold values from -0.375 to 0.375
- residual: bfloat16 [512, 2048], P(('groups', 'ep'), 'half'), parts along dimension 0, may hold values from -5 to 5
- norm_gain: float32 [2048], P('half'), may hold values from 0.1 to 1.9
- expert_ids: int32 [512, 8], P(('groups', 'ep')), parts along dimension 0, may hold values from 0 to 63, all different within a row; in each aligned block of 64 rows (0 to 63, 64 to 127, ...) at most 12 rows name the same one
- gate_weights: float32 [512, 8], P(('groups', 'ep')), parts along dimension 0, may hold values from 0.05 to 1
- w_gate: bfloat16 [64, 768, 2048], P(('ep', 'tp'), 'half'), may hold values from -0.125 to 0.125
- w_up: bfloat16 [64, 768, 2048], P(('ep', 'tp'), 'half'), may hold values from -0.125 to 0.125
- w_down: bfloat16 [64, 768, 2048], P(('ep', 'tp'), 'half'), may hold values from -0.625 to 0.625
Outputs:
- layer_out: bfloat16 [512, 2048], P(('groups', 'ep'), ('half', 'tp')), parts along dimension 0
There are 2 independent parts, one for each index of `groups`. A program takes and returns all parts, laid end to end along the dimension named above; an argument that names none is the same for every part. Nothing has to cross between parts.
Inputs may be any that keep to these rules, and one draw needn't show every extreme that they name: `expert_ids`: in each block of 64 consecutive rows (the tokens of one index of ep) no expert is named by more than 12 rows. `lengths`: among each device's 32 requests one has 64 cached tokens.
All inputs are finite; a program needn't handle non-finite values.
Results may differ from a plain program's by a relative error of at most 0.014.
Values may be sent and summed in bfloat16 or wider, within the bound.
No kernel may reach another device: no remote copies, remote signals or barrier semaphores. Data moves between devices by JAX's collectives and lax.ppermute only.
A program may use at most 128 MiB of HBM per device.

v0:
```python
import functools
import math

import jax
import jax.numpy as jnp
from jax import lax
from jax.experimental import pallas as pl
from jax.experimental.pallas import tpu as pltpu
from jax.sharding import PartitionSpec as P


EXPERTS = 64


EPSILON = 1e-06

MIB = 2**20


def attend(queries, new_keys, new_values, cache_keys, cache_values, lengths):
    requests, key_heads, context, head_size = cache_keys.shape
    sharing = queries.shape[1] // (key_heads * head_size)
    query_blocks = queries.reshape(requests, key_heads, sharing, head_size)
    score_scale = 1.0 / math.sqrt(head_size)
    scores = (
        jnp.einsum("rkgd,rkcd->rkgc", query_blocks, cache_keys, preferred_element_type=jnp.float32)
        * score_scale
    )
    own_score = (
        jnp.einsum(
            "rkgd,rkd->rkg",
            query_blocks,
            new_keys.reshape(requests, key_heads, head_size),
            preferred_element_type=jnp.float32,
        )
        * score_scale
    )
    valid = lax.iota(jnp.int32, context)[None, :] < lengths[:, None]
    scores = jnp.where(valid[:, None, None, :], scores, -1e30)
    highest = jnp.maximum(jnp.max(scores, axis=-1), own_score)
    weights = jnp.exp(scores - highest[..., None])
    own_weight = jnp.exp(own_score - highest)
    denominator = jnp.sum(weights, axis=-1) + own_weight
    probs = (weights / denominator[..., None]).astype(jnp.bfloat16)
    own_prob = (own_weight / denominator).astype(jnp.bfloat16)
    mixture = jnp.einsum("rkgc,rkcd->rkgd", probs, cache_values, preferred_element_type=jnp.float32)
    mixture = mixture + own_prob.astype(jnp.float32)[..., None] * new_values.reshape(
        requests, key_heads, 1, head_size
    ).astype(jnp.float32)
    return mixture.astype(jnp.bfloat16).reshape(requests, key_heads * sharing * head_size)


def combine_rows(returned_rows, target, gates):
    token_rows, top_count = target.shape
    safe_target = jnp.maximum(target, 0).reshape(-1)
    picked = jnp.take(returned_rows, safe_target, axis=0).reshape(
        token_rows, top_count, returned_rows.shape[1]
    )
    weighting = jnp.where(target >= 0, gates, 0.0)
    return jnp.sum(picked.astype(jnp.float32) * weighting[..., None], axis=1)


def by_slots(
    queries,
    new_keys,
    new_values,
    cache_keys,
    cache_values,
    lengths,
    out_weight,
    residual,
    norm_gain,
    expert_ids,
    gate_weights,
    w_gate,
    w_up,
    w_down,
):
    attended = attend(queries, new_keys, new_values, cache_keys, cache_values, lengths)
    partial_mix = jnp.dot(
        lax.all_gather(attended, "half", axis=0, tiled=True),
        out_weight,
        preferred_element_type=jnp.float32,
    )
    mixed = lax.psum(partial_mix.astype(jnp.bfloat16), "tp").astype(jnp.float32)
    hidden = residual.astype(jnp.float32) + mixed
    squares = lax.psum(jnp.sum(hidden * hidden, axis=1), "half")
    half_width = hidden.shape[1]
    width = half_width * lax.axis_size("half")
    normed = (hidden * lax.rsqrt(squares / width + EPSILON)[:, None] * norm_gain[None, :]).astype(
        jnp.bfloat16
    )
    token_rows, top_count = expert_ids.shape
    ep_count = lax.axis_size("ep")
    tp_count = lax.axis_size("tp")
    local_experts = w_gate.shape[0]
    capacity = token_rows * top_count * 3 // (2 * EXPERTS)
    slot_count = ep_count * local_experts * capacity
    flat_ids = expert_ids.reshape(-1)
    one_hot = (flat_ids[:, None] == lax.iota(jnp.int32, EXPERTS)[None, :]).astype(jnp.int32)
    earlier = jnp.cumsum(one_hot, axis=0) - one_hot
    slot = jnp.sum(earlier * one_hot, axis=1)
    owner_ep = flat_ids // (local_experts * tp_count)
    owner_tp = flat_ids // local_experts % tp_count
    target = owner_ep * (local_experts * capacity) + flat_ids % local_experts * capacity + slot
    target = jnp.where(owner_tp == lax.axis_index("tp"), target, -1).reshape(token_rows, top_count)
    dispatch_matrix = jnp.any(
        lax.iota(jnp.int32, slot_count)[:, None, None] == target[None, :, :], axis=2
    ).astype(jnp.bfloat16)
    gates = gate_weights / jnp.sum(gate_weights, axis=1, keepdims=True)
    full_rows = lax.all_gather(normed, "half", axis=1, tiled=True)
    outgoing = jnp.dot(dispatch_matrix, full_rows, preferred_element_type=jnp.float32).astype(
        jnp.bfloat16
    )
    arrived = lax.all_to_all(
        outgoing.reshape(ep_count, local_experts, capacity, width),
        "ep",
        split_axis=0,
        concat_axis=0,
        tiled=True,
    )
    gate_part = jnp.einsum("secd,efd->secf", arrived, w_gate, preferred_element_type=jnp.float32)
    up_part = jnp.einsum("secd,efd->secf", arrived, w_up, preferred_element_type=jnp.float32)
    activation = (jax.nn.silu(gate_part) * up_part).astype(jnp.bfloat16)
    expert_out = jnp.einsum(
        "secf,efd->secd", activation, w_down, preferred_element_type=jnp.float32
    ).astype(jnp.bfloat16)
    summed = lax.psum_scatter(
        expert_out.astype(jnp.float32).astype(jnp.bfloat16), "half", scatter_dimension=3, tiled=True
    ).astype(jnp.float32)
    returned = lax.all_to_all(
        summed.reshape(ep_count, local_experts * capacity, half_width).astype(jnp.bfloat16),
        "ep",
        split_axis=0,
        concat_axis=0,
        tiled=True,
    ).astype(jnp.float32)
    term = combine_rows(returned.reshape(slot_count, half_width), target, gates)
    expert_sum = lax.psum_scatter(
        term.astype(jnp.bfloat16), "tp", scatter_dimension=1, tiled=True
    ).astype(jnp.float32)
    slice_width = expert_sum.shape[1]
    own_columns = lax.dynamic_slice_in_dim(
        hidden, lax.axis_index("tp") * slice_width, slice_width, 1
    )
    return (own_columns + expert_sum).astype(jnp.bfloat16)


VMEM_SPEC = pl.BlockSpec(memory_space=pltpu.VMEM)
HBM_SPEC = pl.BlockSpec(memory_space=pltpu.HBM)
SMEM_SPEC = pl.BlockSpec(memory_space=pltpu.SMEM)
NT = (((1,), (1,)), ((), ()))
TN = (((0,), (0,)), ((), ()))
F32 = jnp.float32
BF16 = jnp.bfloat16


def kernel_call(body, outs, specs=None, scratch=(), flops=1000, vmem=8, args=()):
    return pallas_kernel(body, outs, specs, scratch, flops, vmem, args)


def pallas_kernel(body, outs, specs, scratch, flops, vmem, args):
    return pl.pallas_call(
        body,
        out_shape=tuple(jax.ShapeDtypeStruct(s, d) for s, d in outs),
        in_specs=specs or [VMEM_SPEC] * len(args),
        out_specs=tuple(VMEM_SPEC for _ in outs),
        scratch_shapes=list(scratch),
        cost_estimate=pl.CostEstimate(flops=flops, bytes_accessed=1000, transcendentals=0),
        compiler_params=pltpu.CompilerParams(vmem_limit_bytes=vmem * MIB),
    )(*args)


def load_body(*refs):
    count = len(refs) // 2
    sems = refs[-1]
    copies = [
        pltpu.make_async_copy(refs[i], refs[count + i], sems.at[i]) for i in range(count)
    ]
    for copy in copies:
        copy.start()
    for copy in copies:
        copy.wait()


def attend_body(sharing, context, q_ref, nk_ref, nv_ref, k_ref, v_ref, len_ref, out_ref):
    requests = q_ref.shape[0]
    head_size = nk_ref.shape[1]
    group = 8
    rows = group * sharing
    keys = group * context
    score_scale = 1.0 / math.sqrt(head_size)
    lane = lax.broadcasted_iota(jnp.int32, (rows, keys), 1)
    position = jnp.where(
        lane // context == lax.broadcasted_iota(jnp.int32, (rows, keys), 0) % group,
        lane % context,
        context,
    )
    request = lax.broadcasted_iota(jnp.int32, (group, requests), 1)
    offset = request - lax.broadcasted_iota(jnp.int32, (group, requests), 0)
    for j in range(requests // group):
        here = slice(group * j, group * (j + 1))
        q = q_ref[here, :].astype(F32)
        q = jnp.concatenate(
            [q[:, g * head_size : (g + 1) * head_size] for g in range(sharing)], axis=0
        )
        own_key = jnp.concatenate([nk_ref[here, :].astype(F32)] * sharing, axis=0)
        own_value = jnp.concatenate([nv_ref[here, :].astype(F32)] * sharing, axis=0)
        length = jnp.sum(
            jnp.where(offset == group * j, len_ref[...], 0).astype(F32), axis=1, keepdims=True
        ).astype(jnp.int32)
        length = jnp.concatenate([length] * sharing, axis=0)
        scores = (
            lax.dot_general(
                q.astype(BF16), k_ref[keys * j : keys * (j + 1), :], NT, preferred_element_type=F32
            )
            * score_scale
        )
        scores = jnp.where(position < length, scores, -1e30)
        own_score = jnp.sum(q * own_key, axis=1, keepdims=True) * score_scale
        highest = jnp.maximum(jnp.max(scores, axis=1, keepdims=True), own_score)
        weights = jnp.exp(scores - highest)
        own_weight = jnp.exp(own_score - highest)
        inverse = 1.0 / (jnp.sum(weights, axis=1, keepdims=True) + own_weight)
        probs = (weights * inverse).astype(BF16)
        own_prob = (own_weight * inverse).astype(BF16).astype(F32)
        mixture = jnp.dot(probs, v_ref[keys * j : keys * (j + 1), :], preferred_element_type=F32)
        mixture = (mixture + own_prob * own_value).astype(BF16)
        for g in range(sharing):
            out_ref[here, g * head_size : (g + 1) * head_size] = mixture[group * g : group * (g + 1), :]


def project_body(own_ref, other_ref, w_ref, keep_ref, send_ref, rows_ref):
    x = lax.axis_index("half")
    t = lax.axis_index("tp")
    count = own_ref.shape[0]
    cols = keep_ref.shape[1]
    rows_ref[pl.ds(pl.multiple_of(x * count, count), count), :] = own_ref[...]
    rows_ref[pl.ds(pl.multiple_of((1 - x) * count, count), count), :] = other_ref[...]
    rows = rows_ref[...]
    send_ref[...] = jnp.dot(
        rows, w_ref[:, pl.ds(pl.multiple_of((1 - t) * cols, cols), cols)], preferred_element_type=F32
    )
    keep_ref[...] = jnp.dot(
        rows, w_ref[:, pl.ds(pl.multiple_of(t * cols, cols), cols)], preferred_element_type=F32
    )


LANES = 128
TAIL = 8


def hidden_body(res_ref, ids_ref, gw_ref, gain_ref, keep_ref, got_ref, h32_ref, load_ref, tail_ref):
    t = lax.axis_index("tp")
    rows, cols = keep_ref.shape
    here = pl.ds(pl.multiple_of(t * cols, cols), cols)
    hidden = res_ref[:, here].astype(F32) + (keep_ref[...] + got_ref[...])
    h32_ref[...] = hidden
    load_ref[0:rows, :] = hidden.astype(BF16)
    gw = gw_ref[...]
    gates = gw / jnp.sum(gw, axis=0, keepdims=True)
    high = gates.astype(BF16).astype(F32)
    gain = gain_ref[:, here]
    gain_high = gain.astype(BF16).astype(F32)
    tail_ref[...] = jnp.zeros(tail_ref.shape, F32)
    tail_ref[:, 0:rows] = ids_ref[...].astype(F32)
    tail_ref[:, LANES : LANES + rows] = high
    tail_ref[:, 2 * LANES : 2 * LANES + rows] = gates - high
    for i in range(cols // LANES):
        part = slice(LANES * i, LANES * (i + 1))
        tail_ref[i : i + 1, 3 * LANES :] = gain_high[:, part]
        tail_ref[TAIL // 2 + i : TAIL // 2 + i + 1, 3 * LANES :] = (gain - gain_high)[:, part]
    load_ref[rows:, :] = tail_ref[...].astype(BF16)


def merge_body(blocks, *refs):
    all_ref, far_ref = refs[-2:]
    rows = all_ref.shape[0] // blocks
    for j in range(blocks):
        all_ref[rows * j : rows * (j + 1), :] = refs[j][0:rows, :]
    for j in range(blocks // 2, blocks):
        start = rows * (j - blocks // 2)
        far_ref[start : start + rows, :] = refs[j][0:rows, :]


def join_body(near, *refs):
    out_ref = refs[-1]
    rows = refs[0].shape[0] - TAIL
    for j in range(near):
        out_ref[rows * j : rows * (j + 1), :] = refs[j][0:rows, :]
    out_ref[rows * near : out_ref.shape[0] - TAIL, :] = refs[near][...]
    out_ref[out_ref.shape[0] - TAIL :, :] = refs[0][rows:, :]


def pick_body(blocks, *refs):
    loads, pick_ref, gate_ref = refs[:blocks], refs[blocks], refs[blocks + 1]
    token_rows = loads[0].shape[0] - TAIL
    slot_rows, tokens = pick_ref.shape
    experts = EXPERTS // (lax.axis_size("ep") * lax.axis_size("tp"))
    slots = slot_rows // experts
    low = lax.broadcasted_iota(jnp.int32, (TAIL, LANES), 1) < token_rows
    tails = [ref[token_rows:, :].astype(F32) for ref in loads]

    def side_by_side(values):
        pairs = [
            jnp.where(low, values[j], pltpu.roll(values[j + 1], LANES - token_rows, 1))
            for j in range(0, blocks, 2)
        ]
        return jnp.concatenate(pairs, axis=1)

    ids = side_by_side([v[:, 0:LANES] for v in tails])
    gates = side_by_side([v[:, LANES : 2 * LANES] + v[:, 2 * LANES : 3 * LANES] for v in tails])
    first = (lax.axis_index("ep") * lax.axis_size("tp") + lax.axis_index("tp")) * experts
    number = (first + lax.broadcasted_iota(jnp.int32, (experts, TAIL, tokens), 0)).astype(F32)
    named = ids[None] == number
    chosen = jnp.sum(jnp.where(named, 1.0, 0.0), axis=1)
    gate = jnp.sum(jnp.where(named, gates[None], 0.0), axis=1)
    before = (
        lax.broadcasted_iota(jnp.int32, (tokens, tokens), 0)
        < lax.broadcasted_iota(jnp.int32, (tokens, tokens), 1)
    )
    earlier = jnp.dot(
        chosen.astype(BF16), jnp.where(before, 1.0, 0.0).astype(BF16), preferred_element_type=F32
    )
    place = jnp.where(chosen > 0.0, earlier, -1.0)
    slot = lax.broadcasted_iota(jnp.int32, (experts, slots, tokens), 1).astype(F32)
    pick = jnp.where(slot == place[:, None, :], 1.0, 0.0)
    gate_ref[...] = jnp.sum(pick * gate[:, None, :], axis=2, keepdims=True).reshape(
        slot_rows, 1
    )
    pick_ref[...] = pick.reshape(slot_rows, tokens).astype(BF16)


def gathered_rows(pick, parts, rows_ref):
    total = 0.0
    tokens = pick.shape[1]
    for owner, ref, gain in parts:
        cols = ref.shape[1]
        rows = jnp.dot(pick, ref[0:tokens, :], preferred_element_type=F32)
        total = total + jnp.sum(rows * rows, axis=1, keepdims=True)
        rows_ref[:, pl.ds(pl.multiple_of(owner * cols, cols), cols)] = (rows * gain).astype(BF16)
    return total


def tail_gain(ref):
    rows, cols = ref.shape
    tail = ref[rows - TAIL :, 3 * LANES :].astype(F32)
    gain = tail + pltpu.roll(tail, TAIL // 2, 0)
    return jnp.concatenate([gain[i : i + 1, :] for i in range(cols // LANES)], axis=1)


def products(rows_ref, w_ref, e, slots, start):
    half_width = rows_ref.shape[1]
    return lax.dot_general(
        rows_ref[slots * e : slots * (e + 1), :],
        w_ref[e, :, pl.ds(pl.multiple_of(start, half_width), half_width)],
        NT,
        preferred_element_type=F32,
    )


def first_half_body(
    slots, mine_ref, theirs_ref, gain_ref, wg_ref, wu_ref, pick_ref, squares_ref, rows_ref, ga_ref, ua_ref
):
    t = lax.axis_index("tp")
    cols = mine_ref.shape[1]
    parts = [
        (owner, ref, gain_ref[:, pl.ds(pl.multiple_of(owner * cols, cols), cols)])
        for owner, ref in ((t, mine_ref), (1 - t, theirs_ref))
    ]
    squares_ref[...] = gathered_rows(pick_ref[...], parts, rows_ref)
    start = lax.axis_index("half") * rows_ref.shape[1]
    for e in range(ga_ref.shape[0] // slots):
        here = slice(slots * e, slots * (e + 1))
        ga_ref[here, :] = products(rows_ref, wg_ref, e, slots, start)
        ua_ref[here, :] = products(rows_ref, wu_ref, e, slots, start)


def more_first_half_body(slots, done, rows_ref, wg_ref, wu_ref, ga_ref, ua_ref):
    start = lax.axis_index("half") * rows_ref.shape[1]
    for e in range(ga_ref.shape[0] // slots):
        here = slice(slots * e, slots * (e + 1))
        ga_ref[here, :] = products(rows_ref, wg_ref, done + e, slots, start)
        ua_ref[here, :] = products(rows_ref, wu_ref, done + e, slots, start)


def second_half_body(
    slots, mine_ref, theirs_ref, wg_ref, wu_ref, pick_ref, squares_ref, ga_ref, ua_ref, gb_ref, ub_ref,
    act_ref, rows_ref, inv_ref,
):
    experts, _, width = wg_ref.shape
    t = lax.axis_index("tp")
    parts = [(t, mine_ref, tail_gain(mine_ref)), (1 - t, theirs_ref, tail_gain(theirs_ref))]
    squares = gathered_rows(pick_ref[...], parts, rows_ref)
    inv_ref[...] = lax.rsqrt((squares_ref[...] + squares) / width + EPSILON)
    start = (1 - lax.axis_index("half")) * rows_ref.shape[1]
    done = ga_ref.shape[0] // slots
    for e in range(experts):
        here = slice(slots * e, slots * (e + 1))
        gate_acc, up_acc = (ga_ref, ua_ref) if e < done else (gb_ref, ub_ref)
        row = slots * (e if e < done else e - done)
        there = slice(row, row + slots)
        inverse = inv_ref[here, :]
        gate_part = inverse * (gate_acc[there, :] + products(rows_ref, wg_ref, e, slots, start))
        up_part = inverse * (up_acc[there, :] + products(rows_ref, wu_ref, e, slots, start))
        act_ref[here, :] = (jax.nn.silu(gate_part) * up_part).astype(BF16)


def down_body(other_half, other_core, act_ref, gate_ref, pick_ref, wd_ref, out_ref, y_ref):
    experts = wd_ref.shape[0]
    cols = out_ref.shape[1]
    slots = pick_ref.shape[0] // experts
    x, t = lax.axis_index("half"), lax.axis_index("tp")
    quarter = (1 - x if other_half else x) * lax.axis_size("tp") + (1 - t if other_core else t)
    columns = pl.ds(pl.multiple_of(quarter * cols, cols), cols)

    def one(e, carry):
        here = pl.ds(pl.multiple_of(e * slots, slots), slots)
        y = jnp.dot(act_ref[here, :], wd_ref[e, :, columns], preferred_element_type=F32)
        y_ref[here, :] = (y * gate_ref[here, :]).astype(BF16)
        return carry

    lax.fori_loop(0, experts, one, 0, unroll=True)
    out_ref[...] = lax.dot_general(
        pick_ref[...], y_ref[...], TN, preferred_element_type=F32
    ).astype(out_ref.dtype)


def pair_sum_body(keep_ref, got_ref, far_ref, near_ref):
    rows = near_ref.shape[0]
    for out, start in ((near_ref, 0), (far_ref, rows)):
        here = slice(start, start + out.shape[0])
        out[...] = (keep_ref[here, :] + got_ref[here, :].astype(F32)).astype(BF16)


def block_sum_body(start, keep_ref, got_ref, other_ref, *outs):
    rows = outs[0].shape[0]
    for j, out in enumerate(outs):
        here = slice(start + rows * j, start + rows * (j + 1))
        total = keep_ref[here, :] + got_ref[here, :].astype(F32)
        total = total + other_ref[rows * j : rows * (j + 1), :].astype(F32)
        out[...] = total.astype(out.dtype)


def final_body(h32_ref, own_ref, *refs):
    out_ref = refs[-1]
    total = own_ref[...]
    for ref in refs[:-1]:
        total = total + ref[...].astype(F32)
    out_ref[...] = (h32_ref[...] + total).astype(BF16)


def swap(value, axis, partner=1):
    return lax.ppermute(
        value, axis, [(i, i ^ partner) for i in range(lax.axis_size(axis))]
    )


def by_rows(
    queries,
    new_keys,
    new_values,
    cache_keys,
    cache_values,
    lengths,
    out_weight,
    residual,
    norm_gain,
    expert_ids,
    gate_weights,
    w_gate,
    w_up,
    w_down,
):
    requests, _, context, head_size = cache_keys.shape
    sharing = queries.shape[1] // head_size
    token_rows, top_count = expert_ids.shape
    blocks = lax.axis_size("ep")
    tokens = blocks * token_rows
    experts, hidden_units, _ = w_gate.shape
    half_width = residual.shape[1]
    cols = half_width // lax.axis_size("tp")
    slots = token_rows * top_count * 3 // (2 * EXPERTS) * blocks
    slot_rows = experts * slots
    w_gate, w_up, w_down = (
        pltpu.with_memory_space_constraint(w, pltpu.VMEM) for w in (w_gate, w_up, w_down)
    )

    gain = norm_gain.reshape(1, half_width)
    cache = (requests * context, head_size)
    sources = tuple(
        pltpu.with_memory_space_constraint(v, pltpu.HBM)
        for v in (
            queries,
            new_keys,
            new_values,
            cache_keys.reshape(cache),
            cache_values.reshape(cache),
            lengths.reshape(1, requests),
        )
    )
    loaded = kernel_call(
        load_body,
        [(v.shape, v.dtype) for v in sources],
        specs=[HBM_SPEC] * len(sources),
        scratch=[pltpu.SemaphoreType.DMA((len(sources),))],
        args=sources,
    )
    (attended,) = kernel_call(
        functools.partial(attend_body, sharing, context),
        [((requests, sharing * head_size), BF16)],
        flops=10**11,
        args=loaded,
    )
    other_attended = swap(attended, "half")
    keep, send = kernel_call(
        project_body,
        [((token_rows, cols), F32)] * 2,
        scratch=[pltpu.VMEM((token_rows, sharing * head_size), BF16)],
        args=(attended, other_attended, out_weight),
    )
    h32, payload = kernel_call(
        hidden_body,
        [((token_rows, cols), F32), ((token_rows + TAIL, cols), BF16)],
        scratch=[pltpu.VMEM((TAIL, cols), F32)],
        args=(residual, expert_ids.T, gate_weights.T, gain, keep, swap(send, "tp")),
    )
    arrived = [payload] + [swap(payload, "ep", j) for j in range(1, blocks)]
    near = blocks // 2
    near_x = [swap(arrived[j], "half") for j in range(near)]
    mine, far = kernel_call(
        functools.partial(merge_body, blocks),
        [((tokens, cols), BF16), ((tokens // 2, cols), BF16)],
        args=arrived,
    )
    theirs = swap(mine, "tp")
    far_x = swap(far, "half")
    pick, gate = kernel_call(
        functools.partial(pick_body, blocks),
        [((slot_rows, tokens), BF16), ((slot_rows, 1), F32)],
        args=arrived,
    )
    early = experts * 3 // 4
    squares, rows, gate_a, up_a = kernel_call(
        functools.partial(first_half_body, slots),
        [
            ((slot_rows, 1), F32),
            ((slot_rows, half_width), BF16),
            ((slots * early, hidden_units), F32),
            ((slots * early, hidden_units), F32),
        ],
        args=(mine, theirs, gain, w_gate, w_up, pick),
    )
    far_x, squares, near_x = lax.optimization_barrier((far_x, squares, near_x))
    (mine_x,) = kernel_call(
        functools.partial(join_body, near), [((tokens + TAIL, cols), BF16)], args=(*near_x, far_x)
    )
    theirs_x = swap(mine_x, "tp")
    gate_b, up_b = kernel_call(
        functools.partial(more_first_half_body, slots, early),
        [((slots * (experts - early), hidden_units), F32)] * 2,
        args=(rows, w_gate, w_up),
    )
    (act,) = kernel_call(
        functools.partial(second_half_body, slots),
        [((slot_rows, hidden_units), BF16)],
        scratch=[pltpu.VMEM((slot_rows, half_width), BF16), pltpu.VMEM((slot_rows, 1), F32)],
        args=(
            mine_x, theirs_x, w_gate, w_up, pick, squares, gate_a, up_a, gate_b, up_b,
        ),
    )

    def down(act, other_half, other_core):
        return kernel_call(
            functools.partial(down_body, other_half, other_core),
            [((tokens, cols), BF16 if other_core else F32)],
            scratch=[pltpu.VMEM((slot_rows, cols), BF16)],
            flops=10**9,
            args=(act, gate, pick, w_down),
        )[0]

    got_a = swap(down(act, True, True), "tp")
    keep_a = down(act, True, False)
    near_rows = tokens // 2
    far, near = kernel_call(
        pair_sum_body,
        [((tokens - near_rows, cols), BF16), ((near_rows, cols), BF16)],
        args=(keep_a, got_a),
    )
    act, far, near = lax.optimization_barrier((act, far, near))
    far_x = swap(far, "half")
    near_x = swap(near, "half")
    got_b = swap(down(act, False, True), "tp")
    keep_b = down(act, False, False)
    far_sums = kernel_call(
        functools.partial(block_sum_body, near_rows),
        [((token_rows, cols), BF16)] * (blocks // 2),
        args=(keep_b, got_b, far_x),
    )
    near_sums = kernel_call(
        functools.partial(block_sum_body, 0),
        [((token_rows, cols), F32)] + [((token_rows, cols), BF16)] * (blocks // 2 - 1),
        args=(keep_b, got_b, near_x),
    )
    home = [swap(v, "ep", blocks // 2 + j) for j, v in enumerate(far_sums)]
    home += [swap(v, "ep", 1 + j) for j, v in enumerate(near_sums[1:])]
    (out,) = kernel_call(final_body, [((token_rows, cols), BF16)], args=(h32, near_sums[0], *home))
    return out


def solution(mesh):
    placed = (
        P(("groups", "ep", "half"), "tp"),
        P(("groups", "ep", "half"), "tp"),
        P(("groups", "ep", "half"), "tp"),
        P(("groups", "ep", "half"), "tp", None, None),
        P(("groups", "ep", "half"), "tp", None, None),
        P(("groups", "ep", "half")),
        P("tp", "half"),
        P(("groups", "ep"), "half"),
        P("half"),
        P(("groups", "ep"), None),
        P(("groups", "ep"), None),
        P(("ep", "tp"), "half", None),
        P(("ep", "tp"), "half", None),
        P(("ep", "tp"), "half", None),
    )
    few = mesh.shape["half"] == 2 and mesh.shape["tp"] == 2 and mesh.shape["ep"] == 4

    def on_device(*args):
        return by_rows(*args) if few else by_slots(*args)

    return jax.shard_map(
        on_device,
        mesh=mesh,
        in_specs=placed,
        out_specs=P(("groups", "ep"), ("half", "tp")),
        check_vma=False,
    )
```

profile of v0, /device:TPU:0, one launch (start us, length us, event | category | flops | bytes accessed | tf_op | source)
XLA Modules:
  0.0 54.6 jit_solution(6583941274925949752)
XLA Ops:
  0.0 1.3 %shard_map.136 = (bf16[32,1024]{1,0:T(8,128)(2,1)S(1)}, bf16[32,128]{1,0:T(8,128)(2,1)S(1)}, bf16[32,128]{1,0:T(8,128)(2,1)S(1)}, bf16[2048,128]{1,0:T(8,128)(2,...) custom-call(bf16[32,1024]{1,0:T(8,128)(2,1)} %refs_0_.1, bf16[32,128]{1,0:T(8,128)(2,1)} %refs_1_.1, ...), custom_call_target="tpu_custom_call" | custom-call | flops 1000 | bytes 1000 | tf_op jit(solution)/shard_map/pallas_call | solution.py:163
  1.4 1.5 %shard_map.137.own_ref = bf16[32,1024]{1,0:T(8,128)(2,1)S(1)} custom-call(bf16[32,1024]{1,0:T(8,128)(2,1)S(1)} %get-tuple-element.38.q_ref, bf16[32,128]{1,0:T(8,128)(2,1)S(1)} %get-tuple-element.39.nk_ref, bf16[32,128]{1,0:T(8,128)(2,1)S(1)} %get-tuple-element.40.nv_ref, bf16[2048,128]{1,0:T(8,128)(2,1)S(1)} %get-tuple-element.41.k_ref, ...), custom_call_target="tpu_custom_call" | custom-call | flops 99999997952 | bytes 1000 | tf_op jit(solution)/shard_map/pallas_call | solution.py:163
  2.9 3.0 %collective-permute-start = (bf16[32,1024]{1,0:T(8,128)(2,1)S(1)}, bf16[32,1024]{1,0:T(8,128)(2,1)S(1)}, u32[]{:S(2)}, u32[]{:S(2)}) collective-permute-start(bf16[32,1024]{1,0:T(8,128)(2,1)S(1)} %shard_map.137.own_ref), channel_id=1, source_target_pairs={{0,2},{2,0},{1,3},{3,1},{4,6},{6,4},{5,7},{7,5},{8,10},{10,8},{9,1... | collective-permute-start | bytes 196616 | tf_op jit(solution)/shard_map/ppermute | solution.py:454
  5.9 2.2 %collective-permute-done.other_ref = bf16[32,1024]{1,0:T(8,128)(2,1)S(1)} collective-permute-done((bf16[32,1024]{1,0:T(8,128)(2,1)S(1)}, bf16[32,1024]{1,0:T(8,128)(2,1)S(1)}, u32[]{:S(2)}, u32[]{:S(2)}) %collective-permute-start) | collective-permute-done | bytes 65568 | tf_op jit(solution)/shard_map/ppermute | solution.py:454
  8.8 1.3 %collective-permute-done.1.got_ref = f32[64,512]{1,0:T(8,128)S(1)} collective-permute-done((f32[64,512]{1,0:T(8,128)S(1)}, f32[64,512]{1,0:T(8,128)S(1)}, u32[]{:S(2)}, u32[]{:S(2)}) %collective-permute-start.1) | collective-permute-done | bytes 131104 | tf_op jit(solution)/shard_map/ppermute | solution.py:454
  10.2 4.2 %collective-permute-start.4 = (bf16[72,512]{1,0:T(8,128)(2,1)S(1)}, bf16[72,512]{1,0:T(8,128)(2,1)S(1)}, u32[]{:S(2)}, u32[]{:S(2)}) collective-permute-start(bf16[72,512]{1,0:T(8,128)(2,1)S(1)} %get-tuple-element.47.refs_0_), channel_id=1, source_target_pairs={{0,12},{4,8},{8,4},{12,0},{1,13},{5,9},{9,5},{13,1},{2,14},{6,10},... | collective-permute-start | bytes 221192 | tf_op jit(solution)/shard_map/ppermute | solution.py:454
  15.0 2.3 %collective-permute-done.4.refs_3_ = bf16[72,512]{1,0:T(8,128)(2,1)S(1)} collective-permute-done((bf16[72,512]{1,0:T(8,128)(2,1)S(1)}, bf16[72,512]{1,0:T(8,128)(2,1)S(1)}, u32[]{:S(2)}, u32[]{:S(2)}) %collective-permute-start.4) | collective-permute-done | bytes 73760 | tf_op jit(solution)/shard_map/ppermute | solution.py:454
  17.3 3.5 %collective-permute-done.3.refs_2_ = bf16[72,512]{1,0:T(8,128)(2,1)S(1)} collective-permute-done((bf16[72,512]{1,0:T(8,128)(2,1)S(1)}, bf16[72,512]{1,0:T(8,128)(2,1)S(1)}, u32[]{:S(2)}, u32[]{:S(2)}) %collective-permute-start.3) | collective-permute-done | bytes 73760 | tf_op jit(solution)/shard_map/ppermute | solution.py:454
  21.0 1.6 %collective-permute-start.5 = (bf16[128,512]{1,0:T(8,128)(2,1)S(1)}, bf16[128,512]{1,0:T(8,128)(2,1)S(1)}, u32[]{:S(2)}, u32[]{:S(2)}) collective-permute-start(bf16[128,512]{1,0:T(8,128)(2,1)S(1)} %get-tuple-element.48), channel_id=1, source_target_pairs={{0,2},{2,0},{1,3},{3,1},{4,6},{6,4},{5,7},{7,5},{8,10},{10,8},{9,1... | collective-permute-start | bytes 393224 | tf_op jit(solution)/shard_map/ppermute | solution.py:454
  23.1 1.5 %collective-permute-start.8 = (bf16[72,512]{1,0:T(8,128)(2,1)S(1)}, bf16[72,512]{1,0:T(8,128)(2,1)S(1)}, u32[]{:S(2)}, u32[]{:S(2)}) collective-permute-start(bf16[72,512]{1,0:T(8,128)(2,1)S(1)} %collective-permute-done.2.refs_1_), channel_id=1, source_target_pairs={{0,2},{2,0},{1,3},{3,1},{4,6},{6,4},{5,7},{7,5},{8,10},{10,8},{9,1... | collective-permute-start | bytes 221192 | tf_op jit(solution)/shard_map/ppermute | solution.py:454
  24.9 3.0 %shard_map.142 = (f32[384,1]{1,0:T(8,128)S(1)}, bf16[384,1024]{1,0:T(8,128)(2,1)S(1)}, f32[288,384]{1,0:T(8,128)S(1)}, f32[288,384]{1,0:T(8,128)S(1)}) custom-call(bf16[256,512]{1,0:T(8,128)(2,1)S(1)} %get-tuple-element.49.mine_ref, bf16[256,512]{1,0:T(8,128)(2,1)S(1)} %collective-permute-done.6.theirs_ref, f32[1,1024]{1,0:T(1,128)S(1)} %bitcast.9, ...), custom_call_target="tpu_custom_call" | custom-call | flops 1000 | bytes 1000 | tf_op jit(solution)/shard_map/pallas_call | solution.py:163
  28.0 1.0 %collective-permute-done.7.refs_0_ = bf16[72,512]{1,0:T(8,128)(2,1)S(1)} collective-permute-done((bf16[72,512]{1,0:T(8,128)(2,1)S(1)}, bf16[72,512]{1,0:T(8,128)(2,1)S(1)}, u32[]{:S(2)}, u32[]{:S(2)}) %collective-permute-start.7) | collective-permute-done | bytes 73760 | tf_op jit(solution)/shard_map/ppermute | solution.py:454
  29.0 1.0 %collective-permute-done.8.refs_1_ = bf16[72,512]{1,0:T(8,128)(2,1)S(1)} collective-permute-done((bf16[72,512]{1,0:T(8,128)(2,1)S(1)}, bf16[72,512]{1,0:T(8,128)(2,1)S(1)}, u32[]{:S(2)}, u32[]{:S(2)}) %collective-permute-start.8) | collective-permute-done | bytes 73760 | tf_op jit(solution)/shard_map/ppermute | solution.py:454
  30.2 1.0 %shard_map.144 = (f32[96,384]{1,0:T(8,128)S(1)}, f32[96,384]{1,0:T(8,128)S(1)}) custom-call(bf16[384,1024]{1,0:T(8,128)(2,1)S(1)} %get-tuple-element.58.rows_ref, bf16[8,384,2048]{2,1,0:T(8,128)(2,1)S(1)} %copy-done, bf16[8,384,2048]{2,1,0:T(8,128)(2,1)S(1)} %copy-done.1), custom_call_target="tpu_custom_call" | custom-call | flops 1000 | bytes 1000 | tf_op jit(solution)/shard_map/pallas_call | solution.py:163
  31.7 4.0 %shard_map.145.act_ref = bf16[384,384]{1,0:T(8,128)(2,1)S(1)} custom-call(bf16[264,512]{1,0:T(8,128)(2,1)S(1)} %shard_map.143.mine_ref, bf16[264,512]{1,0:T(8,128)(2,1)S(1)} %collective-permute-done.9.theirs_ref, bf16[8,384,2048]{2,1,0:T(8,128)(2,1)S(1)} %copy-done, bf16[8,384,2048]{2,1,0:T(8,128)(2,1)S(1)} %copy-done.1, ...), custom_call_target="tpu_custom_call" | custom-call | flops 1000 | bytes 1000 | tf_op jit(solution)/shard_map/pallas_call | solution.py:163
  35.7 0.9 %shard_map.147 = bf16[256,512]{1,0:T(8,128)(2,1)S(1)} custom-call(bf16[384,384]{1,0:T(8,128)(2,1)S(1)} %shard_map.145.act_ref, f32[384,1]{1,0:T(8,128)S(1)} %get-tuple-element.61.gate_ref, bf16[384,256]{1,0:T(8,128)(2,1)S(1)} %get-tuple-element.50.pick_ref, bf16[8,384,2048]{2,1,0:T(8,128)(2,1)S(1)} %bitcast.7), custom_call_target="tpu_custom_call" | custom-call | flops 1000000000 | bytes 1000 | tf_op jit(solution)/shard_map/pallas_call | solution.py:163
  36.8 0.9 %shard_map.146.keep_ref = f32[256,512]{1,0:T(8,128)S(1)} custom-call(bf16[384,384]{1,0:T(8,128)(2,1)S(1)} %shard_map.145.act_ref, f32[384,1]{1,0:T(8,128)S(1)} %get-tuple-element.61.gate_ref, bf16[384,256]{1,0:T(8,128)(2,1)S(1)} %get-tuple-element.50.pick_ref, bf16[8,384,2048]{2,1,0:T(8,128)(2,1)S(1)} %bitcast.7), custom_call_target="tpu_custom_call" | custom-call | flops 1000000000 | bytes 1000 | tf_op jit(solution)/shard_map/pallas_call | solution.py:163
  38.3 0.9 %shard_map.150 = bf16[256,512]{1,0:T(8,128)(2,1)S(1)} custom-call(bf16[384,384]{1,0:T(8,128)(2,1)S(1)} %shard_map.145.act_ref, f32[384,1]{1,0:T(8,128)S(1)} %get-tuple-element.61.gate_ref, bf16[384,256]{1,0:T(8,128)(2,1)S(1)} %get-tuple-element.50.pick_ref, bf16[8,384,2048]{2,1,0:T(8,128)(2,1)S(1)} %bitcast.7), custom_call_target="tpu_custom_call" | custom-call | flops 1000000000 | bytes 1000 | tf_op jit(solution)/shard_map/pallas_call | solution.py:163
  39.4 1.5 %collective-permute-start.13 = (bf16[128,512]{1,0:T(8,128)(2,1)S(1)}, bf16[128,512]{1,0:T(8,128)(2,1)S(1)}, u32[]{:S(2)}, u32[]{:S(2)}) collective-permute-start(bf16[128,512]{1,0:T(8,128)(2,1)S(1)} %get-tuple-element.67), channel_id=1, source_target_pairs={{0,2},{2,0},{1,3},{3,1},{4,6},{6,4},{5,7},{7,5},{8,10},{10,8},{9,1... | collective-permute-start | bytes 393224 | tf_op jit(solution)/shard_map/ppermute | solution.py:454
  41.4 0.9 %shard_map.149.keep_ref = f32[256,512]{1,0:T(8,128)S(1)} custom-call(bf16[384,384]{1,0:T(8,128)(2,1)S(1)} %shard_map.145.act_ref, f32[384,1]{1,0:T(8,128)S(1)} %get-tuple-element.61.gate_ref, bf16[384,256]{1,0:T(8,128)(2,1)S(1)} %get-tuple-element.50.pick_ref, bf16[8,384,2048]{2,1,0:T(8,128)(2,1)S(1)} %bitcast.7), custom_call_target="tpu_custom_call" | custom-call | flops 1000000000 | bytes 1000 | tf_op jit(solution)/shard_map/pallas_call | solution.py:163
  42.3 3.5 %collective-permute-done.13.other_ref = bf16[128,512]{1,0:T(8,128)(2,1)S(1)} collective-permute-done((bf16[128,512]{1,0:T(8,128)(2,1)S(1)}, bf16[128,512]{1,0:T(8,128)(2,1)S(1)}, u32[]{:S(2)}, u32[]{:S(2)}) %collective-permute-start.13) | collective-permute-done | bytes 131104 | tf_op jit(solution)/shard_map/ppermute | solution.py:454
  45.8 1.2 %collective-permute-start.14 = (bf16[64,512]{1,0:T(8,128)(2,1)S(1)}, bf16[64,512]{1,0:T(8,128)(2,1)S(1)}, u32[]{:S(2)}, u32[]{:S(2)}) collective-permute-start(bf16[64,512]{1,0:T(8,128)(2,1)S(1)} %get-tuple-element.68), channel_id=1, source_target_pairs={{0,8},{4,12},{8,0},{12,4},{1,9},{5,13},{9,1},{13,5},{2,10},{6,14},... | collective-permute-start | bytes 196616 | tf_op jit(solution)/shard_map/ppermute | solution.py:454
  47.0 2.2 %collective-permute-start.15 = (bf16[64,512]{1,0:T(8,128)(2,1)S(1)}, bf16[64,512]{1,0:T(8,128)(2,1)S(1)}, u32[]{:S(2)}, u32[]{:S(2)}) collective-permute-start(bf16[64,512]{1,0:T(8,128)(2,1)S(1)} %get-tuple-element.69), channel_id=1, source_target_pairs={{0,12},{4,8},{8,4},{12,0},{1,13},{5,9},{9,5},{13,1},{2,14},{6,10},... | collective-permute-start | bytes 196616 | tf_op jit(solution)/shard_map/ppermute | solution.py:454
  49.4 3.8 %collective-permute-done.14.refs_0_ = bf16[64,512]{1,0:T(8,128)(2,1)S(1)} collective-permute-done((bf16[64,512]{1,0:T(8,128)(2,1)S(1)}, bf16[64,512]{1,0:T(8,128)(2,1)S(1)}, u32[]{:S(2)}, u32[]{:S(2)}) %collective-permute-start.14) | collective-permute-done | bytes 65568 | tf_op jit(solution)/shard_map/ppermute | solution.py:454
  (49 shorter events, 6.0 us)
Async XLA Ops:
  1.3 6.9 %copy-start.2 = (bf16[1024,1024]{1,0:T(8,128)(2,1)S(1)}, bf16[1024,1024]{1,0:T(8,128)(2,1)}, u32[]{:S(2)}) copy-start(bf16[1024,1024]{1,0:T(8,128)(2,1)} %w_ref.1) | copy-start | bytes 6291460
  1.3 8.8 %copy-start.3 = (bf16[64,1024]{1,0:T(8,128)(2,1)S(1)}, bf16[64,1024]{1,0:T(8,128)(2,1)}, u32[]{:S(2)}) copy-start(bf16[64,1024]{1,0:T(8,128)(2,1)} %res_ref.1) | copy-start | bytes 393220
  1.4 8.7 %copy-start.4 = (f32[1024]{0:T(1024)S(1)}, f32[1024]{0:T(1024)}, u32[]{:S(2)}) copy-start(f32[1024]{0:T(1024)} %param.22) | copy-start | bytes 12292
  1.4 8.7 %copy-start.5 = (s32[64,8]{0,1:T(8,128)S(1)}, s32[64,8]{0,1:T(8,128)}, u32[]{:S(2)}) copy-start(s32[64,8]{0,1:T(8,128)} %param.23) | copy-start | bytes 6148
  1.4 8.7 %copy-start.6 = (f32[64,8]{0,1:T(8,128)S(1)}, f32[64,8]{0,1:T(8,128)}, u32[]{:S(2)}) copy-start(f32[64,8]{0,1:T(8,128)} %param.24) | copy-start | bytes 6148
  1.4 23.5 %copy-start = (bf16[8,384,2048]{2,1,0:T(8,128)(2,1)S(1)}, bf16[8,384,2048]{2,1,0:T(8,128)(2,1)}, u32[]{:S(2)}) copy-start(bf16[8,384,2048]{2,1,0:T(8,128)(2,1)} %wg_ref.5) | copy-start | bytes 37748740
  1.4 23.5 %copy-start.1 = (bf16[8,384,2048]{2,1,0:T(8,128)(2,1)S(1)}, bf16[8,384,2048]{2,1,0:T(8,128)(2,1)}, u32[]{:S(2)}) copy-start(bf16[8,384,2048]{2,1,0:T(8,128)(2,1)} %wu_ref.5) | copy-start | bytes 37748740
  2.9 5.3 %collective-permute-start = (bf16[32,1024]{1,0:T(8,128)(2,1)S(1)}, bf16[32,1024]{1,0:T(8,128)(2,1)S(1)}, u32[]{:S(2)}, u32[]{:S(2)}) collective-permute-start(bf16[32,1024]{1,0:T(8,128)(2,1)S(1)} %shard_map.137.own_ref), channel_id=1, source_target_pairs={{0,2},{2,0},{1,3},{3,1},{4,6},{6,4},{5,7},{7,5},{8,10},{10,8},{9,1... | collective-permute-start | bytes 196616 | tf_op jit(solution)/shard_map/ppermute | solution.py:454
  8.7 1.4 %collective-permute-start.1 = (f32[64,512]{1,0:T(8,128)S(1)}, f32[64,512]{1,0:T(8,128)S(1)}, u32[]{:S(2)}, u32[]{:S(2)}) collective-permute-start(f32[64,512]{1,0:T(8,128)S(1)} %get-tuple-element.45), channel_id=1, source_target_pairs={{0,1},{1,0},{2,3},{3,2},{4,5},{5,4},{6,7},{7,6},{8,9},{9,8},{10,11... | collective-permute-start | bytes 393224 | tf_op jit(solution)/shard_map/ppermute | solution.py:454
  10.2 7.1 %collective-permute-start.4 = (bf16[72,512]{1,0:T(8,128)(2,1)S(1)}, bf16[72,512]{1,0:T(8,128)(2,1)S(1)}, u32[]{:S(2)}, u32[]{:S(2)}) collective-permute-start(bf16[72,512]{1,0:T(8,128)(2,1)S(1)} %get-tuple-element.47.refs_0_), channel_id=1, source_target_pairs={{0,12},{4,8},{8,4},{12,0},{1,13},{5,9},{9,5},{13,1},{2,14},{6,10},... | collective-permute-start | bytes 221192 | tf_op jit(solution)/shard_map/ppermute | solution.py:454
  14.4 6.5 %collective-permute-start.3 = (bf16[72,512]{1,0:T(8,128)(2,1)S(1)}, bf16[72,512]{1,0:T(8,128)(2,1)S(1)}, u32[]{:S(2)}, u32[]{:S(2)}) collective-permute-start(bf16[72,512]{1,0:T(8,128)(2,1)S(1)} %get-tuple-element.47.refs_0_), channel_id=1, source_target_pairs={{0,8},{4,12},{8,0},{12,4},{1,9},{5,13},{9,1},{13,5},{2,10},{6,14},... | collective-permute-start | bytes 221192 | tf_op jit(solution)/shard_map/ppermute | solution.py:454
  14.4 6.5 %collective-permute-start.2 = (bf16[72,512]{1,0:T(8,128)(2,1)S(1)}, bf16[72,512]{1,0:T(8,128)(2,1)S(1)}, u32[]{:S(2)}, u32[]{:S(2)}) collective-permute-start(bf16[72,512]{1,0:T(8,128)(2,1)S(1)} %get-tuple-element.47.refs_0_), channel_id=1, source_target_pairs={{0,4},{4,0},{8,12},{12,8},{1,5},{5,1},{9,13},{13,9},{2,6},{6,2},{1... | collective-permute-start | bytes 221192 | tf_op jit(solution)/shard_map/ppermute | solution.py:454
  20.9 4.0 %collective-permute-start.6 = (bf16[256,512]{1,0:T(8,128)(2,1)S(1)}, bf16[256,512]{1,0:T(8,128)(2,1)S(1)}, u32[]{:S(2)}, u32[]{:S(2)}) collective-permute-start(bf16[256,512]{1,0:T(8,128)(2,1)S(1)} %get-tuple-element.49.mine_ref), channel_id=1, source_target_pairs={{0,1},{1,0},{2,3},{3,2},{4,5},{5,4},{6,7},{7,6},{8,9},{9,8},{10,11... | collective-permute-start | bytes 786440 | tf_op jit(solution)/shard_map/ppermute | solution.py:454
  21.0 9.1 %collective-permute-start.5 = (bf16[128,512]{1,0:T(8,128)(2,1)S(1)}, bf16[128,512]{1,0:T(8,128)(2,1)S(1)}, u32[]{:S(2)}, u32[]{:S(2)}) collective-permute-start(bf16[128,512]{1,0:T(8,128)(2,1)S(1)} %get-tuple-element.48), channel_id=1, source_target_pairs={{0,2},{2,0},{1,3},{3,1},{4,6},{6,4},{5,7},{7,5},{8,10},{10,8},{9,1... | collective-permute-start | bytes 393224 | tf_op jit(solution)/shard_map/ppermute | solution.py:454
  22.5 6.5 %collective-permute-start.7 = (bf16[72,512]{1,0:T(8,128)(2,1)S(1)}, bf16[72,512]{1,0:T(8,128)(2,1)S(1)}, u32[]{:S(2)}, u32[]{:S(2)}) collective-permute-start(bf16[72,512]{1,0:T(8,128)(2,1)S(1)} %get-tuple-element.47.refs_0_), channel_id=1, source_target_pairs={{0,2},{2,0},{1,3},{3,1},{4,6},{6,4},{5,7},{7,5},{8,10},{10,8},{9,1... | collective-permute-start | bytes 221192 | tf_op jit(solution)/shard_map/ppermute | solution.py:454
  23.1 7.0 %collective-permute-start.8 = (bf16[72,512]{1,0:T(8,128)(2,1)S(1)}, bf16[72,512]{1,0:T(8,128)(2,1)S(1)}, u32[]{:S(2)}, u32[]{:S(2)}) collective-permute-start(bf16[72,512]{1,0:T(8,128)(2,1)S(1)} %collective-permute-done.2.refs_1_), channel_id=1, source_target_pairs={{0,2},{2,0},{1,3},{3,1},{4,6},{6,4},{5,7},{7,5},{8,10},{10,8},{9,1... | collective-permute-start | bytes 221192 | tf_op jit(solution)/shard_map/ppermute | solution.py:454
  30.1 1.6 %collective-permute-start.9 = (bf16[264,512]{1,0:T(8,128)(2,1)S(1)}, bf16[264,512]{1,0:T(8,128)(2,1)S(1)}, u32[]{:S(2)}, u32[]{:S(2)}) collective-permute-start(bf16[264,512]{1,0:T(8,128)(2,1)S(1)} %shard_map.143.mine_ref), channel_id=1, source_target_pairs={{0,1},{1,0},{2,3},{3,2},{4,5},{5,4},{6,7},{7,6},{8,9},{9,8},{10,11... | collective-permute-start | bytes 811016 | tf_op jit(solution)/shard_map/ppermute | solution.py:454
  36.6 1.6 %collective-permute-start.10 = (bf16[256,512]{1,0:T(8,128)(2,1)S(1)}, bf16[256,512]{1,0:T(8,128)(2,1)S(1)}, u32[]{:S(2)}, u32[]{:S(2)}) collective-permute-start(bf16[256,512]{1,0:T(8,128)(2,1)S(1)} %shard_map.147), channel_id=1, source_target_pairs={{0,1},{1,0},{2,3},{3,2},{4,5},{5,4},{6,7},{7,6},{8,9},{9,8},{10,11... | collective-permute-start | bytes 786440 | tf_op jit(solution)/shard_map/ppermute | solution.py:454
  39.2 6.6 %collective-permute-start.11 = (bf16[256,512]{1,0:T(8,128)(2,1)S(1)}, bf16[256,512]{1,0:T(8,128)(2,1)S(1)}, u32[]{:S(2)}, u32[]{:S(2)}) collective-permute-start(bf16[256,512]{1,0:T(8,128)(2,1)S(1)} %shard_map.150), channel_id=1, source_target_pairs={{0,1},{1,0},{2,3},{3,2},{4,5},{5,4},{6,7},{7,6},{8,9},{9,8},{10,11... | collective-permute-start | bytes 786440 | tf_op jit(solution)/shard_map/ppermute | solution.py:454
  39.4 6.4 %collective-permute-start.13 = (bf16[128,512]{1,0:T(8,128)(2,1)S(1)}, bf16[128,512]{1,0:T(8,128)(2,1)S(1)}, u32[]{:S(2)}, u32[]{:S(2)}) collective-permute-start(bf16[128,512]{1,0:T(8,128)(2,1)S(1)} %get-tuple-element.67), channel_id=1, source_target_pairs={{0,2},{2,0},{1,3},{3,1},{4,6},{6,4},{5,7},{7,5},{8,10},{10,8},{9,1... | collective-permute-start | bytes 393224 | tf_op jit(solution)/shard_map/ppermute | solution.py:454
  40.9 8.4 %collective-permute-start.12 = (bf16[128,512]{1,0:T(8,128)(2,1)S(1)}, bf16[128,512]{1,0:T(8,128)(2,1)S(1)}, u32[]{:S(2)}, u32[]{:S(2)}) collective-permute-start(bf16[128,512]{1,0:T(8,128)(2,1)S(1)} %get-tuple-element.65), channel_id=1, source_target_pairs={{0,2},{2,0},{1,3},{3,1},{4,6},{6,4},{5,7},{7,5},{8,10},{10,8},{9,1... | collective-permute-start | bytes 393224 | tf_op jit(solution)/shard_map/ppermute | solution.py:454
  45.8 7.4 %collective-permute-start.14 = (bf16[64,512]{1,0:T(8,128)(2,1)S(1)}, bf16[64,512]{1,0:T(8,128)(2,1)S(1)}, u32[]{:S(2)}, u32[]{:S(2)}) collective-permute-start(bf16[64,512]{1,0:T(8,128)(2,1)S(1)} %get-tuple-element.68), channel_id=1, source_target_pairs={{0,8},{4,12},{8,0},{12,4},{1,9},{5,13},{9,1},{13,5},{2,10},{6,14},... | collective-permute-start | bytes 196616 | tf_op jit(solution)/shard_map/ppermute | solution.py:454
  47.0 6.2 %collective-permute-start.15 = (bf16[64,512]{1,0:T(8,128)(2,1)S(1)}, bf16[64,512]{1,0:T(8,128)(2,1)S(1)}, u32[]{:S(2)}, u32[]{:S(2)}) collective-permute-start(bf16[64,512]{1,0:T(8,128)(2,1)S(1)} %get-tuple-element.69), channel_id=1, source_target_pairs={{0,12},{4,8},{8,4},{12,0},{1,13},{5,9},{9,5},{13,1},{2,14},{6,10},... | collective-permute-start | bytes 196616 | tf_op jit(solution)/shard_map/ppermute | solution.py:454
  49.3 4.6 %collective-permute-start.16 = (bf16[64,512]{1,0:T(8,128)(2,1)S(1)}, bf16[64,512]{1,0:T(8,128)(2,1)S(1)}, u32[]{:S(2)}, u32[]{:S(2)}) collective-permute-start(bf16[64,512]{1,0:T(8,128)(2,1)S(1)} %get-tuple-element.70), channel_id=1, source_target_pairs={{0,4},{4,0},{8,12},{12,8},{1,5},{5,1},{9,13},{13,9},{2,6},{6,2},{1... | collective-permute-start | bytes 196616 | tf_op jit(solution)/shard_map/ppermute | solution.py:454
  (3 other events, 15.1 us)
where the time goes:
time: 54.7 us; the launch traced here: 54.6 us
  waiting for transfers between devices  20.5 us (37%)
  starting transfers between devices  17.7 us (32%)
  Pallas kernels  16.1 us (29%)
    ppermute x17, waiting for transfers between devices, swap(): lax.ppermute(value, axis, [(i, i ^ partner) for i in range(lax.axis_size(...  20.5 us
    ppermute x17, starting transfers between devices, swap(): lax.ppermute(value, axis, [(i, i ^ partner) for i in range(lax.axis_size(...  17.7 us
    pallas_call x18, Pallas kernels, pallas_kernel(): pl.pallas_call(body, out_shape=tuple((jax.ShapeDtypeStruct(s, d) for s, d...  16.1 us
  transfers between devices with their start and end apart: 17, of which 11 were waited for; matrix products, arithmetic and copies ran while one was open for 0% of the time, Pallas kernels for 11%

commit v1 on v0

--- a/solution.py
+++ b/solution.py
@@ -273,22 +273,18 @@
     load_ref[rows:, :] = tail_ref[...].astype(BF16)
 
 
-def merge_body(blocks, *refs):
-    all_ref, far_ref = refs[-2:]
-    rows = all_ref.shape[0] // blocks
-    for j in range(blocks):
-        all_ref[rows * j : rows * (j + 1), :] = refs[j][0:rows, :]
-    for j in range(blocks // 2, blocks):
-        start = rows * (j - blocks // 2)
-        far_ref[start : start + rows, :] = refs[j][0:rows, :]
-
-
-def join_body(near, *refs):
+def merge_body(*refs):
+    all_ref = refs[-1]
+    rows = refs[0].shape[0] - TAIL
+    for j, ref in enumerate(refs[:-1]):
+        all_ref[rows * j : rows * (j + 1), :] = ref[0:rows, :]
+
+
+def join_body(*refs):
     out_ref = refs[-1]
     rows = refs[0].shape[0] - TAIL
-    for j in range(near):
-        out_ref[rows * j : rows * (j + 1), :] = refs[j][0:rows, :]
-    out_ref[rows * near : out_ref.shape[0] - TAIL, :] = refs[near][...]
+    for j, ref in enumerate(refs[:-1]):
+        out_ref[rows * j : rows * (j + 1), :] = ref[0:rows, :]
     out_ref[out_ref.shape[0] - TAIL :, :] = refs[0][rows:, :]
 
 
@@ -352,11 +348,11 @@
 def products(rows_ref, w_ref, e, slots, start):
     half_width = rows_ref.shape[1]
     return lax.dot_general(
+        w_ref[e, :, pl.ds(pl.multiple_of(start, half_width), half_width)],
         rows_ref[slots * e : slots * (e + 1), :],
-        w_ref[e, :, pl.ds(pl.multiple_of(start, half_width), half_width)],
         NT,
         preferred_element_type=F32,
-    )
+    ).T
 
 
 def first_half_body(
@@ -426,25 +422,24 @@
     ).astype(out_ref.dtype)
 
 
-def pair_sum_body(keep_ref, got_ref, far_ref, near_ref):
-    rows = near_ref.shape[0]
-    for out, start in ((near_ref, 0), (far_ref, rows)):
+def pair_sum_body(keep_ref, got_ref, *outs):
+    start = 0
+    for out in outs:
         here = slice(start, start + out.shape[0])
         out[...] = (keep_ref[here, :] + got_ref[here, :].astype(F32)).astype(BF16)
-
-
-def block_sum_body(start, keep_ref, got_ref, other_ref, *outs):
-    rows = outs[0].shape[0]
-    for j, out in enumerate(outs):
-        here = slice(start + rows * j, start + rows * (j + 1))
-        total = keep_ref[here, :] + got_ref[here, :].astype(F32)
-        total = total + other_ref[rows * j : rows * (j + 1), :].astype(F32)
-        out[...] = total.astype(out.dtype)
-
-
-def final_body(h32_ref, own_ref, *refs):
+        start += out.shape[0]
+
+
+def block_sum_body(start, keep_ref, got_ref, other_ref, out_ref):
+    here = slice(start, start + out_ref.shape[0])
+    total = keep_ref[here, :] + got_ref[here, :].astype(F32) + other_ref[...].astype(F32)
+    out_ref[...] = total.astype(BF16)
+
+
+def final_body(h32_ref, keep_ref, got_ref, *refs):
     out_ref = refs[-1]
-    total = own_ref[...]
+    here = slice(0, out_ref.shape[0])
+    total = keep_ref[here, :] + got_ref[here, :].astype(F32)
     for ref in refs[:-1]:
         total = total + ref[...].astype(F32)
     out_ref[...] = (h32_ref[...] + total).astype(BF16)
@@ -526,15 +521,9 @@
         args=(residual, expert_ids.T, gate_weights.T, gain, keep, swap(send, "tp")),
     )
     arrived = [payload] + [swap(payload, "ep", j) for j in range(1, blocks)]
-    near = blocks // 2
-    near_x = [swap(arrived[j], "half") for j in range(near)]
-    mine, far = kernel_call(
-        functools.partial(merge_body, blocks),
-        [((tokens, cols), BF16), ((tokens // 2, cols), BF16)],
-        args=arrived,
-    )
+    from_x = [swap(v, "half") for v in arrived]
+    (mine,) = kernel_call(merge_body, [((tokens, cols), BF16)], args=arrived)
     theirs = swap(mine, "tp")
-    far_x = swap(far, "half")
     pick, gate = kernel_call(
         functools.partial(pick_body, blocks),
         [((slot_rows, tokens), BF16), ((slot_rows, 1), F32)],
@@ -551,10 +540,8 @@
         ],
         args=(mine, theirs, gain, w_gate, w_up, pick),
     )
-    far_x, squares, near_x = lax.optimization_barrier((far_x, squares, near_x))
-    (mine_x,) = kernel_call(
-        functools.partial(join_body, near), [((tokens + TAIL, cols), BF16)], args=(*near_x, far_x)
-    )
+    from_x, squares = lax.optimization_barrier((from_x, squares))
+    (mine_x,) = kernel_call(join_body, [((tokens + TAIL, cols), BF16)], args=from_x)
     theirs_x = swap(mine_x, "tp")
     gate_b, up_b = kernel_call(
         functools.partial(more_first_half_body, slots, early),
@@ -581,30 +568,23 @@
 
     got_a = swap(down(act, True, True), "tp")
     keep_a = down(act, True, False)
-    near_rows = tokens // 2
-    far, near = kernel_call(
-        pair_sum_body,
-        [((tokens - near_rows, cols), BF16), ((near_rows, cols), BF16)],
-        args=(keep_a, got_a),
-    )
-    act, far, near = lax.optimization_barrier((act, far, near))
-    far_x = swap(far, "half")
-    near_x = swap(near, "half")
+    sums = kernel_call(pair_sum_body, [((token_rows, cols), BF16)] * blocks, args=(keep_a, got_a))
+    act, sums = lax.optimization_barrier((act, sums))
+    from_x = [swap(v, "half") for v in sums]
     got_b = swap(down(act, False, True), "tp")
     keep_b = down(act, False, False)
-    far_sums = kernel_call(
-        functools.partial(block_sum_body, near_rows),
-        [((token_rows, cols), BF16)] * (blocks // 2),
-        args=(keep_b, got_b, far_x),
-    )
-    near_sums = kernel_call(
-        functools.partial(block_sum_body, 0),
-        [((token_rows, cols), F32)] + [((token_rows, cols), BF16)] * (blocks // 2 - 1),
-        args=(keep_b, got_b, near_x),
-    )
-    home = [swap(v, "ep", blocks // 2 + j) for j, v in enumerate(far_sums)]
-    home += [swap(v, "ep", 1 + j) for j, v in enumerate(near_sums[1:])]
-    (out,) = kernel_call(final_body, [((token_rows, cols), BF16)], args=(h32, near_sums[0], *home))
+
+    home = []
+    for j in range(blocks - 1, 0, -1):
+        (total,) = kernel_call(
+            functools.partial(block_sum_body, j * token_rows),
+            [((token_rows, cols), BF16)],
+            args=(keep_b, got_b, from_x[j]),
+        )
+        home.append(swap(total, "ep", j))
+    (out,) = kernel_call(
+        final_body, [((token_rows, cols), BF16)], args=(h32, keep_b, got_b, from_x[0], *home)
+    )
     return out
 
 

time: 54.7 us -> 55.2 us (level)
  starting transfers between devices: 17.7 us -> 21.2 us
  waiting for transfers between devices: 20.5 us -> 17.6 us
    ppermute x17 -> x20, starting transfers between devices: 17.7 us -> 21.2 us  [swap(): lax.ppermute(value, axis, [(i, i ^ partner) for i in range(lax.axis_size(...]
    ppermute x17 -> x20, waiting for transfers between devices: 20.5 us -> 17.6 us  [swap(): lax.ppermute(value, axis, [(i, i ^ partner) for i in range(lax.axis_size(...]
    pallas_call x18 -> x19, Pallas kernels: 16.1 us -> 15.9 us  [pallas_kernel(): pl.pallas_call(body, out_shape=tuple((jax.ShapeDtypeStruct(s, d) for s, d...]
  transfers between devices with their start and end apart: 17 -> 20, of which waited for: 11 -> 11; matrix products, arithmetic and copies ran while one was open for 0% -> 0% of each run, Pallas kernels for 11% -> 11%
where the time goes in v1:
time: 55.2 us; the launch traced here: 55 us
  starting transfers between devices  21.2 us (38%)
  waiting for transfers between devices  17.6 us (32%)
  Pallas kernels  15.9 us (29%)
    ppermute x20, starting transfers between devices, swap(): lax.ppermute(value, axis, [(i, i ^ partner) for i in range(lax.axis_size(...  21.2 us
    ppermute x20, waiting for transfers between devices, swap(): lax.ppermute(value, axis, [(i, i ^ partner) for i in range(lax.axis_size(...  17.6 us
    pallas_call x19, Pallas kernels, pallas_kernel(): pl.pallas_call(body, out_shape=tuple((jax.ShapeDtypeStruct(s, d) for s, d...  15.9 us
  transfers between devices with their start and end apart: 20, of which 11 were waited for; matrix products, arithmetic and copies ran while one was open for 0% of the time, Pallas kernels for 11%

profile of v1, /device:TPU:0, one launch (start us, length us, event | category | flops | bytes accessed | tf_op | source)
XLA Modules:
  0.0 55.0 jit_solution(427638101907420733)
XLA Ops:
  0.0 1.3 %shard_map.136 = (bf16[32,1024]{1,0:T(8,128)(2,1)S(1)}, bf16[32,128]{1,0:T(8,128)(2,1)S(1)}, bf16[32,128]{1,0:T(8,128)(2,1)S(1)}, bf16[2048,128]{1,0:T(8,128)(2,...) custom-call(bf16[32,1024]{1,0:T(8,128)(2,1)} %refs_0_.1, bf16[32,128]{1,0:T(8,128)(2,1)} %refs_1_.1, ...), custom_call_target="tpu_custom_call" | custom-call | flops 1000 | bytes 1000 | tf_op jit(solution)/shard_map/pallas_call | solution.py:163
  1.4 1.5 %shard_map.137.own_ref = bf16[32,1024]{1,0:T(8,128)(2,1)S(1)} custom-call(bf16[32,1024]{1,0:T(8,128)(2,1)S(1)} %get-tuple-element.37.q_ref, bf16[32,128]{1,0:T(8,128)(2,1)S(1)} %get-tuple-element.38.nk_ref, bf16[32,128]{1,0:T(8,128)(2,1)S(1)} %get-tuple-element.39.nv_ref, bf16[2048,128]{1,0:T(8,128)(2,1)S(1)} %get-tuple-element.40.k_ref, ...), custom_call_target="tpu_custom_call" | custom-call | flops 99999997952 | bytes 1000 | tf_op jit(solution)/shard_map/pallas_call | solution.py:163
  2.9 3.0 %collective-permute-start = (bf16[32,1024]{1,0:T(8,128)(2,1)S(1)}, bf16[32,1024]{1,0:T(8,128)(2,1)S(1)}, u32[]{:S(2)}, u32[]{:S(2)}) collective-permute-start(bf16[32,1024]{1,0:T(8,128)(2,1)S(1)} %shard_map.137.own_ref), channel_id=1, source_target_pairs={{0,2},{2,0},{1,3},{3,1},{4,6},{6,4},{5,7},{7,5},{8,10},{10,8},{9,1... | collective-permute-start | bytes 196616 | tf_op jit(solution)/shard_map/ppermute | solution.py:449
  5.9 2.2 %collective-permute-done.other_ref = bf16[32,1024]{1,0:T(8,128)(2,1)S(1)} collective-permute-done((bf16[32,1024]{1,0:T(8,128)(2,1)S(1)}, bf16[32,1024]{1,0:T(8,128)(2,1)S(1)}, u32[]{:S(2)}, u32[]{:S(2)}) %collective-permute-start) | collective-permute-done | bytes 65568 | tf_op jit(solution)/shard_map/ppermute | solution.py:449
  8.8 1.3 %collective-permute-done.1.got_ref = f32[64,512]{1,0:T(8,128)S(1)} collective-permute-done((f32[64,512]{1,0:T(8,128)S(1)}, f32[64,512]{1,0:T(8,128)S(1)}, u32[]{:S(2)}, u32[]{:S(2)}) %collective-permute-start.1) | collective-permute-done | bytes 131104 | tf_op jit(solution)/shard_map/ppermute | solution.py:449
  10.2 4.2 %collective-permute-start.7 = (bf16[72,512]{1,0:T(8,128)(2,1)S(1)}, bf16[72,512]{1,0:T(8,128)(2,1)S(1)}, u32[]{:S(2)}, u32[]{:S(2)}) collective-permute-start(bf16[72,512]{1,0:T(8,128)(2,1)S(1)} %get-tuple-element.46.refs_0_), channel_id=1, source_target_pairs={{0,12},{4,8},{8,4},{12,0},{1,13},{5,9},{9,5},{13,1},{2,14},{6,10},... | collective-permute-start | bytes 221192 | tf_op jit(solution)/shard_map/ppermute | solution.py:449
  15.0 2.3 %collective-permute-done.7.refs_3_ = bf16[72,512]{1,0:T(8,128)(2,1)S(1)} collective-permute-done((bf16[72,512]{1,0:T(8,128)(2,1)S(1)}, bf16[72,512]{1,0:T(8,128)(2,1)S(1)}, u32[]{:S(2)}, u32[]{:S(2)}) %collective-permute-start.7) | collective-permute-done | bytes 73760 | tf_op jit(solution)/shard_map/ppermute | solution.py:449
  17.3 3.5 %collective-permute-done.5.refs_2_ = bf16[72,512]{1,0:T(8,128)(2,1)S(1)} collective-permute-done((bf16[72,512]{1,0:T(8,128)(2,1)S(1)}, bf16[72,512]{1,0:T(8,128)(2,1)S(1)}, u32[]{:S(2)}, u32[]{:S(2)}) %collective-permute-start.5) | collective-permute-done | bytes 73760 | tf_op jit(solution)/shard_map/ppermute | solution.py:449
  21.0 1.6 %collective-permute-start.2 = (bf16[72,512]{1,0:T(8,128)(2,1)S(1)}, bf16[72,512]{1,0:T(8,128)(2,1)S(1)}, u32[]{:S(2)}, u32[]{:S(2)}) collective-permute-start(bf16[72,512]{1,0:T(8,128)(2,1)S(1)} %get-tuple-element.46.refs_0_), channel_id=1, source_target_pairs={{0,2},{2,0},{1,3},{3,1},{4,6},{6,4},{5,7},{7,5},{8,10},{10,8},{9,1... | collective-permute-start | bytes 221192 | tf_op jit(solution)/shard_map/ppermute | solution.py:449
  23.1 1.5 %collective-permute-start.6 = (bf16[72,512]{1,0:T(8,128)(2,1)S(1)}, bf16[72,512]{1,0:T(8,128)(2,1)S(1)}, u32[]{:S(2)}, u32[]{:S(2)}) collective-permute-start(bf16[72,512]{1,0:T(8,128)(2,1)S(1)} %collective-permute-done.5.refs_2_), channel_id=1, source_target_pairs={{0,2},{2,0},{1,3},{3,1},{4,6},{6,4},{5,7},{7,5},{8,10},{10,8},{9,1... | collective-permute-start | bytes 221192 | tf_op jit(solution)/shard_map/ppermute | solution.py:449
  25.5 3.0 %shard_map.142 = (f32[384,1]{1,0:T(8,128)S(1)}, bf16[384,1024]{1,0:T(8,128)(2,1)S(1)}, f32[288,384]{1,0:T(8,128)S(1)}, f32[288,384]{1,0:T(8,128)S(1)}) custom-call(bf16[256,512]{1,0:T(8,128)(2,1)S(1)} %shard_map.140.mine_ref, bf16[256,512]{1,0:T(8,128)(2,1)S(1)} %collective-permute-done.9.theirs_ref, f32[1,1024]{1,0:T(1,128)S(1)} %bitcast.9, ...), custom_call_target="tpu_custom_call" | custom-call | flops 1000 | bytes 1000 | tf_op jit(solution)/shard_map/pallas_call | solution.py:163
  29.3 1.1 %collective-permute-done.4.refs_1_ = bf16[72,512]{1,0:T(8,128)(2,1)S(1)} collective-permute-done((bf16[72,512]{1,0:T(8,128)(2,1)S(1)}, bf16[72,512]{1,0:T(8,128)(2,1)S(1)}, u32[]{:S(2)}, u32[]{:S(2)}) %collective-permute-start.4) | collective-permute-done | bytes 73760 | tf_op jit(solution)/shard_map/ppermute | solution.py:449
  30.5 1.0 %shard_map.144 = (f32[96,384]{1,0:T(8,128)S(1)}, f32[96,384]{1,0:T(8,128)S(1)}) custom-call(bf16[384,1024]{1,0:T(8,128)(2,1)S(1)} %get-tuple-element.56.rows_ref, bf16[8,384,2048]{2,1,0:T(8,128)(2,1)S(1)} %copy-done, bf16[8,384,2048]{2,1,0:T(8,128)(2,1)S(1)} %copy-done.1), custom_call_target="tpu_custom_call" | custom-call | flops 1000 | bytes 1000 | tf_op jit(solution)/shard_map/pallas_call | solution.py:163
  32.0 3.8 %shard_map.145.act_ref = bf16[384,384]{1,0:T(8,128)(2,1)S(1)} custom-call(bf16[264,512]{1,0:T(8,128)(2,1)S(1)} %shard_map.143.mine_ref, bf16[264,512]{1,0:T(8,128)(2,1)S(1)} %collective-permute-done.10.theirs_ref, bf16[8,384,2048]{2,1,0:T(8,128)(2,1)S(1)} %copy-done, bf16[8,384,2048]{2,1,0:T(8,128)(2,1)S(1)} %copy-done.1, ...), custom_call_target="tpu_custom_call" | custom-call | flops 1000 | bytes 1000 | tf_op jit(solution)/shard_map/pallas_call | solution.py:163
  35.9 0.9 %shard_map.147 = bf16[256,512]{1,0:T(8,128)(2,1)S(1)} custom-call(bf16[384,384]{1,0:T(8,128)(2,1)S(1)} %shard_map.145.act_ref, f32[384,1]{1,0:T(8,128)S(1)} %get-tuple-element.59.gate_ref, bf16[384,256]{1,0:T(8,128)(2,1)S(1)} %get-tuple-element.47.pick_ref, bf16[8,384,2048]{2,1,0:T(8,128)(2,1)S(1)} %bitcast.7), custom_call_target="tpu_custom_call" | custom-call | flops 1000000000 | bytes 1000 | tf_op jit(solution)/shard_map/pallas_call | solution.py:163
  37.0 0.9 %shard_map.146.keep_ref = f32[256,512]{1,0:T(8,128)S(1)} custom-call(bf16[384,384]{1,0:T(8,128)(2,1)S(1)} %shard_map.145.act_ref, f32[384,1]{1,0:T(8,128)S(1)} %get-tuple-element.59.gate_ref, bf16[384,256]{1,0:T(8,128)(2,1)S(1)} %get-tuple-element.47.pick_ref, bf16[8,384,2048]{2,1,0:T(8,128)(2,1)S(1)} %bitcast.7), custom_call_target="tpu_custom_call" | custom-call | flops 1000000000 | bytes 1000 | tf_op jit(solution)/shard_map/pallas_call | solution.py:163
  38.5 0.9 %shard_map.150 = bf16[256,512]{1,0:T(8,128)(2,1)S(1)} custom-call(bf16[384,384]{1,0:T(8,128)(2,1)S(1)} %shard_map.145.act_ref, f32[384,1]{1,0:T(8,128)S(1)} %get-tuple-element.59.gate_ref, bf16[384,256]{1,0:T(8,128)(2,1)S(1)} %get-tuple-element.47.pick_ref, bf16[8,384,2048]{2,1,0:T(8,128)(2,1)S(1)} %bitcast.7), custom_call_target="tpu_custom_call" | custom-call | flops 1000000000 | bytes 1000 | tf_op jit(solution)/shard_map/pallas_call | solution.py:163
  39.5 1.5 %collective-permute-start.13 = (bf16[64,512]{1,0:T(8,128)(2,1)S(1)}, bf16[64,512]{1,0:T(8,128)(2,1)S(1)}, u32[]{:S(2)}, u32[]{:S(2)}) collective-permute-start(bf16[64,512]{1,0:T(8,128)(2,1)S(1)} %get-tuple-element.65), channel_id=1, source_target_pairs={{0,2},{2,0},{1,3},{3,1},{4,6},{6,4},{5,7},{7,5},{8,10},{10,8},{9,1... | collective-permute-start | bytes 196616 | tf_op jit(solution)/shard_map/ppermute | solution.py:449
  41.6 1.5 %collective-permute-start.16 = (bf16[64,512]{1,0:T(8,128)(2,1)S(1)}, bf16[64,512]{1,0:T(8,128)(2,1)S(1)}, u32[]{:S(2)}, u32[]{:S(2)}) collective-permute-start(bf16[64,512]{1,0:T(8,128)(2,1)S(1)} %get-tuple-element.67), channel_id=1, source_target_pairs={{0,2},{2,0},{1,3},{3,1},{4,6},{6,4},{5,7},{7,5},{8,10},{10,8},{9,1... | collective-permute-start | bytes 196616 | tf_op jit(solution)/shard_map/ppermute | solution.py:449
  44.5 1.5 %collective-permute-done.14.other_ref = bf16[64,512]{1,0:T(8,128)(2,1)S(1)} collective-permute-done((bf16[64,512]{1,0:T(8,128)(2,1)S(1)}, bf16[64,512]{1,0:T(8,128)(2,1)S(1)}, u32[]{:S(2)}, u32[]{:S(2)}) %collective-permute-start.14) | collective-permute-done | bytes 65568 | tf_op jit(solution)/shard_map/ppermute | solution.py:449
  46.0 2.5 %collective-permute-start.15 = (bf16[64,512]{1,0:T(8,128)(2,1)S(1)}, bf16[64,512]{1,0:T(8,128)(2,1)S(1)}, u32[]{:S(2)}, u32[]{:S(2)}) collective-permute-start(bf16[64,512]{1,0:T(8,128)(2,1)S(1)} %shard_map.151), channel_id=1, source_target_pairs={{0,12},{4,8},{8,4},{12,0},{1,13},{5,9},{9,5},{13,1},{2,14},{6,10},... | collective-permute-start | bytes 196616 | tf_op jit(solution)/shard_map/ppermute | solution.py:449
  48.7 2.0 %collective-permute-start.19 = (bf16[64,512]{1,0:T(8,128)(2,1)S(1)}, bf16[64,512]{1,0:T(8,128)(2,1)S(1)}, u32[]{:S(2)}, u32[]{:S(2)}) collective-permute-start(bf16[64,512]{1,0:T(8,128)(2,1)S(1)} %shard_map.153), channel_id=1, source_target_pairs={{0,4},{4,0},{8,12},{12,8},{1,5},{5,1},{9,13},{13,9},{2,6},{6,2},{1... | collective-permute-start | bytes 196616 | tf_op jit(solution)/shard_map/ppermute | solution.py:449
  50.7 1.7 %collective-permute-done.15.refs_1_ = bf16[64,512]{1,0:T(8,128)(2,1)S(1)} collective-permute-done((bf16[64,512]{1,0:T(8,128)(2,1)S(1)}, bf16[64,512]{1,0:T(8,128)(2,1)S(1)}, u32[]{:S(2)}, u32[]{:S(2)}) %collective-permute-start.15) | collective-permute-done | bytes 65568 | tf_op jit(solution)/shard_map/ppermute | solution.py:449
  52.4 1.9 %collective-permute-done.17.refs_2_ = bf16[64,512]{1,0:T(8,128)(2,1)S(1)} collective-permute-done((bf16[64,512]{1,0:T(8,128)(2,1)S(1)}, bf16[64,512]{1,0:T(8,128)(2,1)S(1)}, u32[]{:S(2)}, u32[]{:S(2)}) %collective-permute-start.17) | collective-permute-done | bytes 65568 | tf_op jit(solution)/shard_map/ppermute | solution.py:449
  (56 shorter events, 7.9 us)
Async XLA Ops:
  1.3 8.8 %copy-start.3 = (bf16[64,1024]{1,0:T(8,128)(2,1)S(1)}, bf16[64,1024]{1,0:T(8,128)(2,1)}, u32[]{:S(2)}) copy-start(bf16[64,1024]{1,0:T(8,128)(2,1)} %res_ref.1) | copy-start | bytes 393220
  1.4 8.7 %copy-start.4 = (f32[1024]{0:T(1024)S(1)}, f32[1024]{0:T(1024)}, u32[]{:S(2)}) copy-start(f32[1024]{0:T(1024)} %param.22) | copy-start | bytes 12292
  1.4 24.1 %copy-start = (bf16[8,384,2048]{2,1,0:T(8,128)(2,1)S(1)}, bf16[8,384,2048]{2,1,0:T(8,128)(2,1)}, u32[]{:S(2)}) copy-start(bf16[8,384,2048]{2,1,0:T(8,128)(2,1)} %wg_ref.5) | copy-start | bytes 37748740
  1.4 24.1 %copy-start.1 = (bf16[8,384,2048]{2,1,0:T(8,128)(2,1)S(1)}, bf16[8,384,2048]{2,1,0:T(8,128)(2,1)}, u32[]{:S(2)}) copy-start(bf16[8,384,2048]{2,1,0:T(8,128)(2,1)} %wu_ref.5) | copy-start | bytes 37748740
  2.9 5.3 %collective-permute-start = (bf16[32,1024]{1,0:T(8,128)(2,1)S(1)}, bf16[32,1024]{1,0:T(8,128)(2,1)S(1)}, u32[]{:S(2)}, u32[]{:S(2)}) collective-permute-start(bf16[32,1024]{1,0:T(8,128)(2,1)S(1)} %shard_map.137.own_ref), channel_id=1, source_target_pairs={{0,2},{2,0},{1,3},{3,1},{4,6},{6,4},{5,7},{7,5},{8,10},{10,8},{9,1... | collective-permute-start | bytes 196616 | tf_op jit(solution)/shard_map/ppermute | solution.py:449
  8.7 1.4 %collective-permute-start.1 = (f32[64,512]{1,0:T(8,128)S(1)}, f32[64,512]{1,0:T(8,128)S(1)}, u32[]{:S(2)}, u32[]{:S(2)}) collective-permute-start(f32[64,512]{1,0:T(8,128)S(1)} %get-tuple-element.44), channel_id=1, source_target_pairs={{0,1},{1,0},{2,3},{3,2},{4,5},{5,4},{6,7},{7,6},{8,9},{9,8},{10,11... | collective-permute-start | bytes 393224 | tf_op jit(solution)/shard_map/ppermute | solution.py:449
  10.2 7.1 %collective-permute-start.7 = (bf16[72,512]{1,0:T(8,128)(2,1)S(1)}, bf16[72,512]{1,0:T(8,128)(2,1)S(1)}, u32[]{:S(2)}, u32[]{:S(2)}) collective-permute-start(bf16[72,512]{1,0:T(8,128)(2,1)S(1)} %get-tuple-element.46.refs_0_), channel_id=1, source_target_pairs={{0,12},{4,8},{8,4},{12,0},{1,13},{5,9},{9,5},{13,1},{2,14},{6,10},... | collective-permute-start | bytes 221192 | tf_op jit(solution)/shard_map/ppermute | solution.py:449
  14.4 6.5 %collective-permute-start.5 = (bf16[72,512]{1,0:T(8,128)(2,1)S(1)}, bf16[72,512]{1,0:T(8,128)(2,1)S(1)}, u32[]{:S(2)}, u32[]{:S(2)}) collective-permute-start(bf16[72,512]{1,0:T(8,128)(2,1)S(1)} %get-tuple-element.46.refs_0_), channel_id=1, source_target_pairs={{0,8},{4,12},{8,0},{12,4},{1,9},{5,13},{9,1},{13,5},{2,10},{6,14},... | collective-permute-start | bytes 221192 | tf_op jit(solution)/shard_map/ppermute | solution.py:449
  14.4 6.5 %collective-permute-start.3 = (bf16[72,512]{1,0:T(8,128)(2,1)S(1)}, bf16[72,512]{1,0:T(8,128)(2,1)S(1)}, u32[]{:S(2)}, u32[]{:S(2)}) collective-permute-start(bf16[72,512]{1,0:T(8,128)(2,1)S(1)} %get-tuple-element.46.refs_0_), channel_id=1, source_target_pairs={{0,4},{4,0},{8,12},{12,8},{1,5},{5,1},{9,13},{13,9},{2,6},{6,2},{1... | collective-permute-start | bytes 221192 | tf_op jit(solution)/shard_map/ppermute | solution.py:449
  20.9 4.6 %collective-permute-start.9 = (bf16[256,512]{1,0:T(8,128)(2,1)S(1)}, bf16[256,512]{1,0:T(8,128)(2,1)S(1)}, u32[]{:S(2)}, u32[]{:S(2)}) collective-permute-start(bf16[256,512]{1,0:T(8,128)(2,1)S(1)} %shard_map.140.mine_ref), channel_id=1, source_target_pairs={{0,1},{1,0},{2,3},{3,2},{4,5},{5,4},{6,7},{7,6},{8,9},{9,8},{10,11... | collective-permute-start | bytes 786440 | tf_op jit(solution)/shard_map/ppermute | solution.py:449
  21.0 7.5 %collective-permute-start.2 = (bf16[72,512]{1,0:T(8,128)(2,1)S(1)}, bf16[72,512]{1,0:T(8,128)(2,1)S(1)}, u32[]{:S(2)}, u32[]{:S(2)}) collective-permute-start(bf16[72,512]{1,0:T(8,128)(2,1)S(1)} %get-tuple-element.46.refs_0_), channel_id=1, source_target_pairs={{0,2},{2,0},{1,3},{3,1},{4,6},{6,4},{5,7},{7,5},{8,10},{10,8},{9,1... | collective-permute-start | bytes 221192 | tf_op jit(solution)/shard_map/ppermute | solution.py:449
  22.5 5.9 %collective-permute-start.8 = (bf16[72,512]{1,0:T(8,128)(2,1)S(1)}, bf16[72,512]{1,0:T(8,128)(2,1)S(1)}, u32[]{:S(2)}, u32[]{:S(2)}) collective-permute-start(bf16[72,512]{1,0:T(8,128)(2,1)S(1)} %collective-permute-done.7.refs_3_), channel_id=1, source_target_pairs={{0,2},{2,0},{1,3},{3,1},{4,6},{6,4},{5,7},{7,5},{8,10},{10,8},{9,1... | collective-permute-start | bytes 221192 | tf_op jit(solution)/shard_map/ppermute | solution.py:449
  23.1 6.2 %collective-permute-start.6 = (bf16[72,512]{1,0:T(8,128)(2,1)S(1)}, bf16[72,512]{1,0:T(8,128)(2,1)S(1)}, u32[]{:S(2)}, u32[]{:S(2)}) collective-permute-start(bf16[72,512]{1,0:T(8,128)(2,1)S(1)} %collective-permute-done.5.refs_2_), channel_id=1, source_target_pairs={{0,2},{2,0},{1,3},{3,1},{4,6},{6,4},{5,7},{7,5},{8,10},{10,8},{9,1... | collective-permute-start | bytes 221192 | tf_op jit(solution)/shard_map/ppermute | solution.py:449
  24.6 5.8 %collective-permute-start.4 = (bf16[72,512]{1,0:T(8,128)(2,1)S(1)}, bf16[72,512]{1,0:T(8,128)(2,1)S(1)}, u32[]{:S(2)}, u32[]{:S(2)}) collective-permute-start(bf16[72,512]{1,0:T(8,128)(2,1)S(1)} %collective-permute-done.3.refs_1_), channel_id=1, source_target_pairs={{0,2},{2,0},{1,3},{3,1},{4,6},{6,4},{5,7},{7,5},{8,10},{10,8},{9,1... | collective-permute-start | bytes 221192 | tf_op jit(solution)/shard_map/ppermute | solution.py:449
  30.4 1.6 %collective-permute-start.10 = (bf16[264,512]{1,0:T(8,128)(2,1)S(1)}, bf16[264,512]{1,0:T(8,128)(2,1)S(1)}, u32[]{:S(2)}, u32[]{:S(2)}) collective-permute-start(bf16[264,512]{1,0:T(8,128)(2,1)S(1)} %shard_map.143.mine_ref), channel_id=1, source_target_pairs={{0,1},{1,0},{2,3},{3,2},{4,5},{5,4},{6,7},{7,6},{8,9},{9,8},{10,11... | collective-permute-start | bytes 811016 | tf_op jit(solution)/shard_map/ppermute | solution.py:449
  36.8 1.6 %collective-permute-start.11 = (bf16[256,512]{1,0:T(8,128)(2,1)S(1)}, bf16[256,512]{1,0:T(8,128)(2,1)S(1)}, u32[]{:S(2)}, u32[]{:S(2)}) collective-permute-start(bf16[256,512]{1,0:T(8,128)(2,1)S(1)} %shard_map.147), channel_id=1, source_target_pairs={{0,1},{1,0},{2,3},{3,2},{4,5},{5,4},{6,7},{7,6},{8,9},{9,8},{10,11... | collective-permute-start | bytes 786440 | tf_op jit(solution)/shard_map/ppermute | solution.py:449
  39.4 6.6 %collective-permute-start.12 = (bf16[256,512]{1,0:T(8,128)(2,1)S(1)}, bf16[256,512]{1,0:T(8,128)(2,1)S(1)}, u32[]{:S(2)}, u32[]{:S(2)}) collective-permute-start(bf16[256,512]{1,0:T(8,128)(2,1)S(1)} %shard_map.150), channel_id=1, source_target_pairs={{0,1},{1,0},{2,3},{3,2},{4,5},{5,4},{6,7},{7,6},{8,9},{9,8},{10,11... | collective-permute-start | bytes 786440 | tf_op jit(solution)/shard_map/ppermute | solution.py:449
  39.5 11.1 %collective-permute-start.13 = (bf16[64,512]{1,0:T(8,128)(2,1)S(1)}, bf16[64,512]{1,0:T(8,128)(2,1)S(1)}, u32[]{:S(2)}, u32[]{:S(2)}) collective-permute-start(bf16[64,512]{1,0:T(8,128)(2,1)S(1)} %get-tuple-element.65), channel_id=1, source_target_pairs={{0,2},{2,0},{1,3},{3,1},{4,6},{6,4},{5,7},{7,5},{8,10},{10,8},{9,1... | collective-permute-start | bytes 196616 | tf_op jit(solution)/shard_map/ppermute | solution.py:449
  41.0 5.0 %collective-permute-start.14 = (bf16[64,512]{1,0:T(8,128)(2,1)S(1)}, bf16[64,512]{1,0:T(8,128)(2,1)S(1)}, u32[]{:S(2)}, u32[]{:S(2)}) collective-permute-start(bf16[64,512]{1,0:T(8,128)(2,1)S(1)} %get-tuple-element.66), channel_id=1, source_target_pairs={{0,2},{2,0},{1,3},{3,1},{4,6},{6,4},{5,7},{7,5},{8,10},{10,8},{9,1... | collective-permute-start | bytes 196616 | tf_op jit(solution)/shard_map/ppermute | solution.py:449
  41.6 7.0 %collective-permute-start.16 = (bf16[64,512]{1,0:T(8,128)(2,1)S(1)}, bf16[64,512]{1,0:T(8,128)(2,1)S(1)}, u32[]{:S(2)}, u32[]{:S(2)}) collective-permute-start(bf16[64,512]{1,0:T(8,128)(2,1)S(1)} %get-tuple-element.67), channel_id=1, source_target_pairs={{0,2},{2,0},{1,3},{3,1},{4,6},{6,4},{5,7},{7,5},{8,10},{10,8},{9,1... | collective-permute-start | bytes 196616 | tf_op jit(solution)/shard_map/ppermute | solution.py:449
  43.1 5.6 %collective-permute-start.18 = (bf16[64,512]{1,0:T(8,128)(2,1)S(1)}, bf16[64,512]{1,0:T(8,128)(2,1)S(1)}, u32[]{:S(2)}, u32[]{:S(2)}) collective-permute-start(bf16[64,512]{1,0:T(8,128)(2,1)S(1)} %get-tuple-element.68), channel_id=1, source_target_pairs={{0,2},{2,0},{1,3},{3,1},{4,6},{6,4},{5,7},{7,5},{8,10},{10,8},{9,1... | collective-permute-start | bytes 196616 | tf_op jit(solution)/shard_map/ppermute | solution.py:449
  46.0 6.3 %collective-permute-start.15 = (bf16[64,512]{1,0:T(8,128)(2,1)S(1)}, bf16[64,512]{1,0:T(8,128)(2,1)S(1)}, u32[]{:S(2)}, u32[]{:S(2)}) collective-permute-start(bf16[64,512]{1,0:T(8,128)(2,1)S(1)} %shard_map.151), channel_id=1, source_target_pairs={{0,12},{4,8},{8,4},{12,0},{1,13},{5,9},{9,5},{13,1},{2,14},{6,10},... | collective-permute-start | bytes 196616 | tf_op jit(solution)/shard_map/ppermute | solution.py:449
  48.6 5.7 %collective-permute-start.17 = (bf16[64,512]{1,0:T(8,128)(2,1)S(1)}, bf16[64,512]{1,0:T(8,128)(2,1)S(1)}, u32[]{:S(2)}, u32[]{:S(2)}) collective-permute-start(bf16[64,512]{1,0:T(8,128)(2,1)S(1)} %shard_map.152), channel_id=1, source_target_pairs={{0,8},{4,12},{8,0},{12,4},{1,9},{5,13},{9,1},{13,5},{2,10},{6,14},... | collective-permute-start | bytes 196616 | tf_op jit(solution)/shard_map/ppermute | solution.py:449
  48.7 5.6 %collective-permute-start.19 = (bf16[64,512]{1,0:T(8,128)(2,1)S(1)}, bf16[64,512]{1,0:T(8,128)(2,1)S(1)}, u32[]{:S(2)}, u32[]{:S(2)}) collective-permute-start(bf16[64,512]{1,0:T(8,128)(2,1)S(1)} %shard_map.153), channel_id=1, source_target_pairs={{0,4},{4,0},{8,12},{12,8},{1,5},{5,1},{9,13},{13,9},{2,6},{6,2},{1... | collective-permute-start | bytes 196616 | tf_op jit(solution)/shard_map/ppermute | solution.py:449
  (6 other events, 38.9 us)

commit v2 on v1

--- a/solution.py
+++ b/solution.py
@@ -250,52 +250,69 @@
 TAIL = 8
 
 
-def hidden_body(res_ref, ids_ref, gw_ref, gain_ref, keep_ref, got_ref, h32_ref, load_ref, tail_ref):
+def route_body(ids_ref, gw_ref, out_ref, tail_ref):
+    rows = ids_ref.shape[1]
+    gw = gw_ref[...]
+    gates = gw / jnp.sum(gw, axis=0, keepdims=True)
+    high = gates.astype(BF16).astype(F32)
+    tail_ref[...] = jnp.zeros(tail_ref.shape, F32)
+    tail_ref[:, 0:rows] = ids_ref[...].astype(F32)
+    tail_ref[:, LANES : LANES + rows] = high
+    tail_ref[:, 2 * LANES : 2 * LANES + rows] = gates - high
+    out_ref[...] = tail_ref[...].astype(BF16)
+
+
+def stack_body(first_ref, second_ref, out_ref):
+    out_ref[0:TAIL, :] = first_ref[...]
+    out_ref[TAIL:, :] = second_ref[...]
+
+
+def hidden_body(res_ref, gain_ref, keep_ref, got_ref, h32_ref, h16_ref, load_ref, tail_ref):
     t = lax.axis_index("tp")
     rows, cols = keep_ref.shape
     here = pl.ds(pl.multiple_of(t * cols, cols), cols)
     hidden = res_ref[:, here].astype(F32) + (keep_ref[...] + got_ref[...])
     h32_ref[...] = hidden
+    h16_ref[...] = hidden.astype(BF16)
     load_ref[0:rows, :] = hidden.astype(BF16)
-    gw = gw_ref[...]
-    gates = gw / jnp.sum(gw, axis=0, keepdims=True)
-    high = gates.astype(BF16).astype(F32)
     gain = gain_ref[:, here]
     gain_high = gain.astype(BF16).astype(F32)
     tail_ref[...] = jnp.zeros(tail_ref.shape, F32)
-    tail_ref[:, 0:rows] = ids_ref[...].astype(F32)
-    tail_ref[:, LANES : LANES + rows] = high
-    tail_ref[:, 2 * LANES : 2 * LANES + rows] = gates - high
     for i in range(cols // LANES):
         part = slice(LANES * i, LANES * (i + 1))
-        tail_ref[i : i + 1, 3 * LANES :] = gain_high[:, part]
-        tail_ref[TAIL // 2 + i : TAIL // 2 + i + 1, 3 * LANES :] = (gain - gain_high)[:, part]
+        tail_ref[i : i + 1, 0:LANES] = gain_high[:, part]
+        tail_ref[TAIL // 2 + i : TAIL // 2 + i + 1, 0:LANES] = (gain - gain_high)[:, part]
     load_ref[rows:, :] = tail_ref[...].astype(BF16)
 
 
 def merge_body(*refs):
     all_ref = refs[-1]
-    rows = refs[0].shape[0] - TAIL
+    rows = refs[0].shape[0]
     for j, ref in enumerate(refs[:-1]):
-        all_ref[rows * j : rows * (j + 1), :] = ref[0:rows, :]
-
-
-def join_body(*refs):
+        all_ref[rows * j : rows * (j + 1), :] = ref[...]
+
+
+def join_body(load_ref, *refs):
     out_ref = refs[-1]
-    rows = refs[0].shape[0] - TAIL
+    rows = load_ref.shape[0] - TAIL
+    out_ref[0:rows, :] = load_ref[0:rows, :]
     for j, ref in enumerate(refs[:-1]):
-        out_ref[rows * j : rows * (j + 1), :] = ref[0:rows, :]
-    out_ref[out_ref.shape[0] - TAIL :, :] = refs[0][rows:, :]
-
-
-def pick_body(blocks, *refs):
-    loads, pick_ref, gate_ref = refs[:blocks], refs[blocks], refs[blocks + 1]
-    token_rows = loads[0].shape[0] - TAIL
+        out_ref[rows * (j + 1) : rows * (j + 2), :] = ref[...]
+    out_ref[out_ref.shape[0] - TAIL :, :] = load_ref[rows:, :]
+
+
+def pick_body(mine_ref, theirs_ref, pick_ref, gate_ref):
     slot_rows, tokens = pick_ref.shape
+    blocks = 2 * mine_ref.shape[0] // TAIL
+    token_rows = tokens // blocks
     experts = EXPERTS // (lax.axis_size("ep") * lax.axis_size("tp"))
     slots = slot_rows // experts
     low = lax.broadcasted_iota(jnp.int32, (TAIL, LANES), 1) < token_rows
-    tails = [ref[token_rows:, :].astype(F32) for ref in loads]
+    tails = [
+        ref[start : start + TAIL, :].astype(F32)
+        for start in range(0, mine_ref.shape[0], TAIL)
+        for ref in (mine_ref, theirs_ref)
+    ]
 
     def side_by_side(values):
         pairs = [
@@ -340,7 +357,7 @@
 
 def tail_gain(ref):
     rows, cols = ref.shape
-    tail = ref[rows - TAIL :, 3 * LANES :].astype(F32)
+    tail = ref[rows - TAIL :, 0:LANES].astype(F32)
     gain = tail + pltpu.roll(tail, TAIL // 2, 0)
     return jnp.concatenate([gain[i : i + 1, :] for i in range(cols // LANES)], axis=1)
 
@@ -508,26 +525,35 @@
         args=loaded,
     )
     other_attended = swap(attended, "half")
+    (route,) = kernel_call(
+        route_body,
+        [((TAIL, 4 * LANES), BF16)],
+        scratch=[pltpu.VMEM((TAIL, 4 * LANES), F32)],
+        args=(expert_ids.T, gate_weights.T),
+    )
+    (routes,) = kernel_call(
+        stack_body, [((2 * TAIL, 4 * LANES), BF16)], args=(route, swap(route, "ep", 2))
+    )
     keep, send = kernel_call(
         project_body,
         [((token_rows, cols), F32)] * 2,
         scratch=[pltpu.VMEM((token_rows, sharing * head_size), BF16)],
         args=(attended, other_attended, out_weight),
     )
-    h32, payload = kernel_call(
+    h32, h16, payload = kernel_call(
         hidden_body,
-        [((token_rows, cols), F32), ((token_rows + TAIL, cols), BF16)],
+        [((token_rows, cols), F32), ((token_rows, cols), BF16), ((token_rows + TAIL, cols), BF16)],
         scratch=[pltpu.VMEM((TAIL, cols), F32)],
-        args=(residual, expert_ids.T, gate_weights.T, gain, keep, swap(send, "tp")),
-    )
-    arrived = [payload] + [swap(payload, "ep", j) for j in range(1, blocks)]
-    from_x = [swap(v, "half") for v in arrived]
+        args=(residual, gain, keep, swap(send, "tp")),
+    )
+    arrived = [h16] + [swap(h16, "ep", j) for j in range(1, blocks)]
+    from_x = [swap(payload if j == 0 else v, "half") for j, v in enumerate(arrived)]
     (mine,) = kernel_call(merge_body, [((tokens, cols), BF16)], args=arrived)
     theirs = swap(mine, "tp")
     pick, gate = kernel_call(
-        functools.partial(pick_body, blocks),
+        pick_body,
         [((slot_rows, tokens), BF16), ((slot_rows, 1), F32)],
-        args=arrived,
+        args=(routes, swap(routes, "ep", 1)),
     )
     early = experts * 3 // 4
     squares, rows, gate_a, up_a = kernel_call(

time: 55.2 us -> 59 us (1.069)
  starting transfers between devices: 21.2 us -> 23.7 us
  waiting for transfers between devices: 17.6 us -> 18.9 us
    ppermute x20 -> x22, starting transfers between devices: 21.2 us -> 23.7 us  [swap(): lax.ppermute(value, axis, [(i, i ^ partner) for i in range(lax.axis_size(...]
    ppermute x20 -> x22, waiting for transfers between devices: 17.6 us -> 18.9 us  [swap(): lax.ppermute(value, axis, [(i, i ^ partner) for i in range(lax.axis_size(...]
    pallas_call x19 -> x21, Pallas kernels: 15.9 us -> 15.9 us  [pallas_kernel(): pl.pallas_call(body, out_shape=tuple((jax.ShapeDtypeStruct(s, d) for s, d...]
  transfers between devices with their start and end apart: 20 -> 22, of which waited for: 11 -> 12; matrix products, arithmetic and copies ran while one was open for 0% -> 0% of each run, Pallas kernels for 11% -> 10%
where the time goes in v2:
time: 59 us; the launch traced here: 58.8 us
  starting transfers between devices  23.7 us (40%)
  waiting for transfers between devices  18.9 us (32%)
  Pallas kernels  15.9 us (27%)
    ppermute x22, starting transfers between devices, swap(): lax.ppermute(value, axis, [(i, i ^ partner) for i in range(lax.axis_size(...  23.7 us
    ppermute x22, waiting for transfers between devices, swap(): lax.ppermute(value, axis, [(i, i ^ partner) for i in range(lax.axis_size(...  18.9 us
    pallas_call x21, Pallas kernels, pallas_kernel(): pl.pallas_call(body, out_shape=tuple((jax.ShapeDtypeStruct(s, d) for s, d...  15.9 us
  transfers between devices with their start and end apart: 22, of which 12 were waited for; matrix products, arithmetic and copies ran while one was open for 0% of the time, Pallas kernels for 10%

profile of v2, /device:TPU:0, one launch (start us, length us, event | category | flops | bytes accessed | tf_op | source)
XLA Modules:
  0.0 58.8 jit_solution(15512148166918612954)
XLA Ops:
  0.0 1.3 %shard_map.136 = (bf16[32,1024]{1,0:T(8,128)(2,1)S(1)}, bf16[32,128]{1,0:T(8,128)(2,1)S(1)}, bf16[32,128]{1,0:T(8,128)(2,1)S(1)}, bf16[2048,128]{1,0:T(8,128)(2,...) custom-call(bf16[32,1024]{1,0:T(8,128)(2,1)} %refs_0_.1, bf16[32,128]{1,0:T(8,128)(2,1)} %refs_1_.1, ...), custom_call_target="tpu_custom_call" | custom-call | flops 1000 | bytes 1000 | tf_op jit(solution)/shard_map/pallas_call | solution.py:163
  1.4 1.5 %shard_map.137.own_ref = bf16[32,1024]{1,0:T(8,128)(2,1)S(1)} custom-call(bf16[32,1024]{1,0:T(8,128)(2,1)S(1)} %get-tuple-element.38.q_ref, bf16[32,128]{1,0:T(8,128)(2,1)S(1)} %get-tuple-element.39.nk_ref, bf16[32,128]{1,0:T(8,128)(2,1)S(1)} %get-tuple-element.40.nv_ref, bf16[2048,128]{1,0:T(8,128)(2,1)S(1)} %get-tuple-element.41.k_ref, ...), custom_call_target="tpu_custom_call" | custom-call | flops 99999997952 | bytes 1000 | tf_op jit(solution)/shard_map/pallas_call | solution.py:163
  2.9 3.0 %collective-permute-start = (bf16[32,1024]{1,0:T(8,128)(2,1)S(1)}, bf16[32,1024]{1,0:T(8,128)(2,1)S(1)}, u32[]{:S(2)}, u32[]{:S(2)}) collective-permute-start(bf16[32,1024]{1,0:T(8,128)(2,1)S(1)} %shard_map.137.own_ref), channel_id=1, source_target_pairs={{0,2},{2,0},{1,3},{3,1},{4,6},{6,4},{5,7},{7,5},{8,10},{10,8},{9,1... | collective-permute-start | bytes 196616 | tf_op jit(solution)/shard_map/ppermute | solution.py:466
  5.9 2.2 %collective-permute-done.other_ref = bf16[32,1024]{1,0:T(8,128)(2,1)S(1)} collective-permute-done((bf16[32,1024]{1,0:T(8,128)(2,1)S(1)}, bf16[32,1024]{1,0:T(8,128)(2,1)S(1)}, u32[]{:S(2)}, u32[]{:S(2)}) %collective-permute-start) | collective-permute-done | bytes 65568 | tf_op jit(solution)/shard_map/ppermute | solution.py:466
  8.8 1.3 %collective-permute-done.1.got_ref = f32[64,512]{1,0:T(8,128)S(1)} collective-permute-done((f32[64,512]{1,0:T(8,128)S(1)}, f32[64,512]{1,0:T(8,128)S(1)}, u32[]{:S(2)}, u32[]{:S(2)}) %collective-permute-start.1) | collective-permute-done | bytes 131104 | tf_op jit(solution)/shard_map/ppermute | solution.py:466
  10.1 4.2 %collective-permute-start.7 = (bf16[64,512]{1,0:T(8,128)(2,1)S(1)}, bf16[64,512]{1,0:T(8,128)(2,1)S(1)}, u32[]{:S(2)}, u32[]{:S(2)}) collective-permute-start(bf16[64,512]{1,0:T(8,128)(2,1)S(1)} %get-tuple-element.48.refs_0_), channel_id=1, source_target_pairs={{0,12},{4,8},{8,4},{12,0},{1,13},{5,9},{9,5},{13,1},{2,14},{6,10},... | collective-permute-start | bytes 196616 | tf_op jit(solution)/shard_map/ppermute | solution.py:466
  15.0 2.0 %collective-permute-done.7.refs_3_ = bf16[64,512]{1,0:T(8,128)(2,1)S(1)} collective-permute-done((bf16[64,512]{1,0:T(8,128)(2,1)S(1)}, bf16[64,512]{1,0:T(8,128)(2,1)S(1)}, u32[]{:S(2)}, u32[]{:S(2)}) %collective-permute-start.7) | collective-permute-done | bytes 65568 | tf_op jit(solution)/shard_map/ppermute | solution.py:466
  17.0 3.3 %collective-permute-done.5.refs_2_ = bf16[64,512]{1,0:T(8,128)(2,1)S(1)} collective-permute-done((bf16[64,512]{1,0:T(8,128)(2,1)S(1)}, bf16[64,512]{1,0:T(8,128)(2,1)S(1)}, u32[]{:S(2)}, u32[]{:S(2)}) %collective-permute-start.5) | collective-permute-done | bytes 65568 | tf_op jit(solution)/shard_map/ppermute | solution.py:466
  20.4 1.4 %collective-permute-start.10 = (bf16[8,512]{1,0:T(8,128)(2,1)S(1)}, bf16[8,512]{1,0:T(8,128)(2,1)S(1)}, u32[]{:S(2)}, u32[]{:S(2)}) collective-permute-start(bf16[8,512]{1,0:T(8,128)(2,1)S(1)} %shard_map.141.first_ref), channel_id=1, source_target_pairs={{0,8},{4,12},{8,0},{12,4},{1,9},{5,13},{9,1},{13,5},{2,10},{6,14},... | collective-permute-start | bytes 24584 | tf_op jit(solution)/shard_map/ppermute | solution.py:466
  21.7 3.3 %collective-permute-done.10.second_ref = bf16[8,512]{1,0:T(8,128)(2,1)S(1)} collective-permute-done((bf16[8,512]{1,0:T(8,128)(2,1)S(1)}, bf16[8,512]{1,0:T(8,128)(2,1)S(1)}, u32[]{:S(2)}, u32[]{:S(2)}) %collective-permute-start.10) | collective-permute-done | bytes 8224 | tf_op jit(solution)/shard_map/ppermute | solution.py:466
  25.0 1.1 %collective-permute-start.11 = (bf16[16,512]{1,0:T(8,128)(2,1)S(1)}, bf16[16,512]{1,0:T(8,128)(2,1)S(1)}, u32[]{:S(2)}, u32[]{:S(2)}) collective-permute-start(bf16[16,512]{1,0:T(8,128)(2,1)S(1)} %shard_map.142.mine_ref), channel_id=1, source_target_pairs={{0,4},{4,0},{8,12},{12,8},{1,5},{5,1},{9,13},{13,9},{2,6},{6,2},{1... | collective-permute-start | bytes 49160 | tf_op jit(solution)/shard_map/ppermute | solution.py:466
  26.1 1.5 %collective-permute-start.2 = (bf16[72,512]{1,0:T(8,128)(2,1)S(1)}, bf16[72,512]{1,0:T(8,128)(2,1)S(1)}, u32[]{:S(2)}, u32[]{:S(2)}) collective-permute-start(bf16[72,512]{1,0:T(8,128)(2,1)S(1)} %get-tuple-element.47), channel_id=1, source_target_pairs={{0,2},{2,0},{1,3},{3,1},{4,6},{6,4},{5,7},{7,5},{8,10},{10,8},{9,1... | collective-permute-start | bytes 221192 | tf_op jit(solution)/shard_map/ppermute | solution.py:466
  28.1 1.5 %collective-permute-start.6 = (bf16[64,512]{1,0:T(8,128)(2,1)S(1)}, bf16[64,512]{1,0:T(8,128)(2,1)S(1)}, u32[]{:S(2)}, u32[]{:S(2)}) collective-permute-start(bf16[64,512]{1,0:T(8,128)(2,1)S(1)} %collective-permute-done.5.refs_2_), channel_id=1, source_target_pairs={{0,2},{2,0},{1,3},{3,1},{4,6},{6,4},{5,7},{7,5},{8,10},{10,8},{9,1... | collective-permute-start | bytes 196616 | tf_op jit(solution)/shard_map/ppermute | solution.py:466
  30.6 3.0 %shard_map.144 = (f32[384,1]{1,0:T(8,128)S(1)}, bf16[384,1024]{1,0:T(8,128)(2,1)S(1)}, f32[288,384]{1,0:T(8,128)S(1)}, f32[288,384]{1,0:T(8,128)S(1)}) custom-call(bf16[256,512]{1,0:T(8,128)(2,1)S(1)} %shard_map.140.mine_ref, bf16[256,512]{1,0:T(8,128)(2,1)S(1)} %collective-permute-done.9.theirs_ref, f32[1,1024]{1,0:T(1,128)S(1)} %bitcast.9, ...), custom_call_target="tpu_custom_call" | custom-call | flops 1000 | bytes 1000 | tf_op jit(solution)/shard_map/pallas_call | solution.py:163
  34.1 1.0 %shard_map.146 = (f32[96,384]{1,0:T(8,128)S(1)}, f32[96,384]{1,0:T(8,128)S(1)}) custom-call(bf16[384,1024]{1,0:T(8,128)(2,1)S(1)} %get-tuple-element.58.rows_ref, bf16[8,384,2048]{2,1,0:T(8,128)(2,1)S(1)} %copy-done, bf16[8,384,2048]{2,1,0:T(8,128)(2,1)S(1)} %copy-done.1), custom_call_target="tpu_custom_call" | custom-call | flops 1000 | bytes 1000 | tf_op jit(solution)/shard_map/pallas_call | solution.py:163
  35.6 3.8 %shard_map.147.act_ref = bf16[384,384]{1,0:T(8,128)(2,1)S(1)} custom-call(bf16[264,512]{1,0:T(8,128)(2,1)S(1)} %shard_map.145.mine_ref, bf16[264,512]{1,0:T(8,128)(2,1)S(1)} %collective-permute-done.12.theirs_ref, bf16[8,384,2048]{2,1,0:T(8,128)(2,1)S(1)} %copy-done, bf16[8,384,2048]{2,1,0:T(8,128)(2,1)S(1)} %copy-done.1, ...), custom_call_target="tpu_custom_call" | custom-call | flops 1000 | bytes 1000 | tf_op jit(solution)/shard_map/pallas_call | solution.py:163
  43.2 1.1 %collective-permute-start.15 = (bf16[64,512]{1,0:T(8,128)(2,1)S(1)}, bf16[64,512]{1,0:T(8,128)(2,1)S(1)}, u32[]{:S(2)}, u32[]{:S(2)}) collective-permute-start(bf16[64,512]{1,0:T(8,128)(2,1)S(1)} %get-tuple-element.67), channel_id=1, source_target_pairs={{0,2},{2,0},{1,3},{3,1},{4,6},{6,4},{5,7},{7,5},{8,10},{10,8},{9,1... | collective-permute-start | bytes 196616 | tf_op jit(solution)/shard_map/ppermute | solution.py:466
  45.2 1.1 %collective-permute-start.18 = (bf16[64,512]{1,0:T(8,128)(2,1)S(1)}, bf16[64,512]{1,0:T(8,128)(2,1)S(1)}, u32[]{:S(2)}, u32[]{:S(2)}) collective-permute-start(bf16[64,512]{1,0:T(8,128)(2,1)S(1)} %get-tuple-element.69), channel_id=1, source_target_pairs={{0,2},{2,0},{1,3},{3,1},{4,6},{6,4},{5,7},{7,5},{8,10},{10,8},{9,1... | collective-permute-start | bytes 196616 | tf_op jit(solution)/shard_map/ppermute | solution.py:466
  48.1 1.4 %collective-permute-done.16.other_ref = bf16[64,512]{1,0:T(8,128)(2,1)S(1)} collective-permute-done((bf16[64,512]{1,0:T(8,128)(2,1)S(1)}, bf16[64,512]{1,0:T(8,128)(2,1)S(1)}, u32[]{:S(2)}, u32[]{:S(2)}) %collective-permute-start.16) | collective-permute-done | bytes 65568 | tf_op jit(solution)/shard_map/ppermute | solution.py:466
  49.6 2.1 %collective-permute-start.17 = (bf16[64,512]{1,0:T(8,128)(2,1)S(1)}, bf16[64,512]{1,0:T(8,128)(2,1)S(1)}, u32[]{:S(2)}, u32[]{:S(2)}) collective-permute-start(bf16[64,512]{1,0:T(8,128)(2,1)S(1)} %shard_map.153), channel_id=1, source_target_pairs={{0,12},{4,8},{8,4},{12,0},{1,13},{5,9},{9,5},{13,1},{2,14},{6,10},... | collective-permute-start | bytes 196616 | tf_op jit(solution)/shard_map/ppermute | solution.py:466
  51.8 1.2 %collective-permute-start.19 = (bf16[64,512]{1,0:T(8,128)(2,1)S(1)}, bf16[64,512]{1,0:T(8,128)(2,1)S(1)}, u32[]{:S(2)}, u32[]{:S(2)}) collective-permute-start(bf16[64,512]{1,0:T(8,128)(2,1)S(1)} %shard_map.154), channel_id=1, source_target_pairs={{0,8},{4,12},{8,0},{12,4},{1,9},{5,13},{9,1},{13,5},{2,10},{6,14},... | collective-permute-start | bytes 196616 | tf_op jit(solution)/shard_map/ppermute | solution.py:466
  53.0 1.3 %collective-permute-start.21 = (bf16[64,512]{1,0:T(8,128)(2,1)S(1)}, bf16[64,512]{1,0:T(8,128)(2,1)S(1)}, u32[]{:S(2)}, u32[]{:S(2)}) collective-permute-start(bf16[64,512]{1,0:T(8,128)(2,1)S(1)} %shard_map.155), channel_id=1, source_target_pairs={{0,4},{4,0},{8,12},{12,8},{1,5},{5,1},{9,13},{13,9},{2,6},{6,2},{1... | collective-permute-start | bytes 196616 | tf_op jit(solution)/shard_map/ppermute | solution.py:466
  54.2 1.9 %collective-permute-done.17.refs_1_ = bf16[64,512]{1,0:T(8,128)(2,1)S(1)} collective-permute-done((bf16[64,512]{1,0:T(8,128)(2,1)S(1)}, bf16[64,512]{1,0:T(8,128)(2,1)S(1)}, u32[]{:S(2)}, u32[]{:S(2)}) %collective-permute-start.17) | collective-permute-done | bytes 65568 | tf_op jit(solution)/shard_map/ppermute | solution.py:466
  56.1 1.8 %collective-permute-done.19.refs_2_ = bf16[64,512]{1,0:T(8,128)(2,1)S(1)} collective-permute-done((bf16[64,512]{1,0:T(8,128)(2,1)S(1)}, bf16[64,512]{1,0:T(8,128)(2,1)S(1)}, u32[]{:S(2)}, u32[]{:S(2)}) %collective-permute-start.19) | collective-permute-done | bytes 65568 | tf_op jit(solution)/shard_map/ppermute | solution.py:466
  (62 shorter events, 11.3 us)
Async XLA Ops:
  1.4 29.2 %copy-start = (bf16[8,384,2048]{2,1,0:T(8,128)(2,1)S(1)}, bf16[8,384,2048]{2,1,0:T(8,128)(2,1)}, u32[]{:S(2)}) copy-start(bf16[8,384,2048]{2,1,0:T(8,128)(2,1)} %wg_ref.5) | copy-start | bytes 37748740
  1.4 29.2 %copy-start.1 = (bf16[8,384,2048]{2,1,0:T(8,128)(2,1)S(1)}, bf16[8,384,2048]{2,1,0:T(8,128)(2,1)}, u32[]{:S(2)}) copy-start(bf16[8,384,2048]{2,1,0:T(8,128)(2,1)} %wu_ref.5) | copy-start | bytes 37748740
  2.9 5.3 %collective-permute-start = (bf16[32,1024]{1,0:T(8,128)(2,1)S(1)}, bf16[32,1024]{1,0:T(8,128)(2,1)S(1)}, u32[]{:S(2)}, u32[]{:S(2)}) collective-permute-start(bf16[32,1024]{1,0:T(8,128)(2,1)S(1)} %shard_map.137.own_ref), channel_id=1, source_target_pairs={{0,2},{2,0},{1,3},{3,1},{4,6},{6,4},{5,7},{7,5},{8,10},{10,8},{9,1... | collective-permute-start | bytes 196616 | tf_op jit(solution)/shard_map/ppermute | solution.py:466
  8.7 1.4 %collective-permute-start.1 = (f32[64,512]{1,0:T(8,128)S(1)}, f32[64,512]{1,0:T(8,128)S(1)}, u32[]{:S(2)}, u32[]{:S(2)}) collective-permute-start(f32[64,512]{1,0:T(8,128)S(1)} %get-tuple-element.45), channel_id=1, source_target_pairs={{0,1},{1,0},{2,3},{3,2},{4,5},{5,4},{6,7},{7,6},{8,9},{9,8},{10,11... | collective-permute-start | bytes 393224 | tf_op jit(solution)/shard_map/ppermute | solution.py:466
  10.1 6.8 %collective-permute-start.7 = (bf16[64,512]{1,0:T(8,128)(2,1)S(1)}, bf16[64,512]{1,0:T(8,128)(2,1)S(1)}, u32[]{:S(2)}, u32[]{:S(2)}) collective-permute-start(bf16[64,512]{1,0:T(8,128)(2,1)S(1)} %get-tuple-element.48.refs_0_), channel_id=1, source_target_pairs={{0,12},{4,8},{8,4},{12,0},{1,13},{5,9},{9,5},{13,1},{2,14},{6,10},... | collective-permute-start | bytes 196616 | tf_op jit(solution)/shard_map/ppermute | solution.py:466
  14.3 5.9 %collective-permute-start.5 = (bf16[64,512]{1,0:T(8,128)(2,1)S(1)}, bf16[64,512]{1,0:T(8,128)(2,1)S(1)}, u32[]{:S(2)}, u32[]{:S(2)}) collective-permute-start(bf16[64,512]{1,0:T(8,128)(2,1)S(1)} %get-tuple-element.48.refs_0_), channel_id=1, source_target_pairs={{0,8},{4,12},{8,0},{12,4},{1,9},{5,13},{9,1},{13,5},{2,10},{6,14},... | collective-permute-start | bytes 196616 | tf_op jit(solution)/shard_map/ppermute | solution.py:466
  14.3 5.9 %collective-permute-start.3 = (bf16[64,512]{1,0:T(8,128)(2,1)S(1)}, bf16[64,512]{1,0:T(8,128)(2,1)S(1)}, u32[]{:S(2)}, u32[]{:S(2)}) collective-permute-start(bf16[64,512]{1,0:T(8,128)(2,1)S(1)} %get-tuple-element.48.refs_0_), channel_id=1, source_target_pairs={{0,4},{4,0},{8,12},{12,8},{1,5},{5,1},{9,13},{13,9},{2,6},{6,2},{1... | collective-permute-start | bytes 196616 | tf_op jit(solution)/shard_map/ppermute | solution.py:466
  20.3 10.3 %collective-permute-start.9 = (bf16[256,512]{1,0:T(8,128)(2,1)S(1)}, bf16[256,512]{1,0:T(8,128)(2,1)S(1)}, u32[]{:S(2)}, u32[]{:S(2)}) collective-permute-start(bf16[256,512]{1,0:T(8,128)(2,1)S(1)} %shard_map.140.mine_ref), channel_id=1, source_target_pairs={{0,1},{1,0},{2,3},{3,2},{4,5},{5,4},{6,7},{7,6},{8,9},{9,8},{10,11... | collective-permute-start | bytes 786440 | tf_op jit(solution)/shard_map/ppermute | solution.py:466
  20.4 4.6 %collective-permute-start.10 = (bf16[8,512]{1,0:T(8,128)(2,1)S(1)}, bf16[8,512]{1,0:T(8,128)(2,1)S(1)}, u32[]{:S(2)}, u32[]{:S(2)}) collective-permute-start(bf16[8,512]{1,0:T(8,128)(2,1)S(1)} %shard_map.141.first_ref), channel_id=1, source_target_pairs={{0,8},{4,12},{8,0},{12,4},{1,9},{5,13},{9,1},{13,5},{2,10},{6,14},... | collective-permute-start | bytes 24584 | tf_op jit(solution)/shard_map/ppermute | solution.py:466
  25.0 4.6 %collective-permute-start.11 = (bf16[16,512]{1,0:T(8,128)(2,1)S(1)}, bf16[16,512]{1,0:T(8,128)(2,1)S(1)}, u32[]{:S(2)}, u32[]{:S(2)}) collective-permute-start(bf16[16,512]{1,0:T(8,128)(2,1)S(1)} %shard_map.142.mine_ref), channel_id=1, source_target_pairs={{0,4},{4,0},{8,12},{12,8},{1,5},{5,1},{9,13},{13,9},{2,6},{6,2},{1... | collective-permute-start | bytes 49160 | tf_op jit(solution)/shard_map/ppermute | solution.py:466
  26.1 7.5 %collective-permute-start.2 = (bf16[72,512]{1,0:T(8,128)(2,1)S(1)}, bf16[72,512]{1,0:T(8,128)(2,1)S(1)}, u32[]{:S(2)}, u32[]{:S(2)}) collective-permute-start(bf16[72,512]{1,0:T(8,128)(2,1)S(1)} %get-tuple-element.47), channel_id=1, source_target_pairs={{0,2},{2,0},{1,3},{3,1},{4,6},{6,4},{5,7},{7,5},{8,10},{10,8},{9,1... | collective-permute-start | bytes 221192 | tf_op jit(solution)/shard_map/ppermute | solution.py:466
  27.6 6.0 %collective-permute-start.8 = (bf16[64,512]{1,0:T(8,128)(2,1)S(1)}, bf16[64,512]{1,0:T(8,128)(2,1)S(1)}, u32[]{:S(2)}, u32[]{:S(2)}) collective-permute-start(bf16[64,512]{1,0:T(8,128)(2,1)S(1)} %collective-permute-done.7.refs_3_), channel_id=1, source_target_pairs={{0,2},{2,0},{1,3},{3,1},{4,6},{6,4},{5,7},{7,5},{8,10},{10,8},{9,1... | collective-permute-start | bytes 196616 | tf_op jit(solution)/shard_map/ppermute | solution.py:466
  28.1 5.5 %collective-permute-start.6 = (bf16[64,512]{1,0:T(8,128)(2,1)S(1)}, bf16[64,512]{1,0:T(8,128)(2,1)S(1)}, u32[]{:S(2)}, u32[]{:S(2)}) collective-permute-start(bf16[64,512]{1,0:T(8,128)(2,1)S(1)} %collective-permute-done.5.refs_2_), channel_id=1, source_target_pairs={{0,2},{2,0},{1,3},{3,1},{4,6},{6,4},{5,7},{7,5},{8,10},{10,8},{9,1... | collective-permute-start | bytes 196616 | tf_op jit(solution)/shard_map/ppermute | solution.py:466
  29.6 4.4 %collective-permute-start.4 = (bf16[64,512]{1,0:T(8,128)(2,1)S(1)}, bf16[64,512]{1,0:T(8,128)(2,1)S(1)}, u32[]{:S(2)}, u32[]{:S(2)}) collective-permute-start(bf16[64,512]{1,0:T(8,128)(2,1)S(1)} %collective-permute-done.3.refs_1_), channel_id=1, source_target_pairs={{0,2},{2,0},{1,3},{3,1},{4,6},{6,4},{5,7},{7,5},{8,10},{10,8},{9,1... | collective-permute-start | bytes 196616 | tf_op jit(solution)/shard_map/ppermute | solution.py:466
  34.0 1.6 %collective-permute-start.12 = (bf16[264,512]{1,0:T(8,128)(2,1)S(1)}, bf16[264,512]{1,0:T(8,128)(2,1)S(1)}, u32[]{:S(2)}, u32[]{:S(2)}) collective-permute-start(bf16[264,512]{1,0:T(8,128)(2,1)S(1)} %shard_map.145.mine_ref), channel_id=1, source_target_pairs={{0,1},{1,0},{2,3},{3,2},{4,5},{5,4},{6,7},{7,6},{8,9},{9,8},{10,11... | collective-permute-start | bytes 811016 | tf_op jit(solution)/shard_map/ppermute | solution.py:466
  40.4 1.6 %collective-permute-start.13 = (bf16[256,512]{1,0:T(8,128)(2,1)S(1)}, bf16[256,512]{1,0:T(8,128)(2,1)S(1)}, u32[]{:S(2)}, u32[]{:S(2)}) collective-permute-start(bf16[256,512]{1,0:T(8,128)(2,1)S(1)} %shard_map.149), channel_id=1, source_target_pairs={{0,1},{1,0},{2,3},{3,2},{4,5},{5,4},{6,7},{7,6},{8,9},{9,8},{10,11... | collective-permute-start | bytes 786440 | tf_op jit(solution)/shard_map/ppermute | solution.py:466
  43.0 6.6 %collective-permute-start.14 = (bf16[256,512]{1,0:T(8,128)(2,1)S(1)}, bf16[256,512]{1,0:T(8,128)(2,1)S(1)}, u32[]{:S(2)}, u32[]{:S(2)}) collective-permute-start(bf16[256,512]{1,0:T(8,128)(2,1)S(1)} %shard_map.152), channel_id=1, source_target_pairs={{0,1},{1,0},{2,3},{3,2},{4,5},{5,4},{6,7},{7,6},{8,9},{9,8},{10,11... | collective-permute-start | bytes 786440 | tf_op jit(solution)/shard_map/ppermute | solution.py:466
  43.2 11.0 %collective-permute-start.15 = (bf16[64,512]{1,0:T(8,128)(2,1)S(1)}, bf16[64,512]{1,0:T(8,128)(2,1)S(1)}, u32[]{:S(2)}, u32[]{:S(2)}) collective-permute-start(bf16[64,512]{1,0:T(8,128)(2,1)S(1)} %get-tuple-element.67), channel_id=1, source_target_pairs={{0,2},{2,0},{1,3},{3,1},{4,6},{6,4},{5,7},{7,5},{8,10},{10,8},{9,1... | collective-permute-start | bytes 196616 | tf_op jit(solution)/shard_map/ppermute | solution.py:466
  44.2 5.3 %collective-permute-start.16 = (bf16[64,512]{1,0:T(8,128)(2,1)S(1)}, bf16[64,512]{1,0:T(8,128)(2,1)S(1)}, u32[]{:S(2)}, u32[]{:S(2)}) collective-permute-start(bf16[64,512]{1,0:T(8,128)(2,1)S(1)} %get-tuple-element.68), channel_id=1, source_target_pairs={{0,2},{2,0},{1,3},{3,1},{4,6},{6,4},{5,7},{7,5},{8,10},{10,8},{9,1... | collective-permute-start | bytes 196616 | tf_op jit(solution)/shard_map/ppermute | solution.py:466
  45.2 6.5 %collective-permute-start.18 = (bf16[64,512]{1,0:T(8,128)(2,1)S(1)}, bf16[64,512]{1,0:T(8,128)(2,1)S(1)}, u32[]{:S(2)}, u32[]{:S(2)}) collective-permute-start(bf16[64,512]{1,0:T(8,128)(2,1)S(1)} %get-tuple-element.69), channel_id=1, source_target_pairs={{0,2},{2,0},{1,3},{3,1},{4,6},{6,4},{5,7},{7,5},{8,10},{10,8},{9,1... | collective-permute-start | bytes 196616 | tf_op jit(solution)/shard_map/ppermute | solution.py:466
  46.3 6.7 %collective-permute-start.20 = (bf16[64,512]{1,0:T(8,128)(2,1)S(1)}, bf16[64,512]{1,0:T(8,128)(2,1)S(1)}, u32[]{:S(2)}, u32[]{:S(2)}) collective-permute-start(bf16[64,512]{1,0:T(8,128)(2,1)S(1)} %get-tuple-element.70), channel_id=1, source_target_pairs={{0,2},{2,0},{1,3},{3,1},{4,6},{6,4},{5,7},{7,5},{8,10},{10,8},{9,1... | collective-permute-start | bytes 196616 | tf_op jit(solution)/shard_map/ppermute | solution.py:466
  49.6 6.5 %collective-permute-start.17 = (bf16[64,512]{1,0:T(8,128)(2,1)S(1)}, bf16[64,512]{1,0:T(8,128)(2,1)S(1)}, u32[]{:S(2)}, u32[]{:S(2)}) collective-permute-start(bf16[64,512]{1,0:T(8,128)(2,1)S(1)} %shard_map.153), channel_id=1, source_target_pairs={{0,12},{4,8},{8,4},{12,0},{1,13},{5,9},{9,5},{13,1},{2,14},{6,10},... | collective-permute-start | bytes 196616 | tf_op jit(solution)/shard_map/ppermute | solution.py:466
  51.8 6.2 %collective-permute-start.19 = (bf16[64,512]{1,0:T(8,128)(2,1)S(1)}, bf16[64,512]{1,0:T(8,128)(2,1)S(1)}, u32[]{:S(2)}, u32[]{:S(2)}) collective-permute-start(bf16[64,512]{1,0:T(8,128)(2,1)S(1)} %shard_map.154), channel_id=1, source_target_pairs={{0,8},{4,12},{8,0},{12,4},{1,9},{5,13},{9,1},{13,5},{2,10},{6,14},... | collective-permute-start | bytes 196616 | tf_op jit(solution)/shard_map/ppermute | solution.py:466
  53.0 5.2 %collective-permute-start.21 = (bf16[64,512]{1,0:T(8,128)(2,1)S(1)}, bf16[64,512]{1,0:T(8,128)(2,1)S(1)}, u32[]{:S(2)}, u32[]{:S(2)}) collective-permute-start(bf16[64,512]{1,0:T(8,128)(2,1)S(1)} %shard_map.155), channel_id=1, source_target_pairs={{0,4},{4,0},{8,12},{12,8},{1,5},{5,1},{9,13},{13,9},{2,6},{6,2},{1... | collective-permute-start | bytes 196616 | tf_op jit(solution)/shard_map/ppermute | solution.py:466
  (8 other events, 76.9 us)

commit v3 on v2

--- a/solution.py
+++ b/solution.py
@@ -447,10 +447,13 @@
         start += out.shape[0]
 
 
-def block_sum_body(start, keep_ref, got_ref, other_ref, out_ref):
-    here = slice(start, start + out_ref.shape[0])
-    total = keep_ref[here, :] + got_ref[here, :].astype(F32) + other_ref[...].astype(F32)
-    out_ref[...] = total.astype(BF16)
+def block_sum_body(start, keep_ref, got_ref, other_ref, *outs):
+    rows = outs[0].shape[0]
+    for j, out in enumerate(outs):
+        here = slice(start + rows * j, start + rows * (j + 1))
+        total = keep_ref[here, :] + got_ref[here, :].astype(F32)
+        total = total + other_ref[rows * j : rows * (j + 1), :].astype(F32)
+        out[...] = total.astype(BF16)
 
 
 def final_body(h32_ref, keep_ref, got_ref, *refs):
@@ -594,24 +597,36 @@
 
     got_a = swap(down(act, True, True), "tp")
     keep_a = down(act, True, False)
-    sums = kernel_call(pair_sum_body, [((token_rows, cols), BF16)] * blocks, args=(keep_a, got_a))
+    sums = kernel_call(
+        pair_sum_body,
+        [((n * token_rows, cols), BF16) for n in (1, blocks - 2, 1)],
+        args=(keep_a, got_a),
+    )
     act, sums = lax.optimization_barrier((act, sums))
     from_x = [swap(v, "half") for v in sums]
     got_b = swap(down(act, False, True), "tp")
     keep_b = down(act, False, False)
 
-    home = []
-    for j in range(blocks - 1, 0, -1):
-        (total,) = kernel_call(
-            functools.partial(block_sum_body, j * token_rows),
-            [((token_rows, cols), BF16)],
-            args=(keep_b, got_b, from_x[j]),
+    totals = []
+    for start, count, other in ((blocks - 1, 1, from_x[2]), (1, blocks - 2, from_x[1])):
+        totals += kernel_call(
+            functools.partial(block_sum_body, start * token_rows),
+            [((token_rows, cols), BF16)] * count,
+            args=(keep_b, got_b, other),
         )
-        home.append(swap(total, "ep", j))
+    partners = (blocks - 1, *range(1, blocks - 1))
+    home = [swap(v, "ep", j) for j, v in zip(partners, totals)]
     (out,) = kernel_call(
         final_body, [((token_rows, cols), BF16)], args=(h32, keep_b, got_b, from_x[0], *home)
     )
     return out
+
+
+def rows_fit(*args):
+    residual, expert_ids = args[7], args[9]
+    token_rows, top_count = expert_ids.shape
+    cols = residual.shape[1] // lax.axis_size("tp")
+    return 2 * token_rows == LANES and top_count == TAIL and cols == TAIL // 2 * LANES
 
 
 def solution(mesh):
@@ -634,7 +649,7 @@
     few = mesh.shape["half"] == 2 and mesh.shape["tp"] == 2 and mesh.shape["ep"] == 4
 
     def on_device(*args):
-        return by_rows(*args) if few else by_slots(*args)
+        return by_rows(*args) if few and rows_fit(*args) else by_slots(*args)
 
     return jax.shard_map(
         on_device,

time: 59 us -> 59.3 us (level)
  waiting for transfers between devices: 18.9 us -> 20.3 us
  starting transfers between devices: 23.7 us -> 22.6 us
    ppermute x22 -> x21, waiting for transfers between devices: 18.9 us -> 20.3 us  [swap(): lax.ppermute(value, axis, [(i, i ^ partner) for i in range(lax.axis_size(...]
    ppermute x22 -> x21, starting transfers between devices: 23.7 us -> 22.6 us  [swap(): lax.ppermute(value, axis, [(i, i ^ partner) for i in range(lax.axis_size(...]
    pallas_call x21 -> x20, Pallas kernels: 15.9 us -> 15.9 us  [pallas_kernel(): pl.pallas_call(body, out_shape=tuple((jax.ShapeDtypeStruct(s, d) for s, d...]
  transfers between devices with their start and end apart: 22 -> 21, of which waited for: 12 -> 11; matrix products, arithmetic and copies ran while one was open for 0% -> 0% of each run, Pallas kernels for 10% -> 10%
where the time goes in v3:
time: 59.3 us; the launch traced here: 59.2 us
  starting transfers between devices  22.6 us (38%)
  waiting for transfers between devices  20.3 us (34%)
  Pallas kernels  15.9 us (27%)
    ppermute x21, starting transfers between devices, swap(): lax.ppermute(value, axis, [(i, i ^ partner) for i in range(lax.axis_size(...  22.6 us
    ppermute x21, waiting for transfers between devices, swap(): lax.ppermute(value, axis, [(i, i ^ partner) for i in range(lax.axis_size(...  20.3 us
    pallas_call x20, Pallas kernels, pallas_kernel(): pl.pallas_call(body, out_shape=tuple((jax.ShapeDtypeStruct(s, d) for s, d...  15.9 us
  transfers between devices with their start and end apart: 21, of which 11 were waited for; matrix products, arithmetic and copies ran while one was open for 0% of the time, Pallas kernels for 10%

profile of v3, /device:TPU:0, one launch (start us, length us, event | category | flops | bytes accessed | tf_op | source)
XLA Modules:
  0.0 59.2 jit_solution(12807793624591847983)
XLA Ops:
  0.0 1.3 %shard_map.136 = (bf16[32,1024]{1,0:T(8,128)(2,1)S(1)}, bf16[32,128]{1,0:T(8,128)(2,1)S(1)}, bf16[32,128]{1,0:T(8,128)(2,1)S(1)}, bf16[2048,128]{1,0:T(8,128)(2,...) custom-call(bf16[32,1024]{1,0:T(8,128)(2,1)} %refs_0_.1, bf16[32,128]{1,0:T(8,128)(2,1)} %refs_1_.1, ...), custom_call_target="tpu_custom_call" | custom-call | flops 1000 | bytes 1000 | tf_op jit(solution)/shard_map/pallas_call | solution.py:163
  1.4 1.5 %shard_map.137.own_ref = bf16[32,1024]{1,0:T(8,128)(2,1)S(1)} custom-call(bf16[32,1024]{1,0:T(8,128)(2,1)S(1)} %get-tuple-element.38.q_ref, bf16[32,128]{1,0:T(8,128)(2,1)S(1)} %get-tuple-element.39.nk_ref, bf16[32,128]{1,0:T(8,128)(2,1)S(1)} %get-tuple-element.40.nv_ref, bf16[2048,128]{1,0:T(8,128)(2,1)S(1)} %get-tuple-element.41.k_ref, ...), custom_call_target="tpu_custom_call" | custom-call | flops 99999997952 | bytes 1000 | tf_op jit(solution)/shard_map/pallas_call | solution.py:163
  2.9 3.0 %collective-permute-start = (bf16[32,1024]{1,0:T(8,128)(2,1)S(1)}, bf16[32,1024]{1,0:T(8,128)(2,1)S(1)}, u32[]{:S(2)}, u32[]{:S(2)}) collective-permute-start(bf16[32,1024]{1,0:T(8,128)(2,1)S(1)} %shard_map.137.own_ref), channel_id=1, source_target_pairs={{0,2},{2,0},{1,3},{3,1},{4,6},{6,4},{5,7},{7,5},{8,10},{10,8},{9,1... | collective-permute-start | bytes 196616 | tf_op jit(solution)/shard_map/ppermute | solution.py:469
  5.9 2.2 %collective-permute-done.other_ref = bf16[32,1024]{1,0:T(8,128)(2,1)S(1)} collective-permute-done((bf16[32,1024]{1,0:T(8,128)(2,1)S(1)}, bf16[32,1024]{1,0:T(8,128)(2,1)S(1)}, u32[]{:S(2)}, u32[]{:S(2)}) %collective-permute-start) | collective-permute-done | bytes 65568 | tf_op jit(solution)/shard_map/ppermute | solution.py:469
  8.8 1.3 %collective-permute-done.1.got_ref = f32[64,512]{1,0:T(8,128)S(1)} collective-permute-done((f32[64,512]{1,0:T(8,128)S(1)}, f32[64,512]{1,0:T(8,128)S(1)}, u32[]{:S(2)}, u32[]{:S(2)}) %collective-permute-start.1) | collective-permute-done | bytes 131104 | tf_op jit(solution)/shard_map/ppermute | solution.py:469
  10.1 4.2 %collective-permute-start.7 = (bf16[64,512]{1,0:T(8,128)(2,1)S(1)}, bf16[64,512]{1,0:T(8,128)(2,1)S(1)}, u32[]{:S(2)}, u32[]{:S(2)}) collective-permute-start(bf16[64,512]{1,0:T(8,128)(2,1)S(1)} %get-tuple-element.48.refs_0_), channel_id=1, source_target_pairs={{0,12},{4,8},{8,4},{12,0},{1,13},{5,9},{9,5},{13,1},{2,14},{6,10},... | collective-permute-start | bytes 196616 | tf_op jit(solution)/shard_map/ppermute | solution.py:469
  15.0 2.0 %collective-permute-done.7.refs_3_ = bf16[64,512]{1,0:T(8,128)(2,1)S(1)} collective-permute-done((bf16[64,512]{1,0:T(8,128)(2,1)S(1)}, bf16[64,512]{1,0:T(8,128)(2,1)S(1)}, u32[]{:S(2)}, u32[]{:S(2)}) %collective-permute-start.7) | collective-permute-done | bytes 65568 | tf_op jit(solution)/shard_map/ppermute | solution.py:469
  17.0 3.3 %collective-permute-done.5.refs_2_ = bf16[64,512]{1,0:T(8,128)(2,1)S(1)} collective-permute-done((bf16[64,512]{1,0:T(8,128)(2,1)S(1)}, bf16[64,512]{1,0:T(8,128)(2,1)S(1)}, u32[]{:S(2)}, u32[]{:S(2)}) %collective-permute-start.5) | collective-permute-done | bytes 65568 | tf_op jit(solution)/shard_map/ppermute | solution.py:469
  20.4 1.4 %collective-permute-start.10 = (bf16[8,512]{1,0:T(8,128)(2,1)S(1)}, bf16[8,512]{1,0:T(8,128)(2,1)S(1)}, u32[]{:S(2)}, u32[]{:S(2)}) collective-permute-start(bf16[8,512]{1,0:T(8,128)(2,1)S(1)} %shard_map.141.first_ref), channel_id=1, source_target_pairs={{0,8},{4,12},{8,0},{12,4},{1,9},{5,13},{9,1},{13,5},{2,10},{6,14},... | collective-permute-start | bytes 24584 | tf_op jit(solution)/shard_map/ppermute | solution.py:469
  21.7 3.3 %collective-permute-done.10.second_ref = bf16[8,512]{1,0:T(8,128)(2,1)S(1)} collective-permute-done((bf16[8,512]{1,0:T(8,128)(2,1)S(1)}, bf16[8,512]{1,0:T(8,128)(2,1)S(1)}, u32[]{:S(2)}, u32[]{:S(2)}) %collective-permute-start.10) | collective-permute-done | bytes 8224 | tf_op jit(solution)/shard_map/ppermute | solution.py:469
  25.0 1.1 %collective-permute-start.11 = (bf16[16,512]{1,0:T(8,128)(2,1)S(1)}, bf16[16,512]{1,0:T(8,128)(2,1)S(1)}, u32[]{:S(2)}, u32[]{:S(2)}) collective-permute-start(bf16[16,512]{1,0:T(8,128)(2,1)S(1)} %shard_map.142.mine_ref), channel_id=1, source_target_pairs={{0,4},{4,0},{8,12},{12,8},{1,5},{5,1},{9,13},{13,9},{2,6},{6,2},{1... | collective-permute-start | bytes 49160 | tf_op jit(solution)/shard_map/ppermute | solution.py:469
  26.1 1.5 %collective-permute-start.2 = (bf16[72,512]{1,0:T(8,128)(2,1)S(1)}, bf16[72,512]{1,0:T(8,128)(2,1)S(1)}, u32[]{:S(2)}, u32[]{:S(2)}) collective-permute-start(bf16[72,512]{1,0:T(8,128)(2,1)S(1)} %get-tuple-element.47), channel_id=1, source_target_pairs={{0,2},{2,0},{1,3},{3,1},{4,6},{6,4},{5,7},{7,5},{8,10},{10,8},{9,1... | collective-permute-start | bytes 221192 | tf_op jit(solution)/shard_map/ppermute | solution.py:469
  28.1 1.5 %collective-permute-start.6 = (bf16[64,512]{1,0:T(8,128)(2,1)S(1)}, bf16[64,512]{1,0:T(8,128)(2,1)S(1)}, u32[]{:S(2)}, u32[]{:S(2)}) collective-permute-start(bf16[64,512]{1,0:T(8,128)(2,1)S(1)} %collective-permute-done.5.refs_2_), channel_id=1, source_target_pairs={{0,2},{2,0},{1,3},{3,1},{4,6},{6,4},{5,7},{7,5},{8,10},{10,8},{9,1... | collective-permute-start | bytes 196616 | tf_op jit(solution)/shard_map/ppermute | solution.py:469
  30.6 3.0 %shard_map.144 = (f32[384,1]{1,0:T(8,128)S(1)}, bf16[384,1024]{1,0:T(8,128)(2,1)S(1)}, f32[288,384]{1,0:T(8,128)S(1)}, f32[288,384]{1,0:T(8,128)S(1)}) custom-call(bf16[256,512]{1,0:T(8,128)(2,1)S(1)} %shard_map.140.mine_ref, bf16[256,512]{1,0:T(8,128)(2,1)S(1)} %collective-permute-done.9.theirs_ref, f32[1,1024]{1,0:T(1,128)S(1)} %bitcast.9, ...), custom_call_target="tpu_custom_call" | custom-call | flops 1000 | bytes 1000 | tf_op jit(solution)/shard_map/pallas_call | solution.py:163
  34.1 1.0 %shard_map.146 = (f32[96,384]{1,0:T(8,128)S(1)}, f32[96,384]{1,0:T(8,128)S(1)}) custom-call(bf16[384,1024]{1,0:T(8,128)(2,1)S(1)} %get-tuple-element.58.rows_ref, bf16[8,384,2048]{2,1,0:T(8,128)(2,1)S(1)} %copy-done, bf16[8,384,2048]{2,1,0:T(8,128)(2,1)S(1)} %copy-done.1), custom_call_target="tpu_custom_call" | custom-call | flops 1000 | bytes 1000 | tf_op jit(solution)/shard_map/pallas_call | solution.py:163
  35.6 3.8 %shard_map.147.act_ref = bf16[384,384]{1,0:T(8,128)(2,1)S(1)} custom-call(bf16[264,512]{1,0:T(8,128)(2,1)S(1)} %shard_map.145.mine_ref, bf16[264,512]{1,0:T(8,128)(2,1)S(1)} %collective-permute-done.12.theirs_ref, bf16[8,384,2048]{2,1,0:T(8,128)(2,1)S(1)} %copy-done, bf16[8,384,2048]{2,1,0:T(8,128)(2,1)S(1)} %copy-done.1, ...), custom_call_target="tpu_custom_call" | custom-call | flops 1000 | bytes 1000 | tf_op jit(solution)/shard_map/pallas_call | solution.py:163
  43.2 1.1 %collective-permute-start.18 = (bf16[128,512]{1,0:T(8,128)(2,1)S(1)}, bf16[128,512]{1,0:T(8,128)(2,1)S(1)}, u32[]{:S(2)}, u32[]{:S(2)}) collective-permute-start(bf16[128,512]{1,0:T(8,128)(2,1)S(1)} %get-tuple-element.68), channel_id=1, source_target_pairs={{0,2},{2,0},{1,3},{3,1},{4,6},{6,4},{5,7},{7,5},{8,10},{10,8},{9,1... | collective-permute-start | bytes 393224 | tf_op jit(solution)/shard_map/ppermute | solution.py:469
  44.2 1.0 %collective-permute-start.15 = (bf16[64,512]{1,0:T(8,128)(2,1)S(1)}, bf16[64,512]{1,0:T(8,128)(2,1)S(1)}, u32[]{:S(2)}, u32[]{:S(2)}) collective-permute-start(bf16[64,512]{1,0:T(8,128)(2,1)S(1)} %get-tuple-element.66), channel_id=1, source_target_pairs={{0,2},{2,0},{1,3},{3,1},{4,6},{6,4},{5,7},{7,5},{8,10},{10,8},{9,1... | collective-permute-start | bytes 196616 | tf_op jit(solution)/shard_map/ppermute | solution.py:469
  45.2 1.1 %collective-permute-start.16 = (bf16[64,512]{1,0:T(8,128)(2,1)S(1)}, bf16[64,512]{1,0:T(8,128)(2,1)S(1)}, u32[]{:S(2)}, u32[]{:S(2)}) collective-permute-start(bf16[64,512]{1,0:T(8,128)(2,1)S(1)} %get-tuple-element.67), channel_id=1, source_target_pairs={{0,2},{2,0},{1,3},{3,1},{4,6},{6,4},{5,7},{7,5},{8,10},{10,8},{9,1... | collective-permute-start | bytes 196616 | tf_op jit(solution)/shard_map/ppermute | solution.py:469
  47.1 2.4 %collective-permute-done.18.other_ref = bf16[128,512]{1,0:T(8,128)(2,1)S(1)} collective-permute-done((bf16[128,512]{1,0:T(8,128)(2,1)S(1)}, bf16[128,512]{1,0:T(8,128)(2,1)S(1)}, u32[]{:S(2)}, u32[]{:S(2)}) %collective-permute-start.18) | collective-permute-done | bytes 131104 | tf_op jit(solution)/shard_map/ppermute | solution.py:469
  50.5 1.8 %collective-permute-start.20 = (bf16[64,512]{1,0:T(8,128)(2,1)S(1)}, bf16[64,512]{1,0:T(8,128)(2,1)S(1)}, u32[]{:S(2)}, u32[]{:S(2)}) collective-permute-start(bf16[64,512]{1,0:T(8,128)(2,1)S(1)} %get-tuple-element.70), channel_id=1, source_target_pairs={{0,8},{4,12},{8,0},{12,4},{1,9},{5,13},{9,1},{13,5},{2,10},{6,14},... | collective-permute-start | bytes 196616 | tf_op jit(solution)/shard_map/ppermute | solution.py:469
  52.3 1.8 %collective-permute-start.17 = (bf16[64,512]{1,0:T(8,128)(2,1)S(1)}, bf16[64,512]{1,0:T(8,128)(2,1)S(1)}, u32[]{:S(2)}, u32[]{:S(2)}) collective-permute-start(bf16[64,512]{1,0:T(8,128)(2,1)S(1)} %shard_map.153), channel_id=1, source_target_pairs={{0,12},{4,8},{8,4},{12,0},{1,13},{5,9},{9,5},{13,1},{2,14},{6,10},... | collective-permute-start | bytes 196616 | tf_op jit(solution)/shard_map/ppermute | solution.py:469
  54.1 3.0 %collective-permute-done.20.refs_3_ = bf16[64,512]{1,0:T(8,128)(2,1)S(1)} collective-permute-done((bf16[64,512]{1,0:T(8,128)(2,1)S(1)}, bf16[64,512]{1,0:T(8,128)(2,1)S(1)}, u32[]{:S(2)}, u32[]{:S(2)}) %collective-permute-start.20) | collective-permute-done | bytes 65568 | tf_op jit(solution)/shard_map/ppermute | solution.py:469
  57.1 1.4 %collective-permute-done.17.refs_1_ = bf16[64,512]{1,0:T(8,128)(2,1)S(1)} collective-permute-done((bf16[64,512]{1,0:T(8,128)(2,1)S(1)}, bf16[64,512]{1,0:T(8,128)(2,1)S(1)}, u32[]{:S(2)}, u32[]{:S(2)}) %collective-permute-start.17) | collective-permute-done | bytes 65568 | tf_op jit(solution)/shard_map/ppermute | solution.py:469
  (59 shorter events, 10.1 us)
Async XLA Ops:
  1.4 19.0 %copy-start.5 = (s32[64,8]{0,1:T(8,128)S(1)}, s32[64,8]{0,1:T(8,128)}, u32[]{:S(2)}) copy-start(s32[64,8]{0,1:T(8,128)} %param.23) | copy-start | bytes 6148
  1.4 29.2 %copy-start = (bf16[8,384,2048]{2,1,0:T(8,128)(2,1)S(1)}, bf16[8,384,2048]{2,1,0:T(8,128)(2,1)}, u32[]{:S(2)}) copy-start(bf16[8,384,2048]{2,1,0:T(8,128)(2,1)} %wg_ref.5) | copy-start | bytes 37748740
  1.4 29.2 %copy-start.1 = (bf16[8,384,2048]{2,1,0:T(8,128)(2,1)S(1)}, bf16[8,384,2048]{2,1,0:T(8,128)(2,1)}, u32[]{:S(2)}) copy-start(bf16[8,384,2048]{2,1,0:T(8,128)(2,1)} %wu_ref.5) | copy-start | bytes 37748740
  2.9 5.3 %collective-permute-start = (bf16[32,1024]{1,0:T(8,128)(2,1)S(1)}, bf16[32,1024]{1,0:T(8,128)(2,1)S(1)}, u32[]{:S(2)}, u32[]{:S(2)}) collective-permute-start(bf16[32,1024]{1,0:T(8,128)(2,1)S(1)} %shard_map.137.own_ref), channel_id=1, source_target_pairs={{0,2},{2,0},{1,3},{3,1},{4,6},{6,4},{5,7},{7,5},{8,10},{10,8},{9,1... | collective-permute-start | bytes 196616 | tf_op jit(solution)/shard_map/ppermute | solution.py:469
  8.7 1.4 %collective-permute-start.1 = (f32[64,512]{1,0:T(8,128)S(1)}, f32[64,512]{1,0:T(8,128)S(1)}, u32[]{:S(2)}, u32[]{:S(2)}) collective-permute-start(f32[64,512]{1,0:T(8,128)S(1)} %get-tuple-element.45), channel_id=1, source_target_pairs={{0,1},{1,0},{2,3},{3,2},{4,5},{5,4},{6,7},{7,6},{8,9},{9,8},{10,11... | collective-permute-start | bytes 393224 | tf_op jit(solution)/shard_map/ppermute | solution.py:469
  10.1 6.8 %collective-permute-start.7 = (bf16[64,512]{1,0:T(8,128)(2,1)S(1)}, bf16[64,512]{1,0:T(8,128)(2,1)S(1)}, u32[]{:S(2)}, u32[]{:S(2)}) collective-permute-start(bf16[64,512]{1,0:T(8,128)(2,1)S(1)} %get-tuple-element.48.refs_0_), channel_id=1, source_target_pairs={{0,12},{4,8},{8,4},{12,0},{1,13},{5,9},{9,5},{13,1},{2,14},{6,10},... | collective-permute-start | bytes 196616 | tf_op jit(solution)/shard_map/ppermute | solution.py:469
  14.3 5.9 %collective-permute-start.5 = (bf16[64,512]{1,0:T(8,128)(2,1)S(1)}, bf16[64,512]{1,0:T(8,128)(2,1)S(1)}, u32[]{:S(2)}, u32[]{:S(2)}) collective-permute-start(bf16[64,512]{1,0:T(8,128)(2,1)S(1)} %get-tuple-element.48.refs_0_), channel_id=1, source_target_pairs={{0,8},{4,12},{8,0},{12,4},{1,9},{5,13},{9,1},{13,5},{2,10},{6,14},... | collective-permute-start | bytes 196616 | tf_op jit(solution)/shard_map/ppermute | solution.py:469
  14.3 5.9 %collective-permute-start.3 = (bf16[64,512]{1,0:T(8,128)(2,1)S(1)}, bf16[64,512]{1,0:T(8,128)(2,1)S(1)}, u32[]{:S(2)}, u32[]{:S(2)}) collective-permute-start(bf16[64,512]{1,0:T(8,128)(2,1)S(1)} %get-tuple-element.48.refs_0_), channel_id=1, source_target_pairs={{0,4},{4,0},{8,12},{12,8},{1,5},{5,1},{9,13},{13,9},{2,6},{6,2},{1... | collective-permute-start | bytes 196616 | tf_op jit(solution)/shard_map/ppermute | solution.py:469
  20.3 10.3 %collective-permute-start.9 = (bf16[256,512]{1,0:T(8,128)(2,1)S(1)}, bf16[256,512]{1,0:T(8,128)(2,1)S(1)}, u32[]{:S(2)}, u32[]{:S(2)}) collective-permute-start(bf16[256,512]{1,0:T(8,128)(2,1)S(1)} %shard_map.140.mine_ref), channel_id=1, source_target_pairs={{0,1},{1,0},{2,3},{3,2},{4,5},{5,4},{6,7},{7,6},{8,9},{9,8},{10,11... | collective-permute-start | bytes 786440 | tf_op jit(solution)/shard_map/ppermute | solution.py:469
  20.4 4.6 %collective-permute-start.10 = (bf16[8,512]{1,0:T(8,128)(2,1)S(1)}, bf16[8,512]{1,0:T(8,128)(2,1)S(1)}, u32[]{:S(2)}, u32[]{:S(2)}) collective-permute-start(bf16[8,512]{1,0:T(8,128)(2,1)S(1)} %shard_map.141.first_ref), channel_id=1, source_target_pairs={{0,8},{4,12},{8,0},{12,4},{1,9},{5,13},{9,1},{13,5},{2,10},{6,14},... | collective-permute-start | bytes 24584 | tf_op jit(solution)/shard_map/ppermute | solution.py:469
  25.0 4.6 %collective-permute-start.11 = (bf16[16,512]{1,0:T(8,128)(2,1)S(1)}, bf16[16,512]{1,0:T(8,128)(2,1)S(1)}, u32[]{:S(2)}, u32[]{:S(2)}) collective-permute-start(bf16[16,512]{1,0:T(8,128)(2,1)S(1)} %shard_map.142.mine_ref), channel_id=1, source_target_pairs={{0,4},{4,0},{8,12},{12,8},{1,5},{5,1},{9,13},{13,9},{2,6},{6,2},{1... | collective-permute-start | bytes 49160 | tf_op jit(solution)/shard_map/ppermute | solution.py:469
  26.1 7.5 %collective-permute-start.2 = (bf16[72,512]{1,0:T(8,128)(2,1)S(1)}, bf16[72,512]{1,0:T(8,128)(2,1)S(1)}, u32[]{:S(2)}, u32[]{:S(2)}) collective-permute-start(bf16[72,512]{1,0:T(8,128)(2,1)S(1)} %get-tuple-element.47), channel_id=1, source_target_pairs={{0,2},{2,0},{1,3},{3,1},{4,6},{6,4},{5,7},{7,5},{8,10},{10,8},{9,1... | collective-permute-start | bytes 221192 | tf_op jit(solution)/shard_map/ppermute | solution.py:469
  27.6 6.0 %collective-permute-start.8 = (bf16[64,512]{1,0:T(8,128)(2,1)S(1)}, bf16[64,512]{1,0:T(8,128)(2,1)S(1)}, u32[]{:S(2)}, u32[]{:S(2)}) collective-permute-start(bf16[64,512]{1,0:T(8,128)(2,1)S(1)} %collective-permute-done.7.refs_3_), channel_id=1, source_target_pairs={{0,2},{2,0},{1,3},{3,1},{4,6},{6,4},{5,7},{7,5},{8,10},{10,8},{9,1... | collective-permute-start | bytes 196616 | tf_op jit(solution)/shard_map/ppermute | solution.py:469
  28.1 5.5 %collective-permute-start.6 = (bf16[64,512]{1,0:T(8,128)(2,1)S(1)}, bf16[64,512]{1,0:T(8,128)(2,1)S(1)}, u32[]{:S(2)}, u32[]{:S(2)}) collective-permute-start(bf16[64,512]{1,0:T(8,128)(2,1)S(1)} %collective-permute-done.5.refs_2_), channel_id=1, source_target_pairs={{0,2},{2,0},{1,3},{3,1},{4,6},{6,4},{5,7},{7,5},{8,10},{10,8},{9,1... | collective-permute-start | bytes 196616 | tf_op jit(solution)/shard_map/ppermute | solution.py:469
  29.6 4.4 %collective-permute-start.4 = (bf16[64,512]{1,0:T(8,128)(2,1)S(1)}, bf16[64,512]{1,0:T(8,128)(2,1)S(1)}, u32[]{:S(2)}, u32[]{:S(2)}) collective-permute-start(bf16[64,512]{1,0:T(8,128)(2,1)S(1)} %collective-permute-done.3.refs_1_), channel_id=1, source_target_pairs={{0,2},{2,0},{1,3},{3,1},{4,6},{6,4},{5,7},{7,5},{8,10},{10,8},{9,1... | collective-permute-start | bytes 196616 | tf_op jit(solution)/shard_map/ppermute | solution.py:469
  34.0 1.6 %collective-permute-start.12 = (bf16[264,512]{1,0:T(8,128)(2,1)S(1)}, bf16[264,512]{1,0:T(8,128)(2,1)S(1)}, u32[]{:S(2)}, u32[]{:S(2)}) collective-permute-start(bf16[264,512]{1,0:T(8,128)(2,1)S(1)} %shard_map.145.mine_ref), channel_id=1, source_target_pairs={{0,1},{1,0},{2,3},{3,2},{4,5},{5,4},{6,7},{7,6},{8,9},{9,8},{10,11... | collective-permute-start | bytes 811016 | tf_op jit(solution)/shard_map/ppermute | solution.py:469
  40.4 1.6 %collective-permute-start.13 = (bf16[256,512]{1,0:T(8,128)(2,1)S(1)}, bf16[256,512]{1,0:T(8,128)(2,1)S(1)}, u32[]{:S(2)}, u32[]{:S(2)}) collective-permute-start(bf16[256,512]{1,0:T(8,128)(2,1)S(1)} %shard_map.149), channel_id=1, source_target_pairs={{0,1},{1,0},{2,3},{3,2},{4,5},{5,4},{6,7},{7,6},{8,9},{9,8},{10,11... | collective-permute-start | bytes 786440 | tf_op jit(solution)/shard_map/ppermute | solution.py:469
  43.0 6.6 %collective-permute-start.14 = (bf16[256,512]{1,0:T(8,128)(2,1)S(1)}, bf16[256,512]{1,0:T(8,128)(2,1)S(1)}, u32[]{:S(2)}, u32[]{:S(2)}) collective-permute-start(bf16[256,512]{1,0:T(8,128)(2,1)S(1)} %shard_map.152), channel_id=1, source_target_pairs={{0,1},{1,0},{2,3},{3,2},{4,5},{5,4},{6,7},{7,6},{8,9},{9,8},{10,11... | collective-permute-start | bytes 786440 | tf_op jit(solution)/shard_map/ppermute | solution.py:469
  43.2 6.4 %collective-permute-start.18 = (bf16[128,512]{1,0:T(8,128)(2,1)S(1)}, bf16[128,512]{1,0:T(8,128)(2,1)S(1)}, u32[]{:S(2)}, u32[]{:S(2)}) collective-permute-start(bf16[128,512]{1,0:T(8,128)(2,1)S(1)} %get-tuple-element.68), channel_id=1, source_target_pairs={{0,2},{2,0},{1,3},{3,1},{4,6},{6,4},{5,7},{7,5},{8,10},{10,8},{9,1... | collective-permute-start | bytes 393224 | tf_op jit(solution)/shard_map/ppermute | solution.py:469
  44.2 9.9 %collective-permute-start.15 = (bf16[64,512]{1,0:T(8,128)(2,1)S(1)}, bf16[64,512]{1,0:T(8,128)(2,1)S(1)}, u32[]{:S(2)}, u32[]{:S(2)}) collective-permute-start(bf16[64,512]{1,0:T(8,128)(2,1)S(1)} %get-tuple-element.66), channel_id=1, source_target_pairs={{0,2},{2,0},{1,3},{3,1},{4,6},{6,4},{5,7},{7,5},{8,10},{10,8},{9,1... | collective-permute-start | bytes 196616 | tf_op jit(solution)/shard_map/ppermute | solution.py:469
  45.2 7.1 %collective-permute-start.16 = (bf16[64,512]{1,0:T(8,128)(2,1)S(1)}, bf16[64,512]{1,0:T(8,128)(2,1)S(1)}, u32[]{:S(2)}, u32[]{:S(2)}) collective-permute-start(bf16[64,512]{1,0:T(8,128)(2,1)S(1)} %get-tuple-element.67), channel_id=1, source_target_pairs={{0,2},{2,0},{1,3},{3,1},{4,6},{6,4},{5,7},{7,5},{8,10},{10,8},{9,1... | collective-permute-start | bytes 196616 | tf_op jit(solution)/shard_map/ppermute | solution.py:469
  49.6 4.6 %collective-permute-start.19 = (bf16[64,512]{1,0:T(8,128)(2,1)S(1)}, bf16[64,512]{1,0:T(8,128)(2,1)S(1)}, u32[]{:S(2)}, u32[]{:S(2)}) collective-permute-start(bf16[64,512]{1,0:T(8,128)(2,1)S(1)} %get-tuple-element.69), channel_id=1, source_target_pairs={{0,4},{4,0},{8,12},{12,8},{1,5},{5,1},{9,13},{13,9},{2,6},{6,2},{1... | collective-permute-start | bytes 196616 | tf_op jit(solution)/shard_map/ppermute | solution.py:469
  50.5 6.6 %collective-permute-start.20 = (bf16[64,512]{1,0:T(8,128)(2,1)S(1)}, bf16[64,512]{1,0:T(8,128)(2,1)S(1)}, u32[]{:S(2)}, u32[]{:S(2)}) collective-permute-start(bf16[64,512]{1,0:T(8,128)(2,1)S(1)} %get-tuple-element.70), channel_id=1, source_target_pairs={{0,8},{4,12},{8,0},{12,4},{1,9},{5,13},{9,1},{13,5},{2,10},{6,14},... | collective-permute-start | bytes 196616 | tf_op jit(solution)/shard_map/ppermute | solution.py:469
  52.3 6.2 %collective-permute-start.17 = (bf16[64,512]{1,0:T(8,128)(2,1)S(1)}, bf16[64,512]{1,0:T(8,128)(2,1)S(1)}, u32[]{:S(2)}, u32[]{:S(2)}) collective-permute-start(bf16[64,512]{1,0:T(8,128)(2,1)S(1)} %shard_map.153), channel_id=1, source_target_pairs={{0,12},{4,8},{8,4},{12,0},{1,13},{5,9},{9,5},{13,1},{2,14},{6,10},... | collective-permute-start | bytes 196616 | tf_op jit(solution)/shard_map/ppermute | solution.py:469
  (7 other events, 57.9 us)

commit v4 on v3

--- a/solution.py
+++ b/solution.py
@@ -240,7 +240,7 @@
     rows = rows_ref[...]
     send_ref[...] = jnp.dot(
         rows, w_ref[:, pl.ds(pl.multiple_of((1 - t) * cols, cols), cols)], preferred_element_type=F32
-    )
+    ).astype(BF16)
     keep_ref[...] = jnp.dot(
         rows, w_ref[:, pl.ds(pl.multiple_of(t * cols, cols), cols)], preferred_element_type=F32
     )
@@ -271,7 +271,7 @@
     t = lax.axis_index("tp")
     rows, cols = keep_ref.shape
     here = pl.ds(pl.multiple_of(t * cols, cols), cols)
-    hidden = res_ref[:, here].astype(F32) + (keep_ref[...] + got_ref[...])
+    hidden = res_ref[:, here].astype(F32) + (keep_ref[...] + got_ref[...].astype(F32))
     h32_ref[...] = hidden
     h16_ref[...] = hidden.astype(BF16)
     load_ref[0:rows, :] = hidden.astype(BF16)
@@ -296,9 +296,11 @@
     out_ref = refs[-1]
     rows = load_ref.shape[0] - TAIL
     out_ref[0:rows, :] = load_ref[0:rows, :]
-    for j, ref in enumerate(refs[:-1]):
-        out_ref[rows * (j + 1) : rows * (j + 2), :] = ref[...]
-    out_ref[out_ref.shape[0] - TAIL :, :] = load_ref[rows:, :]
+    start = rows
+    for ref in refs[:-1]:
+        out_ref[start : start + ref.shape[0], :] = ref[...]
+        start += ref.shape[0]
+    out_ref[start:, :] = load_ref[rows:, :]
 
 
 def pick_body(mine_ref, theirs_ref, pick_ref, gate_ref):
@@ -539,7 +541,7 @@
     )
     keep, send = kernel_call(
         project_body,
-        [((token_rows, cols), F32)] * 2,
+        [((token_rows, cols), F32), ((token_rows, cols), BF16)],
         scratch=[pltpu.VMEM((token_rows, sharing * head_size), BF16)],
         args=(attended, other_attended, out_weight),
     )
@@ -550,7 +552,10 @@
         args=(residual, gain, keep, swap(send, "tp")),
     )
     arrived = [h16] + [swap(h16, "ep", j) for j in range(1, blocks)]
-    from_x = [swap(payload if j == 0 else v, "half") for j, v in enumerate(arrived)]
+    (middle,) = kernel_call(
+        merge_body, [(((blocks - 2) * token_rows, cols), BF16)], args=arrived[1:-1]
+    )
+    from_x = [swap(v, "half") for v in (payload, middle, arrived[-1])]
     (mine,) = kernel_call(merge_body, [((tokens, cols), BF16)], args=arrived)
     theirs = swap(mine, "tp")
     pick, gate = kernel_call(

time: 59.3 us -> 61.3 us (1.034)
  waiting for transfers between devices: 20.3 us -> 23.1 us
  starting transfers between devices: 22.6 us -> 21.8 us
    ppermute x21 -> x20, waiting for transfers between devices: 20.3 us -> 23.1 us  [swap(): lax.ppermute(value, axis, [(i, i ^ partner) for i in range(lax.axis_size(...]
    ppermute x21 -> x20, starting transfers between devices: 22.6 us -> 21.8 us  [swap(): lax.ppermute(value, axis, [(i, i ^ partner) for i in range(lax.axis_size(...]
    pallas_call x20 -> x21, Pallas kernels: 15.9 us -> 15.9 us  [pallas_kernel(): pl.pallas_call(body, out_shape=tuple((jax.ShapeDtypeStruct(s, d) for s, d...]
  transfers between devices with their start and end apart: 21 -> 20, of which waited for: 11 -> 11; matrix products, arithmetic and copies ran while one was open for 0% -> 0% of each run, Pallas kernels for 10% -> 10%
where the time goes in v4:
time: 61.3 us; the launch traced here: 61.1 us
  waiting for transfers between devices  23.1 us (38%)
  starting transfers between devices  21.8 us (36%)
  Pallas kernels  15.9 us (26%)
    ppermute x20, waiting for transfers between devices, swap(): lax.ppermute(value, axis, [(i, i ^ partner) for i in range(lax.axis_size(...  23.1 us
    ppermute x20, starting transfers between devices, swap(): lax.ppermute(value, axis, [(i, i ^ partner) for i in range(lax.axis_size(...  21.8 us
    pallas_call x21, Pallas kernels, pallas_kernel(): pl.pallas_call(body, out_shape=tuple((jax.ShapeDtypeStruct(s, d) for s, d...  15.9 us
  transfers between devices with their start and end apart: 20, of which 11 were waited for; matrix products, arithmetic and copies ran while one was open for 0% of the time, Pallas kernels for 10%

profile of v4, /device:TPU:0, one launch (start us, length us, event | category | flops | bytes accessed | tf_op | source)
XLA Modules:
  0.0 61.1 jit_solution(11814190014005539537)
XLA Ops:
  0.0 1.3 %shard_map.136 = (bf16[32,1024]{1,0:T(8,128)(2,1)S(1)}, bf16[32,128]{1,0:T(8,128)(2,1)S(1)}, bf16[32,128]{1,0:T(8,128)(2,1)S(1)}, bf16[2048,128]{1,0:T(8,128)(2,...) custom-call(bf16[32,1024]{1,0:T(8,128)(2,1)} %refs_0_.1, bf16[32,128]{1,0:T(8,128)(2,1)} %refs_1_.1, ...), custom_call_target="tpu_custom_call" | custom-call | flops 1000 | bytes 1000 | tf_op jit(solution)/shard_map/pallas_call | solution.py:163
  1.4 1.5 %shard_map.137.own_ref = bf16[32,1024]{1,0:T(8,128)(2,1)S(1)} custom-call(bf16[32,1024]{1,0:T(8,128)(2,1)S(1)} %get-tuple-element.37.q_ref, bf16[32,128]{1,0:T(8,128)(2,1)S(1)} %get-tuple-element.38.nk_ref, bf16[32,128]{1,0:T(8,128)(2,1)S(1)} %get-tuple-element.39.nv_ref, bf16[2048,128]{1,0:T(8,128)(2,1)S(1)} %get-tuple-element.40.k_ref, ...), custom_call_target="tpu_custom_call" | custom-call | flops 99999997952 | bytes 1000 | tf_op jit(solution)/shard_map/pallas_call | solution.py:163
  2.9 3.0 %collective-permute-start = (bf16[32,1024]{1,0:T(8,128)(2,1)S(1)}, bf16[32,1024]{1,0:T(8,128)(2,1)S(1)}, u32[]{:S(2)}, u32[]{:S(2)}) collective-permute-start(bf16[32,1024]{1,0:T(8,128)(2,1)S(1)} %shard_map.137.own_ref), channel_id=1, source_target_pairs={{0,2},{2,0},{1,3},{3,1},{4,6},{6,4},{5,7},{7,5},{8,10},{10,8},{9,1... | collective-permute-start | bytes 196616 | tf_op jit(solution)/shard_map/ppermute | solution.py:471
  5.9 2.2 %collective-permute-done.other_ref = bf16[32,1024]{1,0:T(8,128)(2,1)S(1)} collective-permute-done((bf16[32,1024]{1,0:T(8,128)(2,1)S(1)}, bf16[32,1024]{1,0:T(8,128)(2,1)S(1)}, u32[]{:S(2)}, u32[]{:S(2)}) %collective-permute-start) | collective-permute-done | bytes 65568 | tf_op jit(solution)/shard_map/ppermute | solution.py:471
  8.8 1.2 %collective-permute-done.1.got_ref = bf16[64,512]{1,0:T(8,128)(2,1)S(1)} collective-permute-done((bf16[64,512]{1,0:T(8,128)(2,1)S(1)}, bf16[64,512]{1,0:T(8,128)(2,1)S(1)}, u32[]{:S(2)}, u32[]{:S(2)}) %collective-permute-start.1) | collective-permute-done | bytes 65568 | tf_op jit(solution)/shard_map/ppermute | solution.py:471
  10.1 4.2 %collective-permute-start.6 = (bf16[64,512]{1,0:T(8,128)(2,1)S(1)}, bf16[64,512]{1,0:T(8,128)(2,1)S(1)}, u32[]{:S(2)}, u32[]{:S(2)}) collective-permute-start(bf16[64,512]{1,0:T(8,128)(2,1)S(1)} %get-tuple-element.47.refs_0_), channel_id=1, source_target_pairs={{0,12},{4,8},{8,4},{12,0},{1,13},{5,9},{9,5},{13,1},{2,14},{6,10},... | collective-permute-start | bytes 196616 | tf_op jit(solution)/shard_map/ppermute | solution.py:471
  14.9 2.0 %collective-permute-done.6.refs_3_ = bf16[64,512]{1,0:T(8,128)(2,1)S(1)} collective-permute-done((bf16[64,512]{1,0:T(8,128)(2,1)S(1)}, bf16[64,512]{1,0:T(8,128)(2,1)S(1)}, u32[]{:S(2)}, u32[]{:S(2)}) %collective-permute-start.6) | collective-permute-done | bytes 65568 | tf_op jit(solution)/shard_map/ppermute | solution.py:471
  16.9 3.3 %collective-permute-done.4.refs_1_.refs_2_ = bf16[64,512]{1,0:T(8,128)(2,1)S(1)} collective-permute-done((bf16[64,512]{1,0:T(8,128)(2,1)S(1)}, bf16[64,512]{1,0:T(8,128)(2,1)S(1)}, u32[]{:S(2)}, u32[]{:S(2)}) %collective-permute-start.4) | collective-permute-done | bytes 65568 | tf_op jit(solution)/shard_map/ppermute | solution.py:471
  20.3 1.6 %collective-permute-start.5 = (bf16[128,512]{1,0:T(8,128)(2,1)S(1)}, bf16[128,512]{1,0:T(8,128)(2,1)S(1)}, u32[]{:S(2)}, u32[]{:S(2)}) collective-permute-start(bf16[128,512]{1,0:T(8,128)(2,1)S(1)} %shard_map.140), channel_id=1, source_target_pairs={{0,2},{2,0},{1,3},{3,1},{4,6},{6,4},{5,7},{7,5},{8,10},{10,8},{9,1... | collective-permute-start | bytes 393224 | tf_op jit(solution)/shard_map/ppermute | solution.py:471
  22.3 1.5 %collective-permute-start.7 = (bf16[64,512]{1,0:T(8,128)(2,1)S(1)}, bf16[64,512]{1,0:T(8,128)(2,1)S(1)}, u32[]{:S(2)}, u32[]{:S(2)}) collective-permute-start(bf16[64,512]{1,0:T(8,128)(2,1)S(1)} %collective-permute-done.6.refs_3_), channel_id=1, source_target_pairs={{0,2},{2,0},{1,3},{3,1},{4,6},{6,4},{5,7},{7,5},{8,10},{10,8},{9,1... | collective-permute-start | bytes 196616 | tf_op jit(solution)/shard_map/ppermute | solution.py:471
  23.9 1.4 %collective-permute-start.9 = (bf16[8,512]{1,0:T(8,128)(2,1)S(1)}, bf16[8,512]{1,0:T(8,128)(2,1)S(1)}, u32[]{:S(2)}, u32[]{:S(2)}) collective-permute-start(bf16[8,512]{1,0:T(8,128)(2,1)S(1)} %shard_map.142.first_ref), channel_id=1, source_target_pairs={{0,8},{4,12},{8,0},{12,4},{1,9},{5,13},{9,1},{13,5},{2,10},{6,14},... | collective-permute-start | bytes 24584 | tf_op jit(solution)/shard_map/ppermute | solution.py:471
  25.2 3.2 %collective-permute-done.9.second_ref = bf16[8,512]{1,0:T(8,128)(2,1)S(1)} collective-permute-done((bf16[8,512]{1,0:T(8,128)(2,1)S(1)}, bf16[8,512]{1,0:T(8,128)(2,1)S(1)}, u32[]{:S(2)}, u32[]{:S(2)}) %collective-permute-start.9) | collective-permute-done | bytes 8224 | tf_op jit(solution)/shard_map/ppermute | solution.py:471
  28.5 1.1 %collective-permute-start.10 = (bf16[16,512]{1,0:T(8,128)(2,1)S(1)}, bf16[16,512]{1,0:T(8,128)(2,1)S(1)}, u32[]{:S(2)}, u32[]{:S(2)}) collective-permute-start(bf16[16,512]{1,0:T(8,128)(2,1)S(1)} %shard_map.143.mine_ref), channel_id=1, source_target_pairs={{0,4},{4,0},{8,12},{12,8},{1,5},{5,1},{9,13},{13,9},{2,6},{6,2},{1... | collective-permute-start | bytes 49160 | tf_op jit(solution)/shard_map/ppermute | solution.py:471
  29.6 2.6 %collective-permute-done.10.theirs_ref = bf16[16,512]{1,0:T(8,128)(2,1)S(1)} collective-permute-done((bf16[16,512]{1,0:T(8,128)(2,1)S(1)}, bf16[16,512]{1,0:T(8,128)(2,1)S(1)}, u32[]{:S(2)}, u32[]{:S(2)}) %collective-permute-start.10) | collective-permute-done | bytes 16416 | tf_op jit(solution)/shard_map/ppermute | solution.py:471
  32.6 3.0 %shard_map.145 = (f32[384,1]{1,0:T(8,128)S(1)}, bf16[384,1024]{1,0:T(8,128)(2,1)S(1)}, f32[288,384]{1,0:T(8,128)S(1)}, f32[288,384]{1,0:T(8,128)S(1)}) custom-call(bf16[256,512]{1,0:T(8,128)(2,1)S(1)} %shard_map.141.mine_ref, bf16[256,512]{1,0:T(8,128)(2,1)S(1)} %collective-permute-done.8.theirs_ref, f32[1,1024]{1,0:T(1,128)S(1)} %bitcast.9, ...), custom_call_target="tpu_custom_call" | custom-call | flops 1000 | bytes 1000 | tf_op jit(solution)/shard_map/pallas_call | solution.py:163
  35.7 1.0 %shard_map.147 = (f32[96,384]{1,0:T(8,128)S(1)}, f32[96,384]{1,0:T(8,128)S(1)}) custom-call(bf16[384,1024]{1,0:T(8,128)(2,1)S(1)} %get-tuple-element.56.rows_ref, bf16[8,384,2048]{2,1,0:T(8,128)(2,1)S(1)} %copy-done, bf16[8,384,2048]{2,1,0:T(8,128)(2,1)S(1)} %copy-done.1), custom_call_target="tpu_custom_call" | custom-call | flops 1000 | bytes 1000 | tf_op jit(solution)/shard_map/pallas_call | solution.py:163
  37.2 3.8 %shard_map.148.act_ref = bf16[384,384]{1,0:T(8,128)(2,1)S(1)} custom-call(bf16[264,512]{1,0:T(8,128)(2,1)S(1)} %shard_map.146.mine_ref, bf16[264,512]{1,0:T(8,128)(2,1)S(1)} %collective-permute-done.11.theirs_ref, bf16[8,384,2048]{2,1,0:T(8,128)(2,1)S(1)} %copy-done, bf16[8,384,2048]{2,1,0:T(8,128)(2,1)S(1)} %copy-done.1, ...), custom_call_target="tpu_custom_call" | custom-call | flops 1000 | bytes 1000 | tf_op jit(solution)/shard_map/pallas_call | solution.py:163
  45.3 1.5 %collective-permute-start.14 = (bf16[64,512]{1,0:T(8,128)(2,1)S(1)}, bf16[64,512]{1,0:T(8,128)(2,1)S(1)}, u32[]{:S(2)}, u32[]{:S(2)}) collective-permute-start(bf16[64,512]{1,0:T(8,128)(2,1)S(1)} %get-tuple-element.64), channel_id=1, source_target_pairs={{0,2},{2,0},{1,3},{3,1},{4,6},{6,4},{5,7},{7,5},{8,10},{10,8},{9,1... | collective-permute-start | bytes 196616 | tf_op jit(solution)/shard_map/ppermute | solution.py:471
  48.2 2.9 %collective-permute-done.17.other_ref = bf16[128,512]{1,0:T(8,128)(2,1)S(1)} collective-permute-done((bf16[128,512]{1,0:T(8,128)(2,1)S(1)}, bf16[128,512]{1,0:T(8,128)(2,1)S(1)}, u32[]{:S(2)}, u32[]{:S(2)}) %collective-permute-start.17) | collective-permute-done | bytes 131104 | tf_op jit(solution)/shard_map/ppermute | solution.py:471
  51.2 1.2 %collective-permute-start.18 = (bf16[64,512]{1,0:T(8,128)(2,1)S(1)}, bf16[64,512]{1,0:T(8,128)(2,1)S(1)}, u32[]{:S(2)}, u32[]{:S(2)}) collective-permute-start(bf16[64,512]{1,0:T(8,128)(2,1)S(1)} %get-tuple-element.67), channel_id=1, source_target_pairs={{0,4},{4,0},{8,12},{12,8},{1,5},{5,1},{9,13},{13,9},{2,6},{6,2},{1... | collective-permute-start | bytes 196616 | tf_op jit(solution)/shard_map/ppermute | solution.py:471
  52.4 1.9 %collective-permute-start.19 = (bf16[64,512]{1,0:T(8,128)(2,1)S(1)}, bf16[64,512]{1,0:T(8,128)(2,1)S(1)}, u32[]{:S(2)}, u32[]{:S(2)}) collective-permute-start(bf16[64,512]{1,0:T(8,128)(2,1)S(1)} %get-tuple-element.68), channel_id=1, source_target_pairs={{0,8},{4,12},{8,0},{12,4},{1,9},{5,13},{9,1},{13,5},{2,10},{6,14},... | collective-permute-start | bytes 196616 | tf_op jit(solution)/shard_map/ppermute | solution.py:471
  54.3 1.6 %collective-permute-start.16 = (bf16[64,512]{1,0:T(8,128)(2,1)S(1)}, bf16[64,512]{1,0:T(8,128)(2,1)S(1)}, u32[]{:S(2)}, u32[]{:S(2)}) collective-permute-start(bf16[64,512]{1,0:T(8,128)(2,1)S(1)} %shard_map.154), channel_id=1, source_target_pairs={{0,12},{4,8},{8,4},{12,0},{1,13},{5,9},{9,5},{13,1},{2,14},{6,10},... | collective-permute-start | bytes 196616 | tf_op jit(solution)/shard_map/ppermute | solution.py:471
  55.9 3.0 %collective-permute-done.19.refs_3_ = bf16[64,512]{1,0:T(8,128)(2,1)S(1)} collective-permute-done((bf16[64,512]{1,0:T(8,128)(2,1)S(1)}, bf16[64,512]{1,0:T(8,128)(2,1)S(1)}, u32[]{:S(2)}, u32[]{:S(2)}) %collective-permute-start.19) | collective-permute-done | bytes 65568 | tf_op jit(solution)/shard_map/ppermute | solution.py:471
  59.0 1.5 %collective-permute-done.16.refs_1_ = bf16[64,512]{1,0:T(8,128)(2,1)S(1)} collective-permute-done((bf16[64,512]{1,0:T(8,128)(2,1)S(1)}, bf16[64,512]{1,0:T(8,128)(2,1)S(1)}, u32[]{:S(2)}, u32[]{:S(2)}) %collective-permute-start.16) | collective-permute-done | bytes 65568 | tf_op jit(solution)/shard_map/ppermute | solution.py:471
  (58 shorter events, 9.2 us)
Async XLA Ops:
  1.4 22.5 %copy-start.5 = (s32[64,8]{0,1:T(8,128)S(1)}, s32[64,8]{0,1:T(8,128)}, u32[]{:S(2)}) copy-start(s32[64,8]{0,1:T(8,128)} %param.23) | copy-start | bytes 6148
  1.4 22.5 %copy-start.6 = (f32[64,8]{0,1:T(8,128)S(1)}, f32[64,8]{0,1:T(8,128)}, u32[]{:S(2)}) copy-start(f32[64,8]{0,1:T(8,128)} %param.24) | copy-start | bytes 6148
  1.4 31.2 %copy-start = (bf16[8,384,2048]{2,1,0:T(8,128)(2,1)S(1)}, bf16[8,384,2048]{2,1,0:T(8,128)(2,1)}, u32[]{:S(2)}) copy-start(bf16[8,384,2048]{2,1,0:T(8,128)(2,1)} %wg_ref.5) | copy-start | bytes 37748740
  1.4 31.2 %copy-start.1 = (bf16[8,384,2048]{2,1,0:T(8,128)(2,1)S(1)}, bf16[8,384,2048]{2,1,0:T(8,128)(2,1)}, u32[]{:S(2)}) copy-start(bf16[8,384,2048]{2,1,0:T(8,128)(2,1)} %wu_ref.5) | copy-start | bytes 37748740
  2.9 5.3 %collective-permute-start = (bf16[32,1024]{1,0:T(8,128)(2,1)S(1)}, bf16[32,1024]{1,0:T(8,128)(2,1)S(1)}, u32[]{:S(2)}, u32[]{:S(2)}) collective-permute-start(bf16[32,1024]{1,0:T(8,128)(2,1)S(1)} %shard_map.137.own_ref), channel_id=1, source_target_pairs={{0,2},{2,0},{1,3},{3,1},{4,6},{6,4},{5,7},{7,5},{8,10},{10,8},{9,1... | collective-permute-start | bytes 196616 | tf_op jit(solution)/shard_map/ppermute | solution.py:471
  8.7 1.3 %collective-permute-start.1 = (bf16[64,512]{1,0:T(8,128)(2,1)S(1)}, bf16[64,512]{1,0:T(8,128)(2,1)S(1)}, u32[]{:S(2)}, u32[]{:S(2)}) collective-permute-start(bf16[64,512]{1,0:T(8,128)(2,1)S(1)} %get-tuple-element.44), channel_id=1, source_target_pairs={{0,1},{1,0},{2,3},{3,2},{4,5},{5,4},{6,7},{7,6},{8,9},{9,8},{10,11... | collective-permute-start | bytes 196616 | tf_op jit(solution)/shard_map/ppermute | solution.py:471
  10.1 6.8 %collective-permute-start.6 = (bf16[64,512]{1,0:T(8,128)(2,1)S(1)}, bf16[64,512]{1,0:T(8,128)(2,1)S(1)}, u32[]{:S(2)}, u32[]{:S(2)}) collective-permute-start(bf16[64,512]{1,0:T(8,128)(2,1)S(1)} %get-tuple-element.47.refs_0_), channel_id=1, source_target_pairs={{0,12},{4,8},{8,4},{12,0},{1,13},{5,9},{9,5},{13,1},{2,14},{6,10},... | collective-permute-start | bytes 196616 | tf_op jit(solution)/shard_map/ppermute | solution.py:471
  14.2 5.9 %collective-permute-start.4 = (bf16[64,512]{1,0:T(8,128)(2,1)S(1)}, bf16[64,512]{1,0:T(8,128)(2,1)S(1)}, u32[]{:S(2)}, u32[]{:S(2)}) collective-permute-start(bf16[64,512]{1,0:T(8,128)(2,1)S(1)} %get-tuple-element.47.refs_0_), channel_id=1, source_target_pairs={{0,8},{4,12},{8,0},{12,4},{1,9},{5,13},{9,1},{13,5},{2,10},{6,14},... | collective-permute-start | bytes 196616 | tf_op jit(solution)/shard_map/ppermute | solution.py:471
  14.2 5.9 %collective-permute-start.3 = (bf16[64,512]{1,0:T(8,128)(2,1)S(1)}, bf16[64,512]{1,0:T(8,128)(2,1)S(1)}, u32[]{:S(2)}, u32[]{:S(2)}) collective-permute-start(bf16[64,512]{1,0:T(8,128)(2,1)S(1)} %get-tuple-element.47.refs_0_), channel_id=1, source_target_pairs={{0,4},{4,0},{8,12},{12,8},{1,5},{5,1},{9,13},{13,9},{2,6},{6,2},{1... | collective-permute-start | bytes 196616 | tf_op jit(solution)/shard_map/ppermute | solution.py:471
  20.2 12.4 %collective-permute-start.8 = (bf16[256,512]{1,0:T(8,128)(2,1)S(1)}, bf16[256,512]{1,0:T(8,128)(2,1)S(1)}, u32[]{:S(2)}, u32[]{:S(2)}) collective-permute-start(bf16[256,512]{1,0:T(8,128)(2,1)S(1)} %shard_map.141.mine_ref), channel_id=1, source_target_pairs={{0,1},{1,0},{2,3},{3,2},{4,5},{5,4},{6,7},{7,6},{8,9},{9,8},{10,11... | collective-permute-start | bytes 786440 | tf_op jit(solution)/shard_map/ppermute | solution.py:471
  20.3 15.3 %collective-permute-start.5 = (bf16[128,512]{1,0:T(8,128)(2,1)S(1)}, bf16[128,512]{1,0:T(8,128)(2,1)S(1)}, u32[]{:S(2)}, u32[]{:S(2)}) collective-permute-start(bf16[128,512]{1,0:T(8,128)(2,1)S(1)} %shard_map.140), channel_id=1, source_target_pairs={{0,2},{2,0},{1,3},{3,1},{4,6},{6,4},{5,7},{7,5},{8,10},{10,8},{9,1... | collective-permute-start | bytes 393224 | tf_op jit(solution)/shard_map/ppermute | solution.py:471
  21.8 13.8 %collective-permute-start.2 = (bf16[72,512]{1,0:T(8,128)(2,1)S(1)}, bf16[72,512]{1,0:T(8,128)(2,1)S(1)}, u32[]{:S(2)}, u32[]{:S(2)}) collective-permute-start(bf16[72,512]{1,0:T(8,128)(2,1)S(1)} %get-tuple-element.46), channel_id=1, source_target_pairs={{0,2},{2,0},{1,3},{3,1},{4,6},{6,4},{5,7},{7,5},{8,10},{10,8},{9,1... | collective-permute-start | bytes 221192 | tf_op jit(solution)/shard_map/ppermute | solution.py:471
  22.3 13.2 %collective-permute-start.7 = (bf16[64,512]{1,0:T(8,128)(2,1)S(1)}, bf16[64,512]{1,0:T(8,128)(2,1)S(1)}, u32[]{:S(2)}, u32[]{:S(2)}) collective-permute-start(bf16[64,512]{1,0:T(8,128)(2,1)S(1)} %collective-permute-done.6.refs_3_), channel_id=1, source_target_pairs={{0,2},{2,0},{1,3},{3,1},{4,6},{6,4},{5,7},{7,5},{8,10},{10,8},{9,1... | collective-permute-start | bytes 196616 | tf_op jit(solution)/shard_map/ppermute | solution.py:471
  23.9 4.6 %collective-permute-start.9 = (bf16[8,512]{1,0:T(8,128)(2,1)S(1)}, bf16[8,512]{1,0:T(8,128)(2,1)S(1)}, u32[]{:S(2)}, u32[]{:S(2)}) collective-permute-start(bf16[8,512]{1,0:T(8,128)(2,1)S(1)} %shard_map.142.first_ref), channel_id=1, source_target_pairs={{0,8},{4,12},{8,0},{12,4},{1,9},{5,13},{9,1},{13,5},{2,10},{6,14},... | collective-permute-start | bytes 24584 | tf_op jit(solution)/shard_map/ppermute | solution.py:471
  28.5 3.7 %collective-permute-start.10 = (bf16[16,512]{1,0:T(8,128)(2,1)S(1)}, bf16[16,512]{1,0:T(8,128)(2,1)S(1)}, u32[]{:S(2)}, u32[]{:S(2)}) collective-permute-start(bf16[16,512]{1,0:T(8,128)(2,1)S(1)} %shard_map.143.mine_ref), channel_id=1, source_target_pairs={{0,4},{4,0},{8,12},{12,8},{1,5},{5,1},{9,13},{13,9},{2,6},{6,2},{1... | collective-permute-start | bytes 49160 | tf_op jit(solution)/shard_map/ppermute | solution.py:471
  35.6 1.6 %collective-permute-start.11 = (bf16[264,512]{1,0:T(8,128)(2,1)S(1)}, bf16[264,512]{1,0:T(8,128)(2,1)S(1)}, u32[]{:S(2)}, u32[]{:S(2)}) collective-permute-start(bf16[264,512]{1,0:T(8,128)(2,1)S(1)} %shard_map.146.mine_ref), channel_id=1, source_target_pairs={{0,1},{1,0},{2,3},{3,2},{4,5},{5,4},{6,7},{7,6},{8,9},{9,8},{10,11... | collective-permute-start | bytes 811016 | tf_op jit(solution)/shard_map/ppermute | solution.py:471
  42.0 1.6 %collective-permute-start.12 = (bf16[256,512]{1,0:T(8,128)(2,1)S(1)}, bf16[256,512]{1,0:T(8,128)(2,1)S(1)}, u32[]{:S(2)}, u32[]{:S(2)}) collective-permute-start(bf16[256,512]{1,0:T(8,128)(2,1)S(1)} %shard_map.150), channel_id=1, source_target_pairs={{0,1},{1,0},{2,3},{3,2},{4,5},{5,4},{6,7},{7,6},{8,9},{9,8},{10,11... | collective-permute-start | bytes 786440 | tf_op jit(solution)/shard_map/ppermute | solution.py:471
  44.6 6.6 %collective-permute-start.13 = (bf16[256,512]{1,0:T(8,128)(2,1)S(1)}, bf16[256,512]{1,0:T(8,128)(2,1)S(1)}, u32[]{:S(2)}, u32[]{:S(2)}) collective-permute-start(bf16[256,512]{1,0:T(8,128)(2,1)S(1)} %shard_map.153), channel_id=1, source_target_pairs={{0,1},{1,0},{2,3},{3,2},{4,5},{5,4},{6,7},{7,6},{8,9},{9,8},{10,11... | collective-permute-start | bytes 786440 | tf_op jit(solution)/shard_map/ppermute | solution.py:471
  44.8 6.4 %collective-permute-start.17 = (bf16[128,512]{1,0:T(8,128)(2,1)S(1)}, bf16[128,512]{1,0:T(8,128)(2,1)S(1)}, u32[]{:S(2)}, u32[]{:S(2)}) collective-permute-start(bf16[128,512]{1,0:T(8,128)(2,1)S(1)} %get-tuple-element.66), channel_id=1, source_target_pairs={{0,2},{2,0},{1,3},{3,1},{4,6},{6,4},{5,7},{7,5},{8,10},{10,8},{9,1... | collective-permute-start | bytes 393224 | tf_op jit(solution)/shard_map/ppermute | solution.py:471
  45.3 10.6 %collective-permute-start.14 = (bf16[64,512]{1,0:T(8,128)(2,1)S(1)}, bf16[64,512]{1,0:T(8,128)(2,1)S(1)}, u32[]{:S(2)}, u32[]{:S(2)}) collective-permute-start(bf16[64,512]{1,0:T(8,128)(2,1)S(1)} %get-tuple-element.64), channel_id=1, source_target_pairs={{0,2},{2,0},{1,3},{3,1},{4,6},{6,4},{5,7},{7,5},{8,10},{10,8},{9,1... | collective-permute-start | bytes 196616 | tf_op jit(solution)/shard_map/ppermute | solution.py:471
  46.8 7.5 %collective-permute-start.15 = (bf16[64,512]{1,0:T(8,128)(2,1)S(1)}, bf16[64,512]{1,0:T(8,128)(2,1)S(1)}, u32[]{:S(2)}, u32[]{:S(2)}) collective-permute-start(bf16[64,512]{1,0:T(8,128)(2,1)S(1)} %get-tuple-element.65), channel_id=1, source_target_pairs={{0,2},{2,0},{1,3},{3,1},{4,6},{6,4},{5,7},{7,5},{8,10},{10,8},{9,1... | collective-permute-start | bytes 196616 | tf_op jit(solution)/shard_map/ppermute | solution.py:471
  51.2 4.8 %collective-permute-start.18 = (bf16[64,512]{1,0:T(8,128)(2,1)S(1)}, bf16[64,512]{1,0:T(8,128)(2,1)S(1)}, u32[]{:S(2)}, u32[]{:S(2)}) collective-permute-start(bf16[64,512]{1,0:T(8,128)(2,1)S(1)} %get-tuple-element.67), channel_id=1, source_target_pairs={{0,4},{4,0},{8,12},{12,8},{1,5},{5,1},{9,13},{13,9},{2,6},{6,2},{1... | collective-permute-start | bytes 196616 | tf_op jit(solution)/shard_map/ppermute | solution.py:471
  52.4 6.6 %collective-permute-start.19 = (bf16[64,512]{1,0:T(8,128)(2,1)S(1)}, bf16[64,512]{1,0:T(8,128)(2,1)S(1)}, u32[]{:S(2)}, u32[]{:S(2)}) collective-permute-start(bf16[64,512]{1,0:T(8,128)(2,1)S(1)} %get-tuple-element.68), channel_id=1, source_target_pairs={{0,8},{4,12},{8,0},{12,4},{1,9},{5,13},{9,1},{13,5},{2,10},{6,14},... | collective-permute-start | bytes 196616 | tf_op jit(solution)/shard_map/ppermute | solution.py:471
  54.3 6.1 %collective-permute-start.16 = (bf16[64,512]{1,0:T(8,128)(2,1)S(1)}, bf16[64,512]{1,0:T(8,128)(2,1)S(1)}, u32[]{:S(2)}, u32[]{:S(2)}) collective-permute-start(bf16[64,512]{1,0:T(8,128)(2,1)S(1)} %shard_map.154), channel_id=1, source_target_pairs={{0,12},{4,8},{8,4},{12,0},{1,13},{5,9},{9,5},{13,1},{2,14},{6,10},... | collective-permute-start | bytes 196616 | tf_op jit(solution)/shard_map/ppermute | solution.py:471
  (6 other events, 38.8 us)
